TPU v7x, 32 devices: a whole 2x2x4 slice. The times are simulated.
32 devices in a mesh: seq: 4 (over y, x), resp: 8 (over z, core).
Axes of the slice: x: 2, y: 2, z: 4, core: 2. Of those that a mesh axis runs over, the one named last changes fastest.
Arguments:
- queries: bfloat16 [8, 2048, 1024], P('resp', 'seq'), may hold values from -1.796875 to 1.796875
- keys: bfloat16 [8, 2048, 1024], P('resp', 'seq'), may hold values from -1.796875 to 1.796875
- values: bfloat16 [8, 2048, 1024], P('resp', 'seq'), may hold values from -6 to 6
- grad_out: bfloat16 [8, 2048, 1024], P('resp', 'seq'), may hold values from -6 to 6
- lengths: int32 [7], replicated, may hold values from 2 to 4
Outputs:
- attended: bfloat16 [8, 2048, 1024], P('resp', 'seq')
- grad_queries: bfloat16 [8, 2048, 1024], P('resp', 'seq')
- grad_keys: bfloat16 [8, 2048, 1024], P('resp', 'seq')
- grad_values: bfloat16 [8, 2048, 1024], P('resp', 'seq')
All inputs are finite; a program needn't handle non-finite values.
Results may differ from a plain program's by a relative error of at most 0.005.
Values sent between devices are 32-bit elements; how exact they have to be, the bound alone decides.
No kernel may reach another device: no remote copies, remote signals or barrier semaphores. Data moves between devices by JAX's collectives and lax.ppermute only.
A program may use at most 128 MiB of HBM per device.

v0:
```python
import functools
import math

import jax
import jax.numpy as jnp
from jax import lax
from jax.experimental import pallas as pl
from jax.experimental.pallas import tpu as pltpu
from jax.sharding import PartitionSpec as P


HEADS = 8
HEAD = 128
TILE = 256
F32 = jnp.float32
BF16 = jnp.bfloat16
AXES = ("seq", "resp")

NN = (((1,), (0,)), ((), ()))
NT = (((1,), (1,)), ((), ()))
TN = (((0,), (0,)), ((), ()))


def dot(a, b, dims):
    return lax.dot_general(a, b, dims, preferred_element_type=F32)


def kept(lengths_ref):
    row = lax.axis_index("resp")
    limit = lengths_ref[jnp.maximum(row - 1, 0)]
    return jnp.logical_or(row == 0, lax.axis_index("seq") < limit)


def state_kernel(bits, lengths_ref, q_ref, k_ref, v_ref, g_ref, *outs):
    keep = kept(lengths_ref)
    place = lax.axis_index("seq")
    row = lax.axis_index("resp")
    kv = jnp.where(keep, dot(k_ref[...], v_ref[...], TN), 0.0)
    qg = jnp.where(keep, dot(q_ref[...], g_ref[...], TN), 0.0)
    for bit in range(bits):
        late = lax.rem(lax.div(place, 2**bit), 2) == 1
        outs[bit][...] = jnp.where(late, qg, kv)
    outs[bits][...] = jnp.where(row == 0, kv, qg)


def inner_kernel(factor, q_ref, k_ref, v_ref, g_ref, att_ref, gq_ref, gk_ref, gv_ref):
    tiles = q_ref.shape[0] // TILE
    cut = [pl.ds(i * TILE, TILE) for i in range(tiles)]
    q, k, v, g = ([ref[c, :] for c in cut] for ref in (q_ref, k_ref, v_ref, g_ref))
    rows = lax.broadcasted_iota(jnp.int32, (TILE, TILE), 0)
    columns = lax.broadcasted_iota(jnp.int32, (TILE, TILE), 1)
    causal = rows >= columns
    att, gq, gk, gv = ([None] * tiles for _ in range(4))

    def add(where, at, term):
        where[at] = term if where[at] is None else where[at] + term

    for i in range(tiles):
        for j in range(i + 1):
            a = dot(q[i], k[j], NT) * factor
            p = dot(g[i], v[j], NT) * factor
            if i == j:
                a = jnp.where(causal, a, 0.0)
                p = jnp.where(causal, p, 0.0)
            a = a.astype(BF16)
            p = p.astype(BF16)
            add(att, i, dot(a, v[j], NN))
            add(gq, i, dot(p, k[j], NN))
            add(gk, j, dot(p, q[i], TN))
            add(gv, j, dot(a, g[i], TN))
    for ref, parts in ((att_ref, att), (gq_ref, gq), (gk_ref, gk), (gv_ref, gv)):
        for c, part in zip(cut, parts):
            ref[c, :] = part


def outer_kernel(n, factor, lengths_ref, *refs):
    q_ref, k_ref, v_ref, g_ref = refs[:4]
    parts = refs[4:8]
    head = pl.program_id(0)
    mine = pl.ds(pl.multiple_of(head * HEAD, HEAD), HEAD)
    came = refs[8 : 8 + n - 1]
    share_ref = refs[8 + n - 1]
    outs = refs[8 + n :]
    keep = kept(lengths_ref)
    place = lax.axis_index("seq")
    row = lax.axis_index("resp")
    fs = jnp.zeros((HEAD, HEAD), F32)
    bs = jnp.zeros((HEAD, HEAD), F32)
    for m in range(1, n):
        earlier = lax.rem(lax.div(place, 2 ** (m.bit_length() - 1)), 2) == 1
        new = came[m - 1][mine, :]
        fs = fs + jnp.where(earlier, new, 0.0)
        bs = bs + jnp.where(earlier, 0.0, new)
    shared = share_ref[mine, :]
    fs = (fs + jnp.where(row == 0, 0.0, shared)).astype(BF16)
    bs = (bs + jnp.where(row == 0, shared, 0.0)).astype(BF16)
    terms = (
        dot(q_ref[...], fs, NN),
        dot(g_ref[...], fs, NT),
        dot(v_ref[...], bs, NT),
        dot(k_ref[...], bs, NN),
    )
    for out, part, term in zip(outs, parts, terms):
        out[...] = jnp.where(keep, part[:, mine] + factor * term, 0.0).astype(BF16)


def share_kernel(n, rows, came_ref, out_ref):
    prompt = jnp.zeros(came_ref.shape[1:], F32)
    answer = jnp.zeros(came_ref.shape[1:], F32)
    for s in range(n):
        prompt = prompt + came_ref[s * rows]
        for r in range(1, rows):
            answer = answer + came_ref[s * rows + r]
    for s in range(n):
        out_ref[s * rows] = answer
        for r in range(1, rows):
            out_ref[s * rows + r] = prompt


def per_device(n, rows, queries, keys, values, grad_out, lengths):
    tokens = queries.shape[1]
    width = queries.shape[2]
    factor = 1.0 / math.sqrt(2.0 * tokens * n)
    bits = n.bit_length() - 1
    q, k, v, g = (
        pltpu.with_memory_space_constraint(x.reshape(tokens, width), pltpu.HBM)
        for x in (queries, keys, values, grad_out)
    )
    token_spec = pl.BlockSpec((tokens, HEAD), lambda h, *_: (0, h))
    state_spec = pl.BlockSpec((HEAD, HEAD), lambda h, *_: (h, 0))
    whole = pl.BlockSpec(memory_space=pltpu.VMEM)
    state_shape = jax.ShapeDtypeStruct((HEADS * HEAD, HEAD), F32)
    size = tokens * width

    def line(s, r):
        return s * rows + r

    def move(x, pairs):
        return lax.ppermute(x, AXES, pairs)

    *sends, share = pl.pallas_call(
        functools.partial(state_kernel, bits),
        grid_spec=pltpu.PrefetchScalarGridSpec(
            num_scalar_prefetch=1,
            grid=(HEADS,),
            in_specs=[token_spec] * 4,
            out_specs=[state_spec] * (bits + 1),
        ),
        out_shape=[state_shape] * (bits + 1),
        compiler_params=pltpu.CompilerParams(vmem_limit_bytes=16 * 2**20),
        cost_estimate=pl.CostEstimate(
            flops=4 * size * HEAD, bytes_accessed=8 * size, transcendentals=0
        ),
    )(lengths, q, k, v, g)

    devices = n * rows
    piece = HEADS * HEAD // devices
    share = share.reshape(devices, piece, HEAD)
    share = lax.all_to_all(share, AXES, 0, 0, tiled=True)
    share = pl.pallas_call(
        functools.partial(share_kernel, n, rows),
        in_specs=[whole],
        out_specs=whole,
        out_shape=jax.ShapeDtypeStruct(share.shape, F32),
        compiler_params=pltpu.CompilerParams(vmem_limit_bytes=8 * 2**20),
    )(share)
    share = lax.all_to_all(share, AXES, 0, 0, tiled=True)
    share = share.reshape(HEADS * HEAD, HEAD)
    came = []
    for m in range(1, n):
        came.append(
            move(
                sends[m.bit_length() - 1],
                [(line(s, r), line(s ^ m, r)) for s in range(n) for r in range(rows)],
            )
        )
    part_shape = jax.ShapeDtypeStruct((tokens, width), F32)
    parts = pl.pallas_call(
        functools.partial(inner_kernel, factor),
        grid=(HEADS,),
        in_specs=[token_spec] * 4,
        out_specs=[token_spec] * 4,
        out_shape=[part_shape] * 4,
        compiler_params=pltpu.CompilerParams(vmem_limit_bytes=20 * 2**20),
        cost_estimate=pl.CostEstimate(
            flops=9 * size * tokens, bytes_accessed=24 * size, transcendentals=0
        ),
    )(q, k, v, g)
    outs = pl.pallas_call(
        functools.partial(outer_kernel, n, factor),
        grid_spec=pltpu.PrefetchScalarGridSpec(
            num_scalar_prefetch=1,
            grid=(HEADS,),
            in_specs=[token_spec] * 4 + [whole] * (n + 4),
            out_specs=[token_spec] * 4,
        ),
        out_shape=[jax.ShapeDtypeStruct((tokens, width), BF16)] * 4,
        compiler_params=pltpu.CompilerParams(vmem_limit_bytes=20 * 2**20),
        cost_estimate=pl.CostEstimate(
            flops=8 * size * HEAD, bytes_accessed=32 * size, transcendentals=0
        ),
    )(lengths, q, k, v, g, *parts, *came, share)
    return tuple(x.reshape(1, tokens, width) for x in outs)


def solution(mesh):
    n = mesh.shape["seq"]
    spec = P("resp", "seq", None)

    def body(*args):
        return per_device(n, mesh.shape["resp"], *args)

    return jax.shard_map(
        body,
        mesh=mesh,
        in_specs=(spec, spec, spec, spec, P()),
        out_specs=(spec, spec, spec, spec),
        check_vma=False,
    )
```

profile of v0, /device:TPU:0, one launch (start us, length us, event | category | flops | bytes accessed | tf_op | source)
XLA Modules:
  0.0 84.0 jit_solution(3144503230449882835)
XLA Ops:
  0.6 0.0 copy-start.10
  0.6 0.6 copy-done.10
  1.3 7.5 %shard_map.85 = (f32[1024,128]{1,0:T(8,128)}, f32[1024,128]{1,0:T(8,128)}, f32[1024,128]{1,0:T(8,128)S(1)}) custom-call(s32[7]{0:T(128)S(1)} %copy-done.10, bf16[512,1024]{1,0:T(8,128)(2,1)} %bitcast.12, bf16[512,1024]{1,0:T(8,128)(2,1)} %bitcast.15, bf16[512,1024]{1,0:T(8,128)(2,1)} %bitcast.18, bf16[512,1024]{1,0:T(8,128)(2,1)} %bitcast.21), custom_call_target="tpu_custom_call" | custom-call | flops 268435456 | bytes 4194304 | tf_op jit(solution)/shard_map/pallas_call | solution.py:141
  8.8 23.4 %all_to_all.10.came_ref = f32[32,32,128]{2,1,0:T(8,128)S(1)} all-to-all(f32[32,32,128]{2,1,0:T(8,128)S(1)} %bitcast.11), channel_id=1, replica_groups=mesh['seq'=4,'resp'=8] {'seq','resp'}, dimensions={0} | all-to-all | bytes 1048576 | tf_op jit(solution)/shard_map/all_to_all | solution.py:159
  32.1 0.9 %shard_map.86 = f32[32,32,128]{2,1,0:T(8,128)} custom-call(f32[32,32,128]{2,1,0:T(8,128)S(1)} %all_to_all.10.came_ref), custom_call_target="tpu_custom_call" | custom-call | tf_op jit(solution)/shard_map/pallas_call | solution.py:160
  33.0 2.6 %all-to-all-start.1 = ((f32[32,32,128]{2,1,0:T(8,128)}), f32[32,32,128]{2,1,0:T(8,128)S(1)}, u32[]{:S(2)}, u32[]{:S(2)}) async-start(f32[32,32,128]{2,1,0:T(8,128)} %shard_map.86), calls=%async_computation.1 | async-start | bytes 1048576 | tf_op jit(solution)/shard_map/all_to_all | solution.py:167
  35.6 1.7 %collective-permute-start = (f32[1024,128]{1,0:T(8,128)}, f32[1024,128]{1,0:T(8,128)S(1)}, u32[]{:S(2)}, u32[]{:S(2)}) collective-permute-start(f32[1024,128]{1,0:T(8,128)} %get-tuple-element.19), channel_id=1, source_target_pairs={{0,8},{1,9},{2,10},{3,11},{4,12},{5,13},{6,14},{7,15},{8,0},{9,1},... | collective-permute-start | bytes 1572872 | tf_op jit(solution)/shard_map/ppermute | solution.py:139
  37.3 0.0 copy-start.11
  37.3 1.5 %collective-permute-start.2 = (f32[1024,128]{1,0:T(8,128)}, f32[1024,128]{1,0:T(8,128)S(1)}, u32[]{:S(2)}, u32[]{:S(2)}) collective-permute-start(f32[1024,128]{1,0:T(8,128)} %get-tuple-element.20), channel_id=1, source_target_pairs={{0,24},{1,25},{2,26},{3,27},{4,28},{5,29},{6,30},{7,31},{8,16},{9,... | collective-permute-start | bytes 1572872 | tf_op jit(solution)/shard_map/ppermute | solution.py:139
  38.8 0.4 collective-permute-start.1
  39.2 10.9 %shard_map.84 = (f32[512,1024]{1,0:T(8,128)S(1)}, f32[512,1024]{1,0:T(8,128)S(1)}, f32[512,1024]{1,0:T(8,128)S(1)}, f32[512,1024]{1,0:T(8,128)S(1)}) custom-call(bf16[512,1024]{1,0:T(8,128)(2,1)} %bitcast.13, bf16[512,1024]{1,0:T(8,128)(2,1)} %bitcast.16, bf16[512,1024]{1,0:T(8,128)(2,1)} %bitcast.19, bf16[512,1024]{1,0:T(8,128)(2,1)} %bitcast.22), custom_call_target="tpu_custom_call" | custom-call | flops 2415919104 | bytes 12582912 | tf_op jit(solution)/shard_map/pallas_call | solution.py:178
  50.0 0.0 copy-start
  50.0 1.3 %copy-done = f32[512,1024]{1,0:T(8,128)} copy-done((f32[512,1024]{1,0:T(8,128)}, f32[512,1024]{1,0:T(8,128)S(1)}, u32[]{:S(2)}) %copy-start) | copy-done | bytes 2097176
  51.4 0.0 copy-start.2
  51.4 1.3 %copy-done.2 = f32[512,1024]{1,0:T(8,128)} copy-done((f32[512,1024]{1,0:T(8,128)}, f32[512,1024]{1,0:T(8,128)S(1)}, u32[]{:S(2)}) %copy-start.2) | copy-done | bytes 2097176
  52.7 0.0 copy-start.4
  52.7 1.4 %copy-done.4 = f32[512,1024]{1,0:T(8,128)} copy-done((f32[512,1024]{1,0:T(8,128)}, f32[512,1024]{1,0:T(8,128)S(1)}, u32[]{:S(2)}) %copy-start.4) | copy-done | bytes 2097176
  54.0 1.7 %collective-permute-done.refs_8_ = f32[1024,128]{1,0:T(8,128)S(1)} collective-permute-done((f32[1024,128]{1,0:T(8,128)}, f32[1024,128]{1,0:T(8,128)S(1)}, u32[]{:S(2)}, u32[]{:S(2)}) %collective-permute-start) | collective-permute-done | bytes 524320 | tf_op jit(solution)/shard_map/ppermute | solution.py:139
  55.7 11.6 %collective-permute-done.2.refs_10_ = f32[1024,128]{1,0:T(8,128)S(1)} collective-permute-done((f32[1024,128]{1,0:T(8,128)}, f32[1024,128]{1,0:T(8,128)S(1)}, u32[]{:S(2)}, u32[]{:S(2)}) %collective-permute-start.2) | collective-permute-done | bytes 524320 | tf_op jit(solution)/shard_map/ppermute | solution.py:139
  67.3 0.0 copy-start.6
  67.3 0.8 copy-done.6
  68.1 0.0 collective-permute-done.1.refs_9_
  68.1 0.0 copy-start.8
  68.1 0.8 copy-done.8
  68.9 0.0 all-to-all-done.1
  68.9 0.0 copy-done.11
  68.9 0.0 copy-start.1
  68.9 1.6 %copy-done.1 = f32[512,1024]{1,0:T(8,128)S(1)} copy-done((f32[512,1024]{1,0:T(8,128)S(1)}, f32[512,1024]{1,0:T(8,128)}, u32[]{:S(2)}) %copy-start.1) | copy-done | bytes 2097176
  70.5 0.0 copy-start.3
  70.5 1.6 %copy-done.3 = f32[512,1024]{1,0:T(8,128)S(1)} copy-done((f32[512,1024]{1,0:T(8,128)S(1)}, f32[512,1024]{1,0:T(8,128)}, u32[]{:S(2)}) %copy-start.3) | copy-done | bytes 2097176
  72.1 0.0 copy-start.5
  72.1 1.6 %copy-done.5 = f32[512,1024]{1,0:T(8,128)S(1)} copy-done((f32[512,1024]{1,0:T(8,128)S(1)}, f32[512,1024]{1,0:T(8,128)}, u32[]{:S(2)}) %copy-start.5) | copy-done | bytes 2097176
  73.7 0.0 copy-start.7
  73.7 1.0 %copy-done.7 = f32[1024,128]{1,0:T(8,128)S(1)} copy-done((f32[1024,128]{1,0:T(8,128)S(1)}, f32[1024,128]{1,0:T(8,128)}, u32[]{:S(2)}) %copy-start.7) | copy-done | bytes 524312
  74.7 0.0 copy-start.9
  74.7 1.0 %copy-done.9 = f32[1024,128]{1,0:T(8,128)S(1)} copy-done((f32[1024,128]{1,0:T(8,128)S(1)}, f32[1024,128]{1,0:T(8,128)}, u32[]{:S(2)}) %copy-start.9) | copy-done | bytes 524312
  75.8 8.2 %shard_map.87 = (bf16[512,1024]{1,0:T(8,128)(2,1)}, bf16[512,1024]{1,0:T(8,128)(2,1)}, bf16[512,1024]{1,0:T(8,128)(2,1)}, bf16[512,1024]{1,0:T(8,128)(2,1)}) custom-call(s32[7]{0:T(128)S(1)} %copy-done.11, bf16[512,1024]{1,0:T(8,128)(2,1)} %bitcast.14, bf16[512,1024]{1,0:T(8,128)(2,1)} %bitcast.17, bf16[512,1024]{1,0:T(8,128)(2,1)} %bitcast.20, ...), custom_call_target="tpu_custom_call" | custom-call | flops 536870912 | bytes 16777216 | tf_op jit(solution)/shard_map/pallas_call | solution.py:189
Async XLA Ops:
  0.6 0.7 copy-start.10
  33.0 35.9 %all-to-all-start.1 = ((f32[32,32,128]{2,1,0:T(8,128)}), f32[32,32,128]{2,1,0:T(8,128)S(1)}, u32[]{:S(2)}, u32[]{:S(2)}) async-start(f32[32,32,128]{2,1,0:T(8,128)} %shard_map.86), calls=%async_computation.1 | async-start | bytes 1048576 | tf_op jit(solution)/shard_map/all_to_all | solution.py:167
  35.6 20.1 %collective-permute-start = (f32[1024,128]{1,0:T(8,128)}, f32[1024,128]{1,0:T(8,128)S(1)}, u32[]{:S(2)}, u32[]{:S(2)}) collective-permute-start(f32[1024,128]{1,0:T(8,128)} %get-tuple-element.19), channel_id=1, source_target_pairs={{0,8},{1,9},{2,10},{3,11},{4,12},{5,13},{6,14},{7,15},{8,0},{9,1},... | collective-permute-start | bytes 1572872 | tf_op jit(solution)/shard_map/ppermute | solution.py:139
  37.3 31.6 %copy-start.11 = (s32[7]{0:T(128)S(1)}, s32[7]{0:T(128)}, u32[]{:S(2)}) copy-start(s32[7]{0:T(128)} %lengths_ref.3) | copy-start | bytes 88
  37.3 30.0 %collective-permute-start.2 = (f32[1024,128]{1,0:T(8,128)}, f32[1024,128]{1,0:T(8,128)S(1)}, u32[]{:S(2)}, u32[]{:S(2)}) collective-permute-start(f32[1024,128]{1,0:T(8,128)} %get-tuple-element.20), channel_id=1, source_target_pairs={{0,24},{1,25},{2,26},{3,27},{4,28},{5,29},{6,30},{7,31},{8,16},{9,... | collective-permute-start | bytes 1572872 | tf_op jit(solution)/shard_map/ppermute | solution.py:139
  38.8 29.3 %collective-permute-start.1 = (f32[1024,128]{1,0:T(8,128)}, f32[1024,128]{1,0:T(8,128)S(1)}, u32[]{:S(2)}, u32[]{:S(2)}) collective-permute-start(f32[1024,128]{1,0:T(8,128)} %get-tuple-element.20), channel_id=1, source_target_pairs={{0,16},{1,17},{2,18},{3,19},{4,20},{5,21},{6,22},{7,23},{8,24},{9,... | collective-permute-start | bytes 1572872 | tf_op jit(solution)/shard_map/ppermute | solution.py:139
  50.0 1.3 %copy-start = (f32[512,1024]{1,0:T(8,128)}, f32[512,1024]{1,0:T(8,128)S(1)}, u32[]{:S(2)}) copy-start(f32[512,1024]{1,0:T(8,128)S(1)} %get-tuple-element.16.refs_5_) | copy-start | bytes 6291460
  51.4 1.3 %copy-start.2 = (f32[512,1024]{1,0:T(8,128)}, f32[512,1024]{1,0:T(8,128)S(1)}, u32[]{:S(2)}) copy-start(f32[512,1024]{1,0:T(8,128)S(1)} %get-tuple-element.17.refs_6_) | copy-start | bytes 6291460
  52.7 1.4 %copy-start.4 = (f32[512,1024]{1,0:T(8,128)}, f32[512,1024]{1,0:T(8,128)S(1)}, u32[]{:S(2)}) copy-start(f32[512,1024]{1,0:T(8,128)S(1)} %get-tuple-element.18.refs_7_) | copy-start | bytes 6291460
  67.3 0.8 copy-start.6
  68.1 0.8 copy-start.8
  68.9 1.6 %copy-start.1 = (f32[512,1024]{1,0:T(8,128)S(1)}, f32[512,1024]{1,0:T(8,128)}, u32[]{:S(2)}) copy-start(f32[512,1024]{1,0:T(8,128)} %copy-done) | copy-start | bytes 6291460
  70.5 1.6 %copy-start.3 = (f32[512,1024]{1,0:T(8,128)S(1)}, f32[512,1024]{1,0:T(8,128)}, u32[]{:S(2)}) copy-start(f32[512,1024]{1,0:T(8,128)} %copy-done.2) | copy-start | bytes 6291460
  72.1 1.6 %copy-start.5 = (f32[512,1024]{1,0:T(8,128)S(1)}, f32[512,1024]{1,0:T(8,128)}, u32[]{:S(2)}) copy-start(f32[512,1024]{1,0:T(8,128)} %copy-done.4) | copy-start | bytes 6291460
  73.7 1.0 %copy-start.7 = (f32[1024,128]{1,0:T(8,128)S(1)}, f32[1024,128]{1,0:T(8,128)}, u32[]{:S(2)}) copy-start(f32[1024,128]{1,0:T(8,128)} %copy-done.6) | copy-start | bytes 1572868
  74.7 1.0 %copy-start.9 = (f32[1024,128]{1,0:T(8,128)S(1)}, f32[1024,128]{1,0:T(8,128)}, u32[]{:S(2)}) copy-start(f32[1024,128]{1,0:T(8,128)} %copy-done.8) | copy-start | bytes 1572868
where the time goes:
time: 84.8 us; the launch traced here: 84 us
  Pallas kernels  27.4 us (32%)
  blocking collectives  23.4 us (28%)
  waiting for transfers between devices  13.3 us (16%)
  local copies, waits for them, and re-layouts  13.1 us (15%)
  starting transfers between devices  6.16 us (7%)
    all_to_all x1, blocking collectives, per_device(): share = lax.all_to_all(share, AXES, 0, 0, tiled=True)  23.4 us
    ppermute x3, waiting for transfers between devices, move(): return lax.ppermute(x, AXES, pairs)  13.3 us
    unnamed x24, local copies, waits for them, and re-layouts  13.1 us
    pallas_call x1, Pallas kernels, per_device(): pl.pallas_call(functools.partial(inner_kernel, factor), grid=(HEADS,), in...  10.9 us
    pallas_call x1, Pallas kernels, per_device(): pl.pallas_call(functools.partial(outer_kernel, n, factor), grid_spec=pltp...  8.24 us
    pallas_call x1, Pallas kernels, per_device(): pl.pallas_call(functools.partial(state_kernel, bits), grid_spec=pltpu.Pre...  7.47 us
    ppermute x3, starting transfers between devices, move(): return lax.ppermute(x, AXES, pairs)  3.55 us
    all_to_all x1, starting transfers between devices, per_device(): share = lax.all_to_all(share, AXES, 0, 0, tiled=True)  2.61 us
  transfers between devices with their start and end apart: 4, of which 2 were waited for; matrix products, arithmetic and copies ran while one was open for 0% of the time, Pallas kernels for 13%

commit v1 on v0

v1 whole, which is shorter than its diff:
```python
import functools
import math

import jax
import jax.numpy as jnp
from jax import lax
from jax.experimental import pallas as pl
from jax.experimental.pallas import tpu as pltpu
from jax.sharding import PartitionSpec as P


HEADS = 8
HEAD = 128
TILE = 256
GROUPS = 4
STATE_VMEM = 12
WRITE = 4
F32 = jnp.float32
BF16 = jnp.bfloat16
AXES = ("seq", "resp")

NN = (((1,), (0,)), ((), ()))
NT = (((1,), (1,)), ((), ()))
TN = (((0,), (0,)), ((), ()))


def dot(a, b, dims):
    return lax.dot_general(a, b, dims, preferred_element_type=F32)


def kept(lengths_ref):
    row = lax.axis_index("resp")
    limit = lengths_ref[jnp.maximum(row - 1, 0)]
    return jnp.logical_or(row == 0, lax.axis_index("seq") < limit)


def state_kernel(n, *refs):
    ins = refs[:5]
    share_refs = refs[5 : 5 + n]
    rest_refs = refs[5 + n : 5 + 2 * n]
    q_ref, k_ref, v_ref, g_ref = held = refs[5 + 2 * n : 9 + 2 * n]
    share, rest, lengths_ref, sem = refs[9 + 2 * n :]
    piece = share_refs[0].shape[0]
    counts = pltpu.make_async_copy(ins[4], lengths_ref, sem.at[4])
    counts.start()
    copies = [pltpu.make_async_copy(ins[i], held[i], sem.at[i]) for i in (1, 2, 0, 3)]
    for copy in copies:
        copy.start()
    place = lax.axis_index("seq")
    prompt = lax.axis_index("resp") == 0
    heads = [pl.ds(h * HEAD, HEAD) for h in range(HEADS)]
    counts.wait()
    keep = kept(lengths_ref)
    copies[0].wait()
    copies[1].wait()
    for h in heads:
        rest[h, :] = jnp.where(keep, dot(k_ref[:, h], v_ref[:, h], TN), 0.0)
    copies[2].wait()
    copies[3].wait()
    for h in heads:
        kv = rest[h, :]
        qg = jnp.where(keep, dot(q_ref[:, h], g_ref[:, h], TN), 0.0)
        share[h, :] = jnp.where(prompt, kv, qg)
        rest[h, :] = jnp.where(prompt, qg, kv)
    for m in range(n):
        at = pl.multiple_of(jnp.bitwise_xor(place, m) * piece, piece)
        share_refs[m][...] = share[pl.ds(at, piece), :]
        rest_refs[m][...] = rest[pl.ds(at, piece), :]


def inner_kernel(factor, first, q_ref, k_ref, v_ref, g_ref, *outs):
    tiles = q_ref.shape[0] // TILE
    cut = [pl.ds(i * TILE, TILE) for i in range(tiles)]
    rows = lax.broadcasted_iota(jnp.int32, (TILE, TILE), 0)
    columns = lax.broadcasted_iota(jnp.int32, (TILE, TILE), 1)
    causal = rows >= columns
    for h in range(outs[0].shape[1] // HEAD):
        here = pl.ds((first + h) * HEAD, HEAD)
        q, k, v, g = ([ref[c, here] for c in cut] for ref in (q_ref, k_ref, v_ref, g_ref))
        sums = [[None] * tiles for _ in range(4)]

        def add(which, at, term):
            old = sums[which][at]
            sums[which][at] = term if old is None else old + term

        for i in range(tiles):
            for j in range(i + 1):
                a = dot(q[i], k[j], NT) * factor
                p = dot(g[i], v[j], NT) * factor
                if i == j:
                    a = jnp.where(causal, a, 0.0)
                    p = jnp.where(causal, p, 0.0)
                a = a.astype(BF16)
                p = p.astype(BF16)
                add(0, i, dot(a, v[j], NN))
                add(1, i, dot(p, k[j], NN))
                add(2, j, dot(p, q[i], TN))
                add(3, j, dot(a, g[i], TN))
        for ref, parts in zip(outs, sums):
            for c, part in zip(cut, parts):
                ref[c, pl.ds(h * HEAD, HEAD)] = part


def outer_kernel(factor, groups, n, lengths_hbm, *refs):
    q_ref, k_ref, v_ref, g_ref = refs[:4]
    parts = refs[4 : 4 + 4 * groups]
    refs = refs[4 + 4 * groups :]
    share_refs, rest_refs = refs[:n], refs[n : 2 * n]
    outs = refs[2 * n : 2 * n + 4]
    buffers = refs[2 * n + 4 : 2 * n + 8]
    share, rest, lengths_ref, sem, count_sem = refs[2 * n + 8 :]
    counts = pltpu.make_async_copy(lengths_hbm, lengths_ref, count_sem)
    counts.start()
    place = lax.axis_index("seq")
    prompt = lax.axis_index("resp") == 0
    piece = share_refs[0].shape[0]
    for m in range(n):
        at = pl.multiple_of(jnp.bitwise_xor(place, m) * piece, piece)
        share[pl.ds(at, piece), :] = share_refs[m][...]
        rest[pl.ds(at, piece), :] = rest_refs[m][...]
    counts.wait()
    keep = kept(lengths_ref)
    span = HEADS // groups
    copies = []
    for head in range(HEADS):
        h = pl.ds(head * HEAD, HEAD)
        within = pl.ds(head % span * HEAD, HEAD)
        fs = jnp.where(prompt, share[h, :], rest[h, :]).astype(BF16)
        bs = jnp.where(prompt, rest[h, :], share[h, :]).astype(BF16)
        sides = ((q_ref, fs, NN), (g_ref, fs, NT), (v_ref, bs, NT), (k_ref, bs, NN))
        for which, (ref, state, dims) in enumerate(sides):
            part = parts[head // span * 4 + which][:, within]
            total = part + factor * dot(ref[:, h], state, dims)
            buffers[which][:, h] = jnp.where(keep, total, 0.0).astype(BF16)
        if head % WRITE == WRITE - 1:
            at = head // WRITE
            wide = pl.ds(at * WRITE * HEAD, WRITE * HEAD)
            for which in range(4):
                copy = pltpu.make_async_copy(
                    buffers[which].at[:, wide], outs[which].at[:, wide], sem.at[which, at]
                )
                copy.start()
                copies.append(copy)
    for copy in copies:
        copy.wait()


def step_kernel(step, total_ref, new_ref, answer_ref, total_out, answer_out):
    row = lax.axis_index("resp")
    gets = jnp.logical_and(row >= step, row < 2 * step)
    total = total_ref[...]
    new = new_ref[...]
    summed = jnp.where(row == 0, total, total + new)
    total_out[...] = jnp.where(gets, new, summed)
    answer_out[...] = answer_ref[...] + new if step > 1 else new


def scan_kernel(n, step, *refs):
    place = lax.axis_index("seq")
    row = lax.axis_index("resp")
    prompt = row == 0
    count = n + 3 if step else n
    came = refs[:count]
    outs = refs[count : count + n]
    order, sums = refs[-2:]
    for m in range(n):
        order[jnp.bitwise_xor(place, m)] = came[m][...]
    if step:
        gets = jnp.logical_and(row >= step, row < 2 * step)
        total, new, answer = (ref[...] for ref in came[n:])
        forward = jnp.logical_not(prompt)
        before = jnp.where(prompt, answer + new, jnp.where(gets, new, total))
    else:
        forward = prompt
        before = jnp.zeros(order.shape[1:], F32)
    after = before
    for s in range(n):
        sums[s] = before
        before = before + order[s]
    for s in reversed(range(n)):
        sums[s] = jnp.where(forward, sums[s], after)
        after = after + order[s]
    for m in range(n):
        outs[m][...] = sums[jnp.bitwise_xor(place, m)]
    if not step:
        refs[count + n][...] = before


def per_device(n, rows, queries, keys, values, grad_out, lengths):
    tokens = queries.shape[1]
    width = queries.shape[2]
    factor = 1.0 / math.sqrt(2.0 * tokens * n)
    q, k, v, g = (x.reshape(tokens, width) for x in (queries, keys, values, grad_out))
    whole = pl.BlockSpec(memory_space=pltpu.VMEM)
    size = tokens * width

    def line(s, r):
        return s * rows + r

    def move(x, pairs):
        return lax.ppermute(x, AXES, pairs)

    there = pl.BlockSpec(memory_space=pltpu.HBM)
    array = pltpu.VMEM((tokens, width), BF16)
    stack = pltpu.VMEM((HEADS * HEAD, HEAD), F32)
    counts = pltpu.SMEM(lengths.shape, jnp.int32)
    piece = HEADS * HEAD // n
    piece_shape = jax.ShapeDtypeStruct((piece, HEAD), F32)
    small = pltpu.CompilerParams(vmem_limit_bytes=6 * 2**20)

    def far(x):
        return pltpu.with_memory_space_constraint(x, pltpu.HBM)

    *pieces, q, k, v, g = pl.pallas_call(
        functools.partial(state_kernel, n),
        in_specs=[there] * 5,
        out_specs=[whole] * (2 * n + 4),
        scratch_shapes=[stack] * 2 + [counts, pltpu.SemaphoreType.DMA((5,))],
        out_shape=[piece_shape] * (2 * n) + [jax.ShapeDtypeStruct((tokens, width), BF16)] * 4,
        compiler_params=pltpu.CompilerParams(vmem_limit_bytes=STATE_VMEM * 2**20),
        cost_estimate=pl.CostEstimate(
            flops=4 * size * HEAD, bytes_accessed=8 * size, transcendentals=0
        ),
    )(far(q), far(k), far(v), far(g), far(lengths))

    def swapped(pieces):
        came = [pieces[0]]
        for m in range(1, n):
            came.append(
                move(
                    pieces[m],
                    [(line(s, r), line(s ^ m, r)) for s in range(n) for r in range(rows)],
                )
            )
        return came

    def scan(step, *pieces):
        outputs = n if step else n + 1
        return pl.pallas_call(
            functools.partial(scan_kernel, n, step),
            in_specs=[whole] * len(pieces),
            out_specs=[whole] * outputs,
            out_shape=[piece_shape] * outputs,
            scratch_shapes=[pltpu.VMEM((n, piece, HEAD), F32)] * 2,
            compiler_params=small,
        )(*pieces)

    *share, total = scan(0, *swapped(pieces[:n]))
    rest = swapped(pieces[n:])
    share = swapped(share)
    answer = total
    step = 1
    while step < rows:
        pairs = [
            (line(s, at), line(s, at ^ step))
            for s in range(n)
            for at in range(rows)
            if at < step or (at % step == 0 and at & step)
        ]
        new = move(total, pairs)
        if 2 * step == rows:
            break
        total, answer = pl.pallas_call(
            functools.partial(step_kernel, step),
            in_specs=[whole] * 3,
            out_specs=[whole] * 2,
            out_shape=[piece_shape] * 2,
            compiler_params=small,
        )(total, new, answer)
        step *= 2
    rest = swapped(scan(step, *rest, total, new, answer))
    parts = []
    part_shape = jax.ShapeDtypeStruct((tokens, width // GROUPS), F32)
    for group in range(GROUPS):
        parts += pl.pallas_call(
            functools.partial(inner_kernel, factor, group * HEADS // GROUPS),
            in_specs=[whole] * 4,
            out_specs=[whole] * 4,
            out_shape=[part_shape] * 4,
            compiler_params=small,
            cost_estimate=pl.CostEstimate(
                flops=9 * size * tokens // GROUPS,
                bytes_accessed=24 * size // GROUPS,
                transcendentals=0,
            ),
        )(q, k, v, g)
    outs = pl.pallas_call(
        functools.partial(outer_kernel, factor, GROUPS, n),
        in_specs=[there] + [whole] * (4 + 4 * GROUPS + 2 * n),
        out_specs=[there] * 4,
        scratch_shapes=[array] * 4
        + [stack] * 2
        + [
            counts,
            pltpu.SemaphoreType.DMA((4, HEADS // WRITE)),
            pltpu.SemaphoreType.DMA,
        ],
        out_shape=[jax.ShapeDtypeStruct((tokens, width), BF16)] * 4,
        compiler_params=pltpu.CompilerParams(vmem_limit_bytes=12 * 2**20),
        cost_estimate=pl.CostEstimate(
            flops=8 * size * HEAD, bytes_accessed=32 * size, transcendentals=0
        ),
    )(far(lengths), q, k, v, g, *parts, *share, *rest)
    return tuple(x.reshape(1, tokens, width) for x in outs)


def solution(mesh):
    n = mesh.shape["seq"]
    spec = P("resp", "seq", None)

    def body(*args):
        return per_device(n, mesh.shape["resp"], *args)

    return jax.shard_map(
        body,
        mesh=mesh,
        in_specs=(spec, spec, spec, spec, P()),
        out_specs=(spec, spec, spec, spec),
        check_vma=False,
    )
```

time: 84.8 us -> 48.4 us (0.57)
  blocking collectives: 23.4 us -> 0 us
  starting transfers between devices: 6.16 us -> 25 us
  local copies, waits for them, and re-layouts: 13.1 us -> 0 us
  Pallas kernels: 27.4 us -> 14.8 us
  waiting for transfers between devices: 13.3 us -> 7.58 us
    all_to_all x1 -> x0, blocking collectives: 23.4 us -> none  [per_device(): share = lax.all_to_all(share, AXES, 0, 0, tiled=True)]
    ppermute x3 -> x15, starting transfers between devices: 3.55 us -> 25 us  [move(): return lax.ppermute(x, AXES, pairs)]
    unnamed x24 -> x0, local copies, waits for them, and re-layouts: 13.1 us -> none
    pallas_call x4 -> x10, Pallas kernels: 27.4 us -> 14.8 us  [the longest x4 7.82 us: per_device(): pl.pallas_call(functools.partial(inner_kernel, factor, group * HEADS // G...]
    ppermute x3 -> x15, waiting for transfers between devices: 13.3 us -> 7.58 us  [move(): return lax.ppermute(x, AXES, pairs)]
    all_to_all x1 -> x0, starting transfers between devices: 2.61 us -> none  [per_device(): share = lax.all_to_all(share, AXES, 0, 0, tiled=True)]
  transfers between devices with their start and end apart: 4 -> 15, of which waited for: 2 -> 3; matrix products, arithmetic and copies ran while one was open for 0% -> 0% of each run, Pallas kernels for 13% -> 17%
where the time goes in v1:
time: 48.4 us; the launch traced here: 48.2 us
  starting transfers between devices  25 us (52%)
  Pallas kernels  14.8 us (31%)
  waiting for transfers between devices  7.58 us (16%)
  between operations  0.76 us (2%)
    ppermute x15, starting transfers between devices, move(): return lax.ppermute(x, AXES, pairs)  25 us
    pallas_call x4, Pallas kernels, per_device(): pl.pallas_call(functools.partial(inner_kernel, factor, group * HEADS // G...  7.82 us
    ppermute x15, waiting for transfers between devices, move(): return lax.ppermute(x, AXES, pairs)  7.58 us
    pallas_call x1, Pallas kernels, per_device(): pl.pallas_call(functools.partial(outer_kernel, factor, GROUPS, n), in_spe...  3.8 us
    pallas_call x1, Pallas kernels, per_device(): pl.pallas_call(functools.partial(state_kernel, n), in_specs=[there] * 5,...  2.83 us
  transfers between devices with their start and end apart: 15, of which 3 were waited for; matrix products, arithmetic and copies ran while one was open for 0% of the time, Pallas kernels for 17%

profile of v1, /device:TPU:0, one launch (start us, length us, event | category | flops | bytes accessed | tf_op | source)
XLA Modules:
  0.0 48.2 jit_solution(1778786492705195786)
XLA Ops:
  0.6 2.8 %shard_map.84 = (f32[256,128]{1,0:T(8,128)S(1)}, f32[256,128]{1,0:T(8,128)S(1)}, f32[256,128]{1,0:T(8,128)S(1)}, f32[256,128]{1,0:T(8,128)S(1)}, f32[256,128]{1,...) custom-call(bf16[512,1024]{1,0:T(8,128)(2,1)} %bitcast.8, ...), custom_call_target="tpu_custom_call" | custom-call | flops 268435456 | bytes 4194304 | tf_op jit(solution)/shard_map/pallas_call | solution.py:214
  3.5 3.0 %collective-permute-start = (f32[256,128]{1,0:T(8,128)S(1)}, f32[256,128]{1,0:T(8,128)S(1)}, u32[]{:S(2)}, u32[]{:S(2)}) collective-permute-start(f32[256,128]{1,0:T(8,128)S(1)} %get-tuple-element.70), channel_id=1, source_target_pairs={{0,8},{1,9},{2,10},{3,11},{4,12},{5,13},{6,14},{7,15},{8,0},{9,1},... | collective-permute-start | bytes 393224 | tf_op jit(solution)/shard_map/ppermute | solution.py:201
  6.5 1.5 %collective-permute-start.1 = (f32[256,128]{1,0:T(8,128)S(1)}, f32[256,128]{1,0:T(8,128)S(1)}, u32[]{:S(2)}, u32[]{:S(2)}) collective-permute-start(f32[256,128]{1,0:T(8,128)S(1)} %get-tuple-element.71), channel_id=1, source_target_pairs={{0,16},{1,17},{2,18},{3,19},{4,20},{5,21},{6,22},{7,23},{8,24},{9,... | collective-permute-start | bytes 393224 | tf_op jit(solution)/shard_map/ppermute | solution.py:201
  8.0 0.0 collective-permute-start.2
  8.0 2.3 %collective-permute-done.refs_1_ = f32[256,128]{1,0:T(8,128)S(1)} collective-permute-done((f32[256,128]{1,0:T(8,128)S(1)}, f32[256,128]{1,0:T(8,128)S(1)}, u32[]{:S(2)}, u32[]{:S(2)}) %collective-permute-start) | collective-permute-done | bytes 131104 | tf_op jit(solution)/shard_map/ppermute | solution.py:201
  10.4 3.9 %collective-permute-done.1.refs_2_ = f32[256,128]{1,0:T(8,128)S(1)} collective-permute-done((f32[256,128]{1,0:T(8,128)S(1)}, f32[256,128]{1,0:T(8,128)S(1)}, u32[]{:S(2)}, u32[]{:S(2)}) %collective-permute-start.1) | collective-permute-done | bytes 131104 | tf_op jit(solution)/shard_map/ppermute | solution.py:201
  14.3 0.0 collective-permute-done.2.refs_3_
  14.3 0.2 shard_map.89
  14.5 1.9 %collective-permute-start.9 = (f32[256,128]{1,0:T(8,128)S(1)}, f32[256,128]{1,0:T(8,128)S(1)}, u32[]{:S(2)}, u32[]{:S(2)}) collective-permute-start(f32[256,128]{1,0:T(8,128)S(1)} %get-tuple-element.81.total_ref.answer_ref), channel_id=1, source_target_pairs={{0,1},{1,0},{3,2},{5,4},{7,6},{8,9},{9,8},{11,10},{13,12},{15,14},... | collective-permute-start | bytes 393224 | tf_op jit(solution)/shard_map/ppermute | solution.py:201
  16.4 1.3 %collective-permute-done.9.new_ref = f32[256,128]{1,0:T(8,128)S(1)} collective-permute-done((f32[256,128]{1,0:T(8,128)S(1)}, f32[256,128]{1,0:T(8,128)S(1)}, u32[]{:S(2)}, u32[]{:S(2)}) %collective-permute-start.9) | collective-permute-done | bytes 131104 | tf_op jit(solution)/shard_map/ppermute | solution.py:201
  17.7 3.5 %collective-permute-start.10 = (f32[256,128]{1,0:T(8,128)S(1)}, f32[256,128]{1,0:T(8,128)S(1)}, u32[]{:S(2)}, u32[]{:S(2)}) collective-permute-start(f32[256,128]{1,0:T(8,128)S(1)} %get-tuple-element.82.total_ref), channel_id=1, source_target_pairs={{0,2},{1,3},{2,0},{6,4},{8,10},{9,11},{10,8},{14,12},{16,18},{17,1... | collective-permute-start | bytes 393224 | tf_op jit(solution)/shard_map/ppermute | solution.py:201
  21.2 1.3 %collective-permute-start.6 = (f32[256,128]{1,0:T(8,128)S(1)}, f32[256,128]{1,0:T(8,128)S(1)}, u32[]{:S(2)}, u32[]{:S(2)}) collective-permute-start(f32[256,128]{1,0:T(8,128)S(1)} %get-tuple-element.78), channel_id=1, source_target_pairs={{0,8},{1,9},{2,10},{3,11},{4,12},{5,13},{6,14},{7,15},{8,0},{9,1},... | collective-permute-start | bytes 393224 | tf_op jit(solution)/shard_map/ppermute | solution.py:201
  22.5 0.8 %collective-permute-start.7 = (f32[256,128]{1,0:T(8,128)S(1)}, f32[256,128]{1,0:T(8,128)S(1)}, u32[]{:S(2)}, u32[]{:S(2)}) collective-permute-start(f32[256,128]{1,0:T(8,128)S(1)} %get-tuple-element.79), channel_id=1, source_target_pairs={{0,16},{1,17},{2,18},{3,19},{4,20},{5,21},{6,22},{7,23},{8,24},{9,... | collective-permute-start | bytes 393224 | tf_op jit(solution)/shard_map/ppermute | solution.py:201
  23.3 1.4 %collective-permute-start.8 = (f32[256,128]{1,0:T(8,128)S(1)}, f32[256,128]{1,0:T(8,128)S(1)}, u32[]{:S(2)}, u32[]{:S(2)}) collective-permute-start(f32[256,128]{1,0:T(8,128)S(1)} %get-tuple-element.80), channel_id=1, source_target_pairs={{0,24},{1,25},{2,26},{3,27},{4,28},{5,29},{6,30},{7,31},{8,16},{9,... | collective-permute-start | bytes 393224 | tf_op jit(solution)/shard_map/ppermute | solution.py:201
  24.8 0.0 collective-permute-done.10.new_ref
  24.8 4.3 %collective-permute-start.11 = (f32[256,128]{1,0:T(8,128)S(1)}, f32[256,128]{1,0:T(8,128)S(1)}, u32[]{:S(2)}, u32[]{:S(2)}) collective-permute-start(f32[256,128]{1,0:T(8,128)S(1)} %get-tuple-element.84.refs_4_), channel_id=1, source_target_pairs={{0,4},{1,5},{2,6},{3,7},{4,0},{8,12},{9,13},{10,14},{11,15},{12,8}... | collective-permute-start | bytes 393224 | tf_op jit(solution)/shard_map/ppermute | solution.py:201
  29.1 1.3 %collective-permute-start.3 = (f32[256,128]{1,0:T(8,128)S(1)}, f32[256,128]{1,0:T(8,128)S(1)}, u32[]{:S(2)}, u32[]{:S(2)}) collective-permute-start(f32[256,128]{1,0:T(8,128)S(1)} %get-tuple-element.74), channel_id=1, source_target_pairs={{0,8},{1,9},{2,10},{3,11},{4,12},{5,13},{6,14},{7,15},{8,0},{9,1},... | collective-permute-start | bytes 393224 | tf_op jit(solution)/shard_map/ppermute | solution.py:201
  30.4 2.0 %shard_map.88 = (f32[512,256]{1,0:T(8,128)S(1)}, f32[512,256]{1,0:T(8,128)S(1)}, f32[512,256]{1,0:T(8,128)S(1)}, f32[512,256]{1,0:T(8,128)S(1)}) custom-call(bf16[512,1024]{1,0:T(8,128)(2,1)S(1)} %get-tuple-element.49.q_ref.refs_0_, bf16[512,1024]{1,0:T(8,128)(2,1)S(1)} %get-tuple-element.50.k_ref.refs_1_, ...), custom_call_target="tpu_custom_call" | custom-call | flops 603979776 | bytes 3145728 | tf_op jit(solution)/shard_map/pallas_call | solution.py:275
  32.4 0.0 collective-permute-done.6.refs_1_
  32.4 0.8 %collective-permute-start.4 = (f32[256,128]{1,0:T(8,128)S(1)}, f32[256,128]{1,0:T(8,128)S(1)}, u32[]{:S(2)}, u32[]{:S(2)}) collective-permute-start(f32[256,128]{1,0:T(8,128)S(1)} %get-tuple-element.75), channel_id=1, source_target_pairs={{0,16},{1,17},{2,18},{3,19},{4,20},{5,21},{6,22},{7,23},{8,24},{9,... | collective-permute-start | bytes 393224 | tf_op jit(solution)/shard_map/ppermute | solution.py:201
  33.3 0.0 collective-permute-done.7.refs_2_
  33.3 1.5 %collective-permute-start.5 = (f32[256,128]{1,0:T(8,128)S(1)}, f32[256,128]{1,0:T(8,128)S(1)}, u32[]{:S(2)}, u32[]{:S(2)}) collective-permute-start(f32[256,128]{1,0:T(8,128)S(1)} %get-tuple-element.76), channel_id=1, source_target_pairs={{0,24},{1,25},{2,26},{3,27},{4,28},{5,29},{6,30},{7,31},{8,16},{9,... | collective-permute-start | bytes 393224 | tf_op jit(solution)/shard_map/ppermute | solution.py:201
  34.7 0.0 collective-permute-done.8.refs_3_
  34.7 0.0 collective-permute-done.11.refs_5_
  34.7 0.2 shard_map.92
  34.9 1.3 %collective-permute-start.12 = (f32[256,128]{1,0:T(8,128)S(1)}, f32[256,128]{1,0:T(8,128)S(1)}, u32[]{:S(2)}, u32[]{:S(2)}) collective-permute-start(f32[256,128]{1,0:T(8,128)S(1)} %get-tuple-element.87), channel_id=1, source_target_pairs={{0,8},{1,9},{2,10},{3,11},{4,12},{5,13},{6,14},{7,15},{8,0},{9,1},... | collective-permute-start | bytes 393224 | tf_op jit(solution)/shard_map/ppermute | solution.py:201
  36.2 0.8 %collective-permute-start.13 = (f32[256,128]{1,0:T(8,128)S(1)}, f32[256,128]{1,0:T(8,128)S(1)}, u32[]{:S(2)}, u32[]{:S(2)}) collective-permute-start(f32[256,128]{1,0:T(8,128)S(1)} %get-tuple-element.88), channel_id=1, source_target_pairs={{0,16},{1,17},{2,18},{3,19},{4,20},{5,21},{6,22},{7,23},{8,24},{9,... | collective-permute-start | bytes 393224 | tf_op jit(solution)/shard_map/ppermute | solution.py:201
  37.0 0.0 collective-permute-done.3.refs_21_
  37.0 1.5 %collective-permute-start.14 = (f32[256,128]{1,0:T(8,128)S(1)}, f32[256,128]{1,0:T(8,128)S(1)}, u32[]{:S(2)}, u32[]{:S(2)}) collective-permute-start(f32[256,128]{1,0:T(8,128)S(1)} %get-tuple-element.89), channel_id=1, source_target_pairs={{0,24},{1,25},{2,26},{3,27},{4,28},{5,29},{6,30},{7,31},{8,16},{9,... | collective-permute-start | bytes 393224 | tf_op jit(solution)/shard_map/ppermute | solution.py:201
  38.5 1.9 %shard_map.87 = (f32[512,256]{1,0:T(8,128)S(1)}, f32[512,256]{1,0:T(8,128)S(1)}, f32[512,256]{1,0:T(8,128)S(1)}, f32[512,256]{1,0:T(8,128)S(1)}) custom-call(bf16[512,1024]{1,0:T(8,128)(2,1)S(1)} %get-tuple-element.49.q_ref.refs_0_, bf16[512,1024]{1,0:T(8,128)(2,1)S(1)} %get-tuple-element.50.k_ref.refs_1_, ...), custom_call_target="tpu_custom_call" | custom-call | flops 603979776 | bytes 3145728 | tf_op jit(solution)/shard_map/pallas_call | solution.py:275
  40.4 1.9 %shard_map.86 = (f32[512,256]{1,0:T(8,128)S(1)}, f32[512,256]{1,0:T(8,128)S(1)}, f32[512,256]{1,0:T(8,128)S(1)}, f32[512,256]{1,0:T(8,128)S(1)}) custom-call(bf16[512,1024]{1,0:T(8,128)(2,1)S(1)} %get-tuple-element.49.q_ref.refs_0_, bf16[512,1024]{1,0:T(8,128)(2,1)S(1)} %get-tuple-element.50.k_ref.refs_1_, ...), custom_call_target="tpu_custom_call" | custom-call | flops 603979776 | bytes 3145728 | tf_op jit(solution)/shard_map/pallas_call | solution.py:275
  42.4 2.0 %shard_map.85 = (f32[512,256]{1,0:T(8,128)S(1)}, f32[512,256]{1,0:T(8,128)S(1)}, f32[512,256]{1,0:T(8,128)S(1)}, f32[512,256]{1,0:T(8,128)S(1)}) custom-call(bf16[512,1024]{1,0:T(8,128)(2,1)S(1)} %get-tuple-element.49.q_ref.refs_0_, bf16[512,1024]{1,0:T(8,128)(2,1)S(1)} %get-tuple-element.50.k_ref.refs_1_, ...), custom_call_target="tpu_custom_call" | custom-call | flops 603979776 | bytes 3145728 | tf_op jit(solution)/shard_map/pallas_call | solution.py:275
  44.3 0.0 collective-permute-done.4.refs_22_
  44.3 0.0 collective-permute-done.5.refs_23_
  44.4 0.0 collective-permute-done.12.refs_25_
  44.4 0.0 collective-permute-done.13.refs_26_
  44.4 0.0 collective-permute-done.14.refs_27_
  44.4 3.8 %shard_map.93 = (bf16[512,1024]{1,0:T(8,128)(2,1)}, bf16[512,1024]{1,0:T(8,128)(2,1)}, bf16[512,1024]{1,0:T(8,128)(2,1)}, bf16[512,1024]{1,0:T(8,128)(2,1)}) custom-call(s32[7]{0:T(128)} %lengths_hbm.1, bf16[512,1024]{1,0:T(8,128)(2,1)S(1)} %get-tuple-element.49.q_ref.refs_0_, bf16[512,1024]{1,0:T(8,128)(2,1)S(1)} %get-tuple-element.50.k_ref.refs_1_, ...), custom_call_target="tpu_custom_call" | custom-call | flops 536870912 | bytes 16777216 | tf_op jit(solution)/shard_map/pallas_call | solution.py:287
  (2 shorter events, 0.1 us)
Async XLA Ops:
  3.5 6.9 %collective-permute-start = (f32[256,128]{1,0:T(8,128)S(1)}, f32[256,128]{1,0:T(8,128)S(1)}, u32[]{:S(2)}, u32[]{:S(2)}) collective-permute-start(f32[256,128]{1,0:T(8,128)S(1)} %get-tuple-element.70), channel_id=1, source_target_pairs={{0,8},{1,9},{2,10},{3,11},{4,12},{5,13},{6,14},{7,15},{8,0},{9,1},... | collective-permute-start | bytes 393224 | tf_op jit(solution)/shard_map/ppermute | solution.py:201
  6.5 7.8 %collective-permute-start.1 = (f32[256,128]{1,0:T(8,128)S(1)}, f32[256,128]{1,0:T(8,128)S(1)}, u32[]{:S(2)}, u32[]{:S(2)}) collective-permute-start(f32[256,128]{1,0:T(8,128)S(1)} %get-tuple-element.71), channel_id=1, source_target_pairs={{0,16},{1,17},{2,18},{3,19},{4,20},{5,21},{6,22},{7,23},{8,24},{9,... | collective-permute-start | bytes 393224 | tf_op jit(solution)/shard_map/ppermute | solution.py:201
  8.0 6.3 %collective-permute-start.2 = (f32[256,128]{1,0:T(8,128)S(1)}, f32[256,128]{1,0:T(8,128)S(1)}, u32[]{:S(2)}, u32[]{:S(2)}) collective-permute-start(f32[256,128]{1,0:T(8,128)S(1)} %get-tuple-element.72), channel_id=1, source_target_pairs={{0,24},{1,25},{2,26},{3,27},{4,28},{5,29},{6,30},{7,31},{8,16},{9,... | collective-permute-start | bytes 393224 | tf_op jit(solution)/shard_map/ppermute | solution.py:201
  14.5 3.2 %collective-permute-start.9 = (f32[256,128]{1,0:T(8,128)S(1)}, f32[256,128]{1,0:T(8,128)S(1)}, u32[]{:S(2)}, u32[]{:S(2)}) collective-permute-start(f32[256,128]{1,0:T(8,128)S(1)} %get-tuple-element.81.total_ref.answer_ref), channel_id=1, source_target_pairs={{0,1},{1,0},{3,2},{5,4},{7,6},{8,9},{9,8},{11,10},{13,12},{15,14},... | collective-permute-start | bytes 393224 | tf_op jit(solution)/shard_map/ppermute | solution.py:201
  17.7 7.0 %collective-permute-start.10 = (f32[256,128]{1,0:T(8,128)S(1)}, f32[256,128]{1,0:T(8,128)S(1)}, u32[]{:S(2)}, u32[]{:S(2)}) collective-permute-start(f32[256,128]{1,0:T(8,128)S(1)} %get-tuple-element.82.total_ref), channel_id=1, source_target_pairs={{0,2},{1,3},{2,0},{6,4},{8,10},{9,11},{10,8},{14,12},{16,18},{17,1... | collective-permute-start | bytes 393224 | tf_op jit(solution)/shard_map/ppermute | solution.py:201
  21.2 11.2 %collective-permute-start.6 = (f32[256,128]{1,0:T(8,128)S(1)}, f32[256,128]{1,0:T(8,128)S(1)}, u32[]{:S(2)}, u32[]{:S(2)}) collective-permute-start(f32[256,128]{1,0:T(8,128)S(1)} %get-tuple-element.78), channel_id=1, source_target_pairs={{0,8},{1,9},{2,10},{3,11},{4,12},{5,13},{6,14},{7,15},{8,0},{9,1},... | collective-permute-start | bytes 393224 | tf_op jit(solution)/shard_map/ppermute | solution.py:201
  22.5 10.7 %collective-permute-start.7 = (f32[256,128]{1,0:T(8,128)S(1)}, f32[256,128]{1,0:T(8,128)S(1)}, u32[]{:S(2)}, u32[]{:S(2)}) collective-permute-start(f32[256,128]{1,0:T(8,128)S(1)} %get-tuple-element.79), channel_id=1, source_target_pairs={{0,16},{1,17},{2,18},{3,19},{4,20},{5,21},{6,22},{7,23},{8,24},{9,... | collective-permute-start | bytes 393224 | tf_op jit(solution)/shard_map/ppermute | solution.py:201
  23.3 11.4 %collective-permute-start.8 = (f32[256,128]{1,0:T(8,128)S(1)}, f32[256,128]{1,0:T(8,128)S(1)}, u32[]{:S(2)}, u32[]{:S(2)}) collective-permute-start(f32[256,128]{1,0:T(8,128)S(1)} %get-tuple-element.80), channel_id=1, source_target_pairs={{0,24},{1,25},{2,26},{3,27},{4,28},{5,29},{6,30},{7,31},{8,16},{9,... | collective-permute-start | bytes 393224 | tf_op jit(solution)/shard_map/ppermute | solution.py:201
  24.8 9.9 %collective-permute-start.11 = (f32[256,128]{1,0:T(8,128)S(1)}, f32[256,128]{1,0:T(8,128)S(1)}, u32[]{:S(2)}, u32[]{:S(2)}) collective-permute-start(f32[256,128]{1,0:T(8,128)S(1)} %get-tuple-element.84.refs_4_), channel_id=1, source_target_pairs={{0,4},{1,5},{2,6},{3,7},{4,0},{8,12},{9,13},{10,14},{11,15},{12,8}... | collective-permute-start | bytes 393224 | tf_op jit(solution)/shard_map/ppermute | solution.py:201
  29.1 7.9 %collective-permute-start.3 = (f32[256,128]{1,0:T(8,128)S(1)}, f32[256,128]{1,0:T(8,128)S(1)}, u32[]{:S(2)}, u32[]{:S(2)}) collective-permute-start(f32[256,128]{1,0:T(8,128)S(1)} %get-tuple-element.74), channel_id=1, source_target_pairs={{0,8},{1,9},{2,10},{3,11},{4,12},{5,13},{6,14},{7,15},{8,0},{9,1},... | collective-permute-start | bytes 393224 | tf_op jit(solution)/shard_map/ppermute | solution.py:201
  32.4 11.9 %collective-permute-start.4 = (f32[256,128]{1,0:T(8,128)S(1)}, f32[256,128]{1,0:T(8,128)S(1)}, u32[]{:S(2)}, u32[]{:S(2)}) collective-permute-start(f32[256,128]{1,0:T(8,128)S(1)} %get-tuple-element.75), channel_id=1, source_target_pairs={{0,16},{1,17},{2,18},{3,19},{4,20},{5,21},{6,22},{7,23},{8,24},{9,... | collective-permute-start | bytes 393224 | tf_op jit(solution)/shard_map/ppermute | solution.py:201
  33.3 11.1 %collective-permute-start.5 = (f32[256,128]{1,0:T(8,128)S(1)}, f32[256,128]{1,0:T(8,128)S(1)}, u32[]{:S(2)}, u32[]{:S(2)}) collective-permute-start(f32[256,128]{1,0:T(8,128)S(1)} %get-tuple-element.76), channel_id=1, source_target_pairs={{0,24},{1,25},{2,26},{3,27},{4,28},{5,29},{6,30},{7,31},{8,16},{9,... | collective-permute-start | bytes 393224 | tf_op jit(solution)/shard_map/ppermute | solution.py:201
  34.9 9.4 %collective-permute-start.12 = (f32[256,128]{1,0:T(8,128)S(1)}, f32[256,128]{1,0:T(8,128)S(1)}, u32[]{:S(2)}, u32[]{:S(2)}) collective-permute-start(f32[256,128]{1,0:T(8,128)S(1)} %get-tuple-element.87), channel_id=1, source_target_pairs={{0,8},{1,9},{2,10},{3,11},{4,12},{5,13},{6,14},{7,15},{8,0},{9,1},... | collective-permute-start | bytes 393224 | tf_op jit(solution)/shard_map/ppermute | solution.py:201
  36.2 8.1 %collective-permute-start.13 = (f32[256,128]{1,0:T(8,128)S(1)}, f32[256,128]{1,0:T(8,128)S(1)}, u32[]{:S(2)}, u32[]{:S(2)}) collective-permute-start(f32[256,128]{1,0:T(8,128)S(1)} %get-tuple-element.88), channel_id=1, source_target_pairs={{0,16},{1,17},{2,18},{3,19},{4,20},{5,21},{6,22},{7,23},{8,24},{9,... | collective-permute-start | bytes 393224 | tf_op jit(solution)/shard_map/ppermute | solution.py:201
  37.0 7.4 %collective-permute-start.14 = (f32[256,128]{1,0:T(8,128)S(1)}, f32[256,128]{1,0:T(8,128)S(1)}, u32[]{:S(2)}, u32[]{:S(2)}) collective-permute-start(f32[256,128]{1,0:T(8,128)S(1)} %get-tuple-element.89), channel_id=1, source_target_pairs={{0,24},{1,25},{2,26},{3,27},{4,28},{5,29},{6,30},{7,31},{8,16},{9,... | collective-permute-start | bytes 393224 | tf_op jit(solution)/shard_map/ppermute | solution.py:201

commit v2 on v1

--- a/solution.py
+++ b/solution.py
@@ -101,78 +101,104 @@
                 ref[c, pl.ds(h * HEAD, HEAD)] = part
 
 
-def outer_kernel(factor, groups, n, lengths_hbm, *refs):
-    q_ref, k_ref, v_ref, g_ref = refs[:4]
+def outer_kernel(factor, groups, n, first, lengths_hbm, *refs):
+    arrays = refs[:4]
     parts = refs[4 : 4 + 4 * groups]
     refs = refs[4 + 4 * groups :]
-    share_refs, rest_refs = refs[:n], refs[n : 2 * n]
-    outs = refs[2 * n : 2 * n + 4]
-    buffers = refs[2 * n + 4 : 2 * n + 8]
-    share, rest, lengths_ref, sem, count_sem = refs[2 * n + 8 :]
+    pieces = refs[:n]
+    outs = refs[n : n + 4] if first else refs[n + 4 : n + 8]
+    buffers = refs[-6:-4]
+    state, lengths_ref, sem, count_sem = refs[-4:]
     counts = pltpu.make_async_copy(lengths_hbm, lengths_ref, count_sem)
     counts.start()
     place = lax.axis_index("seq")
     prompt = lax.axis_index("resp") == 0
-    piece = share_refs[0].shape[0]
+    piece = pieces[0].shape[0]
     for m in range(n):
         at = pl.multiple_of(jnp.bitwise_xor(place, m) * piece, piece)
-        share[pl.ds(at, piece), :] = share_refs[m][...]
-        rest[pl.ds(at, piece), :] = rest_refs[m][...]
+        state[pl.ds(at, piece), :] = pieces[m][...]
     counts.wait()
     keep = kept(lengths_ref)
     span = HEADS // groups
-    copies = []
-    for head in range(HEADS):
-        h = pl.ds(head * HEAD, HEAD)
-        within = pl.ds(head % span * HEAD, HEAD)
-        fs = jnp.where(prompt, share[h, :], rest[h, :]).astype(BF16)
-        bs = jnp.where(prompt, rest[h, :], share[h, :]).astype(BF16)
-        sides = ((q_ref, fs, NN), (g_ref, fs, NT), (v_ref, bs, NT), (k_ref, bs, NN))
-        for which, (ref, state, dims) in enumerate(sides):
-            part = parts[head // span * 4 + which][:, within]
-            total = part + factor * dot(ref[:, h], state, dims)
-            buffers[which][:, h] = jnp.where(keep, total, 0.0).astype(BF16)
-        if head % WRITE == WRITE - 1:
-            at = head // WRITE
-            wide = pl.ds(at * WRITE * HEAD, WRITE * HEAD)
-            for which in range(4):
-                copy = pltpu.make_async_copy(
-                    buffers[which].at[:, wide], outs[which].at[:, wide], sem.at[which, at]
-                )
-                copy.start()
-                copies.append(copy)
-    for copy in copies:
-        copy.wait()
-
-
-def step_kernel(step, total_ref, new_ref, answer_ref, total_out, answer_out):
+
+    def write(sides):
+        copies = []
+        for head in range(HEADS):
+            h = pl.ds(head * HEAD, HEAD)
+            within = pl.ds(head % span * HEAD, HEAD)
+            low = state[h, :].astype(BF16)
+            for buffer, (which, source, dims) in zip(buffers, sides):
+                part = parts[head // span * 4 + which][:, within]
+                total = part + factor * dot(arrays[source][:, h], low, dims)
+                buffer[:, h] = jnp.where(keep, total, 0.0).astype(BF16)
+            if head % WRITE == WRITE - 1:
+                at = head // WRITE
+                wide = pl.ds(at * WRITE * HEAD, WRITE * HEAD)
+                for i, (which, _, _) in enumerate(sides):
+                    copy = pltpu.make_async_copy(
+                        buffers[i].at[:, wide], outs[which].at[:, wide], sem.at[i, at]
+                    )
+                    copy.start()
+                    copies.append(copy)
+        for copy in copies:
+            copy.wait()
+
+    @pl.when(prompt == first)
+    def _():
+        write(((0, 0, NN), (1, 3, NT)))
+
+    @pl.when(prompt != first)
+    def _():
+        write(((2, 2, NT), (3, 1, NN)))
+
+
+def pair_kernel(mine_ref, new_ref, send_ref, sum_ref):
     row = lax.axis_index("resp")
-    gets = jnp.logical_and(row >= step, row < 2 * step)
-    total = total_ref[...]
+    mine = mine_ref[...]
     new = new_ref[...]
-    summed = jnp.where(row == 0, total, total + new)
-    total_out[...] = jnp.where(gets, new, summed)
-    answer_out[...] = answer_ref[...] + new if step > 1 else new
-
-
-def scan_kernel(n, step, *refs):
+    both = mine + new
+    send_ref[...] = jnp.where(row == 0, mine, jnp.where(row == 1, new, both))
+    sum_ref[...] = jnp.where(row == 0, new, mine)
+
+
+def level_kernel(layers, send_ref, sum_ref, *refs):
+    row = lax.axis_index("resp")
+    layer = lax.div(row, 2)
+    answer = sum_ref[...]
+    prompt = jnp.zeros_like(answer)
+    for k in range(1, layers):
+        new = refs[k - 1][...]
+        answer = answer + new
+        prompt = prompt + jnp.where(layer == k, new, 0.0)
+    total = jnp.where(layer == 0, answer, prompt)
+    send = send_ref[...]
+    own_ref, give_ref = refs[-2:]
+    own_ref[...] = jnp.where(row == 1, send, total)
+    give_ref[...] = jnp.where(row == 0, send, total)
+
+
+def scan_kernel(n, first, *refs):
     place = lax.axis_index("seq")
     row = lax.axis_index("resp")
     prompt = row == 0
-    count = n + 3 if step else n
+    count = n if first else n + 2
     came = refs[:count]
     outs = refs[count : count + n]
     order, sums = refs[-2:]
     for m in range(n):
         order[jnp.bitwise_xor(place, m)] = came[m][...]
-    if step:
-        gets = jnp.logical_and(row >= step, row < 2 * step)
-        total, new, answer = (ref[...] for ref in came[n:])
-        forward = jnp.logical_not(prompt)
-        before = jnp.where(prompt, answer + new, jnp.where(gets, new, total))
-    else:
+    core = lax.rem(row, 2)
+    half = came[-1].shape[0] if not first else refs[count + n].shape[0]
+    here = pl.ds(pl.multiple_of(core * half, half), half)
+    there = pl.ds(pl.multiple_of((1 - core) * half, half), half)
+    if first:
         forward = prompt
         before = jnp.zeros(order.shape[1:], F32)
+    else:
+        forward = jnp.logical_not(prompt)
+        sums[0, here, :] = came[n][...]
+        sums[0, there, :] = came[n + 1][...]
+        before = sums[0]
     after = before
     for s in range(n):
         sums[s] = before
@@ -182,8 +208,10 @@
         after = after + order[s]
     for m in range(n):
         outs[m][...] = sums[jnp.bitwise_xor(place, m)]
-    if not step:
-        refs[count + n][...] = before
+    if first:
+        order[0] = before
+        refs[count + n][...] = order[0, here, :]
+        refs[count + n + 1][...] = order[0, there, :]
 
 
 def per_device(n, rows, queries, keys, values, grad_out, lengths):
@@ -206,6 +234,7 @@
     counts = pltpu.SMEM(lengths.shape, jnp.int32)
     piece = HEADS * HEAD // n
     piece_shape = jax.ShapeDtypeStruct((piece, HEAD), F32)
+    half_shape = jax.ShapeDtypeStruct((piece // 2, HEAD), F32)
     small = pltpu.CompilerParams(vmem_limit_bytes=6 * 2**20)
 
     def far(x):
@@ -234,41 +263,39 @@
             )
         return came
 
-    def scan(step, *pieces):
-        outputs = n if step else n + 1
+    def scan(first, *pieces):
+        shapes = [piece_shape] * n + [half_shape] * (2 * first)
         return pl.pallas_call(
-            functools.partial(scan_kernel, n, step),
+            functools.partial(scan_kernel, n, first),
             in_specs=[whole] * len(pieces),
-            out_specs=[whole] * outputs,
-            out_shape=[piece_shape] * outputs,
+            out_specs=[whole] * len(shapes),
+            out_shape=shapes,
             scratch_shapes=[pltpu.VMEM((n, piece, HEAD), F32)] * 2,
             compiler_params=small,
         )(*pieces)
 
-    *share, total = scan(0, *swapped(pieces[:n]))
+    *share, mine, give = scan(True, *swapped(pieces[:n]))
     rest = swapped(pieces[n:])
     share = swapped(share)
-    answer = total
-    step = 1
-    while step < rows:
-        pairs = [
-            (line(s, at), line(s, at ^ step))
-            for s in range(n)
-            for at in range(rows)
-            if at < step or (at % step == 0 and at & step)
-        ]
-        new = move(total, pairs)
-        if 2 * step == rows:
-            break
-        total, answer = pl.pallas_call(
-            functools.partial(step_kernel, step),
-            in_specs=[whole] * 3,
+
+    def across(x, bits):
+        return move(x, [(line(s, r), line(s, r ^ bits)) for s in range(n) for r in range(rows)])
+
+    def combine(kernel, *inputs):
+        return pl.pallas_call(
+            kernel,
+            in_specs=[whole] * len(inputs),
             out_specs=[whole] * 2,
-            out_shape=[piece_shape] * 2,
+            out_shape=[half_shape] * 2,
             compiler_params=small,
-        )(total, new, answer)
-        step *= 2
-    rest = swapped(scan(step, *rest, total, new, answer))
+        )(*inputs)
+
+    layers = rows // 2
+    send, gathered = combine(pair_kernel, mine, across(give, 1))
+    levels = [across(send, 2 * k) for k in range(1, layers)]
+    own, give = combine(functools.partial(level_kernel, layers), send, gathered, *levels)
+    new = across(give, 1)
+    rest = swapped(scan(False, *rest, own, new))
     parts = []
     part_shape = jax.ShapeDtypeStruct((tokens, width // GROUPS), F32)
     for group in range(GROUPS):
@@ -284,23 +311,27 @@
                 transcendentals=0,
             ),
         )(q, k, v, g)
-    outs = pl.pallas_call(
-        functools.partial(outer_kernel, factor, GROUPS, n),
-        in_specs=[there] + [whole] * (4 + 4 * GROUPS + 2 * n),
-        out_specs=[there] * 4,
-        scratch_shapes=[array] * 4
-        + [stack] * 2
-        + [
-            counts,
-            pltpu.SemaphoreType.DMA((4, HEADS // WRITE)),
-            pltpu.SemaphoreType.DMA,
-        ],
-        out_shape=[jax.ShapeDtypeStruct((tokens, width), BF16)] * 4,
-        compiler_params=pltpu.CompilerParams(vmem_limit_bytes=12 * 2**20),
-        cost_estimate=pl.CostEstimate(
-            flops=8 * size * HEAD, bytes_accessed=32 * size, transcendentals=0
-        ),
-    )(far(lengths), q, k, v, g, *parts, *share, *rest)
+    outs = []
+    for first, pieces in ((True, share), (False, rest)):
+        fixed = 5 + 4 * GROUPS + n
+        outs = pl.pallas_call(
+            functools.partial(outer_kernel, factor, GROUPS, n, first),
+            in_specs=[there] + [whole] * (fixed - 1) + [there] * len(outs),
+            out_specs=[there] * 4,
+            scratch_shapes=[array] * 2
+            + [
+                stack,
+                counts,
+                pltpu.SemaphoreType.DMA((2, HEADS // WRITE)),
+                pltpu.SemaphoreType.DMA,
+            ],
+            out_shape=[jax.ShapeDtypeStruct((tokens, width), BF16)] * 4,
+            input_output_aliases={fixed + i: i for i in range(len(outs))},
+            compiler_params=pltpu.CompilerParams(vmem_limit_bytes=8 * 2**20),
+            cost_estimate=pl.CostEstimate(
+                flops=4 * size * HEAD, bytes_accessed=16 * size, transcendentals=0
+            ),
+        )(far(lengths), q, k, v, g, *parts, *pieces, *outs)
     return tuple(x.reshape(1, tokens, width) for x in outs)
 
 

time: 48.4 us -> 46.6 us (0.963)
  starting transfers between devices: 25 us -> 19.9 us
  waiting for transfers between devices: 7.58 us -> 9.22 us
  Pallas kernels: 14.8 us -> 16.3 us
    ppermute x15 -> x17, starting transfers between devices: 25 us -> 19.9 us  [move(): return lax.ppermute(x, AXES, pairs)]
    ppermute x15 -> x17, waiting for transfers between devices: 7.58 us -> 9.22 us  [move(): return lax.ppermute(x, AXES, pairs)]
    pallas_call x5 -> x6, Pallas kernels: 4.2 us -> 5.68 us  [the longest x2 5.28 us: per_device(): pl.pallas_call(functools.partial(outer_kernel, factor, GROUPS, n, first),...]
  transfers between devices with their start and end apart: 15 -> 17, of which waited for: 3 -> 4; matrix products, arithmetic and copies ran while one was open for 0% -> 0% of each run, Pallas kernels for 17% -> 23%
where the time goes in v2:
time: 46.6 us; the launch traced here: 46.4 us
  starting transfers between devices  19.9 us (43%)
  Pallas kernels  16.3 us (35%)
  waiting for transfers between devices  9.22 us (20%)
  between operations  0.94 us (2%)
    ppermute x17, starting transfers between devices, move(): return lax.ppermute(x, AXES, pairs)  19.9 us
    ppermute x17, waiting for transfers between devices, move(): return lax.ppermute(x, AXES, pairs)  9.22 us
    pallas_call x4, Pallas kernels, per_device(): pl.pallas_call(functools.partial(inner_kernel, factor, group * HEADS // G...  7.79 us
    pallas_call x2, Pallas kernels, per_device(): pl.pallas_call(functools.partial(outer_kernel, factor, GROUPS, n, first),...  5.28 us
    pallas_call x1, Pallas kernels, per_device(): pl.pallas_call(functools.partial(state_kernel, n), in_specs=[there] * 5,...  2.84 us
  transfers between devices with their start and end apart: 17, of which 4 were waited for; matrix products, arithmetic and copies ran while one was open for 0% of the time, Pallas kernels for 23%

profile of v2, /device:TPU:0, one launch (start us, length us, event | category | flops | bytes accessed | tf_op | source)
XLA Modules:
  0.0 46.4 jit_solution(10504588268673670504)
XLA Ops:
  0.6 2.8 %shard_map.84 = (f32[256,128]{1,0:T(8,128)S(1)}, f32[256,128]{1,0:T(8,128)S(1)}, f32[256,128]{1,0:T(8,128)S(1)}, f32[256,128]{1,0:T(8,128)S(1)}, f32[256,128]{1,...) custom-call(bf16[512,1024]{1,0:T(8,128)(2,1)} %bitcast.8, ...), custom_call_target="tpu_custom_call" | custom-call | flops 268435456 | bytes 4194304 | tf_op jit(solution)/shard_map/pallas_call | solution.py:243
  3.5 3.0 %collective-permute-start.3 = (f32[256,128]{1,0:T(8,128)S(1)}, f32[256,128]{1,0:T(8,128)S(1)}, u32[]{:S(2)}, u32[]{:S(2)}) collective-permute-start(f32[256,128]{1,0:T(8,128)S(1)} %get-tuple-element.79), channel_id=1, source_target_pairs={{0,8},{1,9},{2,10},{3,11},{4,12},{5,13},{6,14},{7,15},{8,0},{9,1},... | collective-permute-start | bytes 393224 | tf_op jit(solution)/shard_map/ppermute | solution.py:229
  6.5 1.5 %collective-permute-start.4 = (f32[256,128]{1,0:T(8,128)S(1)}, f32[256,128]{1,0:T(8,128)S(1)}, u32[]{:S(2)}, u32[]{:S(2)}) collective-permute-start(f32[256,128]{1,0:T(8,128)S(1)} %get-tuple-element.80), channel_id=1, source_target_pairs={{0,16},{1,17},{2,18},{3,19},{4,20},{5,21},{6,22},{7,23},{8,24},{9,... | collective-permute-start | bytes 393224 | tf_op jit(solution)/shard_map/ppermute | solution.py:229
  8.0 0.0 collective-permute-start.5
  8.0 2.3 %collective-permute-done.3.refs_1_ = f32[256,128]{1,0:T(8,128)S(1)} collective-permute-done((f32[256,128]{1,0:T(8,128)S(1)}, f32[256,128]{1,0:T(8,128)S(1)}, u32[]{:S(2)}, u32[]{:S(2)}) %collective-permute-start.3) | collective-permute-done | bytes 131104 | tf_op jit(solution)/shard_map/ppermute | solution.py:229
  10.4 3.9 %collective-permute-done.4.refs_2_ = f32[256,128]{1,0:T(8,128)S(1)} collective-permute-done((f32[256,128]{1,0:T(8,128)S(1)}, f32[256,128]{1,0:T(8,128)S(1)}, u32[]{:S(2)}, u32[]{:S(2)}) %collective-permute-start.4) | collective-permute-done | bytes 131104 | tf_op jit(solution)/shard_map/ppermute | solution.py:229
  14.3 0.0 collective-permute-done.5.refs_3_
  14.3 0.2 shard_map.89
  14.5 0.1 collective-permute-start.6
  14.5 1.2 %collective-permute-done.6.new_ref = f32[128,128]{1,0:T(8,128)S(1)} collective-permute-done((f32[128,128]{1,0:T(8,128)S(1)}, f32[128,128]{1,0:T(8,128)S(1)}, u32[]{:S(2)}, u32[]{:S(2)}) %collective-permute-start.6) | collective-permute-done | bytes 65568 | tf_op jit(solution)/shard_map/ppermute | solution.py:229
  15.8 3.7 %collective-permute-start.9 = (f32[128,128]{1,0:T(8,128)S(1)}, f32[128,128]{1,0:T(8,128)S(1)}, u32[]{:S(2)}, u32[]{:S(2)}) collective-permute-start(f32[128,128]{1,0:T(8,128)S(1)} %get-tuple-element.84.send_ref), channel_id=1, source_target_pairs={{0,6},{1,7},{2,4},{3,5},{4,2},{5,3},{6,0},{7,1},{8,14},{9,15},{10,... | collective-permute-start | bytes 196616 | tf_op jit(solution)/shard_map/ppermute | solution.py:229
  19.5 0.0 collective-permute-start.8
  19.5 1.2 %collective-permute-start = (f32[256,128]{1,0:T(8,128)S(1)}, f32[256,128]{1,0:T(8,128)S(1)}, u32[]{:S(2)}, u32[]{:S(2)}) collective-permute-start(f32[256,128]{1,0:T(8,128)S(1)} %get-tuple-element.75), channel_id=1, source_target_pairs={{0,8},{1,9},{2,10},{3,11},{4,12},{5,13},{6,14},{7,15},{8,0},{9,1},... | collective-permute-start | bytes 393224 | tf_op jit(solution)/shard_map/ppermute | solution.py:229
  20.7 0.8 %collective-permute-start.1 = (f32[256,128]{1,0:T(8,128)S(1)}, f32[256,128]{1,0:T(8,128)S(1)}, u32[]{:S(2)}, u32[]{:S(2)}) collective-permute-start(f32[256,128]{1,0:T(8,128)S(1)} %get-tuple-element.76), channel_id=1, source_target_pairs={{0,16},{1,17},{2,18},{3,19},{4,20},{5,21},{6,22},{7,23},{8,24},{9,... | collective-permute-start | bytes 393224 | tf_op jit(solution)/shard_map/ppermute | solution.py:229
  21.5 0.8 %collective-permute-start.7 = (f32[128,128]{1,0:T(8,128)S(1)}, f32[128,128]{1,0:T(8,128)S(1)}, u32[]{:S(2)}, u32[]{:S(2)}) collective-permute-start(f32[128,128]{1,0:T(8,128)S(1)} %get-tuple-element.84.send_ref), channel_id=1, source_target_pairs={{0,2},{1,3},{2,0},{3,1},{4,6},{5,7},{6,4},{7,5},{8,10},{9,11},{10,... | collective-permute-start | bytes 196616 | tf_op jit(solution)/shard_map/ppermute | solution.py:229
  22.3 0.0 collective-permute-done.9.refs_2_
  22.3 1.4 %collective-permute-start.2 = (f32[256,128]{1,0:T(8,128)S(1)}, f32[256,128]{1,0:T(8,128)S(1)}, u32[]{:S(2)}, u32[]{:S(2)}) collective-permute-start(f32[256,128]{1,0:T(8,128)S(1)} %get-tuple-element.77), channel_id=1, source_target_pairs={{0,24},{1,25},{2,26},{3,27},{4,28},{5,29},{6,30},{7,31},{8,16},{9,... | collective-permute-start | bytes 393224 | tf_op jit(solution)/shard_map/ppermute | solution.py:229
  23.7 1.7 %collective-permute-done.8.refs_1_ = f32[128,128]{1,0:T(8,128)S(1)} collective-permute-done((f32[128,128]{1,0:T(8,128)S(1)}, f32[128,128]{1,0:T(8,128)S(1)}, u32[]{:S(2)}, u32[]{:S(2)}) %collective-permute-start.8) | collective-permute-done | bytes 65568 | tf_op jit(solution)/shard_map/ppermute | solution.py:229
  25.5 1.2 %collective-permute-start.14 = (f32[256,128]{1,0:T(8,128)S(1)}, f32[256,128]{1,0:T(8,128)S(1)}, u32[]{:S(2)}, u32[]{:S(2)}) collective-permute-start(f32[256,128]{1,0:T(8,128)S(1)} %get-tuple-element.93), channel_id=1, source_target_pairs={{0,8},{1,9},{2,10},{3,11},{4,12},{5,13},{6,14},{7,15},{8,0},{9,1},... | collective-permute-start | bytes 393224 | tf_op jit(solution)/shard_map/ppermute | solution.py:229
  26.7 0.0 collective-permute-done.7.refs_0_
  26.7 0.1 collective-permute-start.10
  26.8 1.9 %shard_map.88 = (f32[512,256]{1,0:T(8,128)S(1)}, f32[512,256]{1,0:T(8,128)S(1)}, f32[512,256]{1,0:T(8,128)S(1)}, f32[512,256]{1,0:T(8,128)S(1)}) custom-call(bf16[512,1024]{1,0:T(8,128)(2,1)S(1)} %get-tuple-element.54.q_ref.refs_0_, bf16[512,1024]{1,0:T(8,128)(2,1)S(1)} %get-tuple-element.55.k_ref.refs_1_, ...), custom_call_target="tpu_custom_call" | custom-call | flops 603979776 | bytes 3145728 | tf_op jit(solution)/shard_map/pallas_call | solution.py:302
  28.8 0.0 collective-permute-done.refs_1_
  28.8 1.0 %collective-permute-start.15 = (f32[256,128]{1,0:T(8,128)S(1)}, f32[256,128]{1,0:T(8,128)S(1)}, u32[]{:S(2)}, u32[]{:S(2)}) collective-permute-start(f32[256,128]{1,0:T(8,128)S(1)} %get-tuple-element.94), channel_id=1, source_target_pairs={{0,16},{1,17},{2,18},{3,19},{4,20},{5,21},{6,22},{7,23},{8,24},{9,... | collective-permute-start | bytes 393224 | tf_op jit(solution)/shard_map/ppermute | solution.py:229
  29.7 0.0 collective-permute-done.1.refs_2_
  29.7 1.6 %collective-permute-start.16 = (f32[256,128]{1,0:T(8,128)S(1)}, f32[256,128]{1,0:T(8,128)S(1)}, u32[]{:S(2)}, u32[]{:S(2)}) collective-permute-start(f32[256,128]{1,0:T(8,128)S(1)} %get-tuple-element.95), channel_id=1, source_target_pairs={{0,24},{1,25},{2,26},{3,27},{4,28},{5,29},{6,30},{7,31},{8,16},{9,... | collective-permute-start | bytes 393224 | tf_op jit(solution)/shard_map/ppermute | solution.py:229
  31.3 1.9 %shard_map.87 = (f32[512,256]{1,0:T(8,128)S(1)}, f32[512,256]{1,0:T(8,128)S(1)}, f32[512,256]{1,0:T(8,128)S(1)}, f32[512,256]{1,0:T(8,128)S(1)}) custom-call(bf16[512,1024]{1,0:T(8,128)(2,1)S(1)} %get-tuple-element.54.q_ref.refs_0_, bf16[512,1024]{1,0:T(8,128)(2,1)S(1)} %get-tuple-element.55.k_ref.refs_1_, ...), custom_call_target="tpu_custom_call" | custom-call | flops 603979776 | bytes 3145728 | tf_op jit(solution)/shard_map/pallas_call | solution.py:302
  33.2 0.0 collective-permute-done.2.refs_3_
  33.2 0.0 collective-permute-done.10.refs_5_
  33.3 0.2 shard_map.92
  33.4 1.1 %collective-permute-start.11 = (f32[256,128]{1,0:T(8,128)S(1)}, f32[256,128]{1,0:T(8,128)S(1)}, u32[]{:S(2)}, u32[]{:S(2)}) collective-permute-start(f32[256,128]{1,0:T(8,128)S(1)} %get-tuple-element.89), channel_id=1, source_target_pairs={{0,8},{1,9},{2,10},{3,11},{4,12},{5,13},{6,14},{7,15},{8,0},{9,1},... | collective-permute-start | bytes 393224 | tf_op jit(solution)/shard_map/ppermute | solution.py:229
  34.6 0.9 %collective-permute-start.12 = (f32[256,128]{1,0:T(8,128)S(1)}, f32[256,128]{1,0:T(8,128)S(1)}, u32[]{:S(2)}, u32[]{:S(2)}) collective-permute-start(f32[256,128]{1,0:T(8,128)S(1)} %get-tuple-element.90), channel_id=1, source_target_pairs={{0,16},{1,17},{2,18},{3,19},{4,20},{5,21},{6,22},{7,23},{8,24},{9,... | collective-permute-start | bytes 393224 | tf_op jit(solution)/shard_map/ppermute | solution.py:229
  35.4 0.0 collective-permute-done.14.refs_21_
  35.5 1.5 %collective-permute-start.13 = (f32[256,128]{1,0:T(8,128)S(1)}, f32[256,128]{1,0:T(8,128)S(1)}, u32[]{:S(2)}, u32[]{:S(2)}) collective-permute-start(f32[256,128]{1,0:T(8,128)S(1)} %get-tuple-element.91), channel_id=1, source_target_pairs={{0,24},{1,25},{2,26},{3,27},{4,28},{5,29},{6,30},{7,31},{8,16},{9,... | collective-permute-start | bytes 393224 | tf_op jit(solution)/shard_map/ppermute | solution.py:229
  37.0 1.9 %shard_map.86 = (f32[512,256]{1,0:T(8,128)S(1)}, f32[512,256]{1,0:T(8,128)S(1)}, f32[512,256]{1,0:T(8,128)S(1)}, f32[512,256]{1,0:T(8,128)S(1)}) custom-call(bf16[512,1024]{1,0:T(8,128)(2,1)S(1)} %get-tuple-element.54.q_ref.refs_0_, bf16[512,1024]{1,0:T(8,128)(2,1)S(1)} %get-tuple-element.55.k_ref.refs_1_, ...), custom_call_target="tpu_custom_call" | custom-call | flops 603979776 | bytes 3145728 | tf_op jit(solution)/shard_map/pallas_call | solution.py:302
  38.9 1.9 %shard_map.85 = (f32[512,256]{1,0:T(8,128)S(1)}, f32[512,256]{1,0:T(8,128)S(1)}, f32[512,256]{1,0:T(8,128)S(1)}, f32[512,256]{1,0:T(8,128)S(1)}) custom-call(bf16[512,1024]{1,0:T(8,128)(2,1)S(1)} %get-tuple-element.54.q_ref.refs_0_, bf16[512,1024]{1,0:T(8,128)(2,1)S(1)} %get-tuple-element.55.k_ref.refs_1_, ...), custom_call_target="tpu_custom_call" | custom-call | flops 603979776 | bytes 3145728 | tf_op jit(solution)/shard_map/pallas_call | solution.py:302
  40.9 0.0 collective-permute-done.15.refs_22_
  40.9 0.0 collective-permute-done.16.refs_23_
  40.9 2.6 %shard_map.93 = (bf16[512,1024]{1,0:T(8,128)(2,1)}, bf16[512,1024]{1,0:T(8,128)(2,1)}, bf16[512,1024]{1,0:T(8,128)(2,1)}, bf16[512,1024]{1,0:T(8,128)(2,1)}) custom-call(s32[7]{0:T(128)} %lengths_hbm.3, bf16[512,1024]{1,0:T(8,128)(2,1)S(1)} %get-tuple-element.54.q_ref.refs_0_, bf16[512,1024]{1,0:T(8,128)(2,1)S(1)} %get-tuple-element.55.k_ref.refs_1_, ...), custom_call_target="tpu_custom_call" | custom-call | flops 268435456 | bytes 8388608 | tf_op jit(solution)/shard_map/pallas_call | solution.py:317
  43.6 0.0 collective-permute-done.11.refs_21_
  43.6 0.0 collective-permute-done.12.refs_22_
  43.6 0.0 collective-permute-done.13.refs_23_
  43.6 2.7 %shard_map.94 = (bf16[512,1024]{1,0:T(8,128)(2,1)}, bf16[512,1024]{1,0:T(8,128)(2,1)}, bf16[512,1024]{1,0:T(8,128)(2,1)}, bf16[512,1024]{1,0:T(8,128)(2,1)}) custom-call(s32[7]{0:T(128)} %lengths_hbm.3, bf16[512,1024]{1,0:T(8,128)(2,1)S(1)} %get-tuple-element.54.q_ref.refs_0_, ...), custom_call_target="tpu_custom_call", output_to_operand_aliasing={{0}: (25, {}), {1}: (26, {}), {2}: (27, {}), {3}: (28, {})} | custom-call | flops 268435456 | bytes 8388608 | tf_op jit(solution)/shard_map/pallas_call | solution.py:317
  (2 shorter events, 0.1 us)
Async XLA Ops:
  3.5 6.9 %collective-permute-start.3 = (f32[256,128]{1,0:T(8,128)S(1)}, f32[256,128]{1,0:T(8,128)S(1)}, u32[]{:S(2)}, u32[]{:S(2)}) collective-permute-start(f32[256,128]{1,0:T(8,128)S(1)} %get-tuple-element.79), channel_id=1, source_target_pairs={{0,8},{1,9},{2,10},{3,11},{4,12},{5,13},{6,14},{7,15},{8,0},{9,1},... | collective-permute-start | bytes 393224 | tf_op jit(solution)/shard_map/ppermute | solution.py:229
  6.5 7.8 %collective-permute-start.4 = (f32[256,128]{1,0:T(8,128)S(1)}, f32[256,128]{1,0:T(8,128)S(1)}, u32[]{:S(2)}, u32[]{:S(2)}) collective-permute-start(f32[256,128]{1,0:T(8,128)S(1)} %get-tuple-element.80), channel_id=1, source_target_pairs={{0,16},{1,17},{2,18},{3,19},{4,20},{5,21},{6,22},{7,23},{8,24},{9,... | collective-permute-start | bytes 393224 | tf_op jit(solution)/shard_map/ppermute | solution.py:229
  8.0 6.2 %collective-permute-start.5 = (f32[256,128]{1,0:T(8,128)S(1)}, f32[256,128]{1,0:T(8,128)S(1)}, u32[]{:S(2)}, u32[]{:S(2)}) collective-permute-start(f32[256,128]{1,0:T(8,128)S(1)} %get-tuple-element.81), channel_id=1, source_target_pairs={{0,24},{1,25},{2,26},{3,27},{4,28},{5,29},{6,30},{7,31},{8,16},{9,... | collective-permute-start | bytes 393224 | tf_op jit(solution)/shard_map/ppermute | solution.py:229
  14.5 1.3 %collective-permute-start.6 = (f32[128,128]{1,0:T(8,128)S(1)}, f32[128,128]{1,0:T(8,128)S(1)}, u32[]{:S(2)}, u32[]{:S(2)}) collective-permute-start(f32[128,128]{1,0:T(8,128)S(1)} %get-tuple-element.83), channel_id=1, source_target_pairs={{0,1},{1,0},{2,3},{3,2},{4,5},{5,4},{6,7},{7,6},{8,9},{9,8},{10,11... | collective-permute-start | bytes 196616 | tf_op jit(solution)/shard_map/ppermute | solution.py:229
  15.8 6.5 %collective-permute-start.9 = (f32[128,128]{1,0:T(8,128)S(1)}, f32[128,128]{1,0:T(8,128)S(1)}, u32[]{:S(2)}, u32[]{:S(2)}) collective-permute-start(f32[128,128]{1,0:T(8,128)S(1)} %get-tuple-element.84.send_ref), channel_id=1, source_target_pairs={{0,6},{1,7},{2,4},{3,5},{4,2},{5,3},{6,0},{7,1},{8,14},{9,15},{10,... | collective-permute-start | bytes 196616 | tf_op jit(solution)/shard_map/ppermute | solution.py:229
  19.5 6.0 %collective-permute-start.8 = (f32[128,128]{1,0:T(8,128)S(1)}, f32[128,128]{1,0:T(8,128)S(1)}, u32[]{:S(2)}, u32[]{:S(2)}) collective-permute-start(f32[128,128]{1,0:T(8,128)S(1)} %get-tuple-element.84.send_ref), channel_id=1, source_target_pairs={{0,4},{1,5},{2,6},{3,7},{4,0},{5,1},{6,2},{7,3},{8,12},{9,13},{10,... | collective-permute-start | bytes 196616 | tf_op jit(solution)/shard_map/ppermute | solution.py:229
  19.5 9.3 %collective-permute-start = (f32[256,128]{1,0:T(8,128)S(1)}, f32[256,128]{1,0:T(8,128)S(1)}, u32[]{:S(2)}, u32[]{:S(2)}) collective-permute-start(f32[256,128]{1,0:T(8,128)S(1)} %get-tuple-element.75), channel_id=1, source_target_pairs={{0,8},{1,9},{2,10},{3,11},{4,12},{5,13},{6,14},{7,15},{8,0},{9,1},... | collective-permute-start | bytes 393224 | tf_op jit(solution)/shard_map/ppermute | solution.py:229
  20.7 9.0 %collective-permute-start.1 = (f32[256,128]{1,0:T(8,128)S(1)}, f32[256,128]{1,0:T(8,128)S(1)}, u32[]{:S(2)}, u32[]{:S(2)}) collective-permute-start(f32[256,128]{1,0:T(8,128)S(1)} %get-tuple-element.76), channel_id=1, source_target_pairs={{0,16},{1,17},{2,18},{3,19},{4,20},{5,21},{6,22},{7,23},{8,24},{9,... | collective-permute-start | bytes 393224 | tf_op jit(solution)/shard_map/ppermute | solution.py:229
  21.5 5.2 %collective-permute-start.7 = (f32[128,128]{1,0:T(8,128)S(1)}, f32[128,128]{1,0:T(8,128)S(1)}, u32[]{:S(2)}, u32[]{:S(2)}) collective-permute-start(f32[128,128]{1,0:T(8,128)S(1)} %get-tuple-element.84.send_ref), channel_id=1, source_target_pairs={{0,2},{1,3},{2,0},{3,1},{4,6},{5,7},{6,4},{7,5},{8,10},{9,11},{10,... | collective-permute-start | bytes 196616 | tf_op jit(solution)/shard_map/ppermute | solution.py:229
  22.3 10.9 %collective-permute-start.2 = (f32[256,128]{1,0:T(8,128)S(1)}, f32[256,128]{1,0:T(8,128)S(1)}, u32[]{:S(2)}, u32[]{:S(2)}) collective-permute-start(f32[256,128]{1,0:T(8,128)S(1)} %get-tuple-element.77), channel_id=1, source_target_pairs={{0,24},{1,25},{2,26},{3,27},{4,28},{5,29},{6,30},{7,31},{8,16},{9,... | collective-permute-start | bytes 393224 | tf_op jit(solution)/shard_map/ppermute | solution.py:229
  25.5 10.0 %collective-permute-start.14 = (f32[256,128]{1,0:T(8,128)S(1)}, f32[256,128]{1,0:T(8,128)S(1)}, u32[]{:S(2)}, u32[]{:S(2)}) collective-permute-start(f32[256,128]{1,0:T(8,128)S(1)} %get-tuple-element.93), channel_id=1, source_target_pairs={{0,8},{1,9},{2,10},{3,11},{4,12},{5,13},{6,14},{7,15},{8,0},{9,1},... | collective-permute-start | bytes 393224 | tf_op jit(solution)/shard_map/ppermute | solution.py:229
  26.7 6.5 %collective-permute-start.10 = (f32[128,128]{1,0:T(8,128)S(1)}, f32[128,128]{1,0:T(8,128)S(1)}, u32[]{:S(2)}, u32[]{:S(2)}) collective-permute-start(f32[128,128]{1,0:T(8,128)S(1)} %get-tuple-element.87), channel_id=1, source_target_pairs={{0,1},{1,0},{2,3},{3,2},{4,5},{5,4},{6,7},{7,6},{8,9},{9,8},{10,11... | collective-permute-start | bytes 196616 | tf_op jit(solution)/shard_map/ppermute | solution.py:229
  28.8 12.1 %collective-permute-start.15 = (f32[256,128]{1,0:T(8,128)S(1)}, f32[256,128]{1,0:T(8,128)S(1)}, u32[]{:S(2)}, u32[]{:S(2)}) collective-permute-start(f32[256,128]{1,0:T(8,128)S(1)} %get-tuple-element.94), channel_id=1, source_target_pairs={{0,16},{1,17},{2,18},{3,19},{4,20},{5,21},{6,22},{7,23},{8,24},{9,... | collective-permute-start | bytes 393224 | tf_op jit(solution)/shard_map/ppermute | solution.py:229
  29.7 11.2 %collective-permute-start.16 = (f32[256,128]{1,0:T(8,128)S(1)}, f32[256,128]{1,0:T(8,128)S(1)}, u32[]{:S(2)}, u32[]{:S(2)}) collective-permute-start(f32[256,128]{1,0:T(8,128)S(1)} %get-tuple-element.95), channel_id=1, source_target_pairs={{0,24},{1,25},{2,26},{3,27},{4,28},{5,29},{6,30},{7,31},{8,16},{9,... | collective-permute-start | bytes 393224 | tf_op jit(solution)/shard_map/ppermute | solution.py:229
  33.4 10.1 %collective-permute-start.11 = (f32[256,128]{1,0:T(8,128)S(1)}, f32[256,128]{1,0:T(8,128)S(1)}, u32[]{:S(2)}, u32[]{:S(2)}) collective-permute-start(f32[256,128]{1,0:T(8,128)S(1)} %get-tuple-element.89), channel_id=1, source_target_pairs={{0,8},{1,9},{2,10},{3,11},{4,12},{5,13},{6,14},{7,15},{8,0},{9,1},... | collective-permute-start | bytes 393224 | tf_op jit(solution)/shard_map/ppermute | solution.py:229
  34.6 9.0 %collective-permute-start.12 = (f32[256,128]{1,0:T(8,128)S(1)}, f32[256,128]{1,0:T(8,128)S(1)}, u32[]{:S(2)}, u32[]{:S(2)}) collective-permute-start(f32[256,128]{1,0:T(8,128)S(1)} %get-tuple-element.90), channel_id=1, source_target_pairs={{0,16},{1,17},{2,18},{3,19},{4,20},{5,21},{6,22},{7,23},{8,24},{9,... | collective-permute-start | bytes 393224 | tf_op jit(solution)/shard_map/ppermute | solution.py:229
  35.5 8.1 %collective-permute-start.13 = (f32[256,128]{1,0:T(8,128)S(1)}, f32[256,128]{1,0:T(8,128)S(1)}, u32[]{:S(2)}, u32[]{:S(2)}) collective-permute-start(f32[256,128]{1,0:T(8,128)S(1)} %get-tuple-element.91), channel_id=1, source_target_pairs={{0,24},{1,25},{2,26},{3,27},{4,28},{5,29},{6,30},{7,31},{8,16},{9,... | collective-permute-start | bytes 393224 | tf_op jit(solution)/shard_map/ppermute | solution.py:229

commit v3 on v2

--- a/solution.py
+++ b/solution.py
@@ -14,7 +14,7 @@
 TILE = 256
 GROUPS = 4
 STATE_VMEM = 12
-WRITE = 4
+WRITE = 2
 F32 = jnp.float32
 BF16 = jnp.bfloat16
 AXES = ("seq", "resp")
@@ -292,7 +292,15 @@
 
     layers = rows // 2
     send, gathered = combine(pair_kernel, mine, across(give, 1))
-    levels = [across(send, 2 * k) for k in range(1, layers)]
+    levels = []
+    for z in range(1, layers):
+        meets = {0: z, z: 0}
+        pairs = [
+            (line(s, r), line(s, 2 * meets[r // 2] + r % 2 if r // 2 in meets else r ^ 1))
+            for s in range(n)
+            for r in range(rows)
+        ]
+        levels.append(move(send, pairs))
     own, give = combine(functools.partial(level_kernel, layers), send, gathered, *levels)
     new = across(give, 1)
     rest = swapped(scan(False, *rest, own, new))

time: 46.6 us -> 45.9 us (0.985)
  transfers between devices with their start and end apart: 17 -> 17, of which waited for: 4 -> 5; matrix products, arithmetic and copies ran while one was open for 0% -> 0% of each run, Pallas kernels for 23% -> 23%
where the time goes in v3:
time: 45.9 us; the launch traced here: 45.7 us
  starting transfers between devices  19.6 us (43%)
  Pallas kernels  16 us (35%)
  waiting for transfers between devices  9.15 us (20%)
  between operations  0.94 us (2%)
    ppermute x17, starting transfers between devices, move(): return lax.ppermute(x, AXES, pairs)  19.6 us
    ppermute x17, waiting for transfers between devices, move(): return lax.ppermute(x, AXES, pairs)  9.15 us
    pallas_call x4, Pallas kernels, per_device(): pl.pallas_call(functools.partial(inner_kernel, factor, group * HEADS // G...  7.8 us
    pallas_call x2, Pallas kernels, per_device(): pl.pallas_call(functools.partial(outer_kernel, factor, GROUPS, n, first),...  5.01 us
    pallas_call x1, Pallas kernels, per_device(): pl.pallas_call(functools.partial(state_kernel, n), in_specs=[there] * 5,...  2.84 us
  transfers between devices with their start and end apart: 17, of which 5 were waited for; matrix products, arithmetic and copies ran while one was open for 0% of the time, Pallas kernels for 23%

profile of v3, /device:TPU:0, one launch (start us, length us, event | category | flops | bytes accessed | tf_op | source)
XLA Modules:
  0.0 45.7 jit_solution(581789485974246307)
XLA Ops:
  0.6 2.8 %shard_map.84 = (f32[256,128]{1,0:T(8,128)S(1)}, f32[256,128]{1,0:T(8,128)S(1)}, f32[256,128]{1,0:T(8,128)S(1)}, f32[256,128]{1,0:T(8,128)S(1)}, f32[256,128]{1,...) custom-call(bf16[512,1024]{1,0:T(8,128)(2,1)} %bitcast.8, ...), custom_call_target="tpu_custom_call" | custom-call | flops 268435456 | bytes 4194304 | tf_op jit(solution)/shard_map/pallas_call | solution.py:243
  3.5 3.0 %collective-permute-start.3 = (f32[256,128]{1,0:T(8,128)S(1)}, f32[256,128]{1,0:T(8,128)S(1)}, u32[]{:S(2)}, u32[]{:S(2)}) collective-permute-start(f32[256,128]{1,0:T(8,128)S(1)} %get-tuple-element.79), channel_id=1, source_target_pairs={{0,8},{1,9},{2,10},{3,11},{4,12},{5,13},{6,14},{7,15},{8,0},{9,1},... | collective-permute-start | bytes 393224 | tf_op jit(solution)/shard_map/ppermute | solution.py:229
  6.5 1.5 %collective-permute-start.4 = (f32[256,128]{1,0:T(8,128)S(1)}, f32[256,128]{1,0:T(8,128)S(1)}, u32[]{:S(2)}, u32[]{:S(2)}) collective-permute-start(f32[256,128]{1,0:T(8,128)S(1)} %get-tuple-element.80), channel_id=1, source_target_pairs={{0,16},{1,17},{2,18},{3,19},{4,20},{5,21},{6,22},{7,23},{8,24},{9,... | collective-permute-start | bytes 393224 | tf_op jit(solution)/shard_map/ppermute | solution.py:229
  8.0 0.0 collective-permute-start.5
  8.0 2.3 %collective-permute-done.3.refs_1_ = f32[256,128]{1,0:T(8,128)S(1)} collective-permute-done((f32[256,128]{1,0:T(8,128)S(1)}, f32[256,128]{1,0:T(8,128)S(1)}, u32[]{:S(2)}, u32[]{:S(2)}) %collective-permute-start.3) | collective-permute-done | bytes 131104 | tf_op jit(solution)/shard_map/ppermute | solution.py:229
  10.4 3.9 %collective-permute-done.4.refs_2_ = f32[256,128]{1,0:T(8,128)S(1)} collective-permute-done((f32[256,128]{1,0:T(8,128)S(1)}, f32[256,128]{1,0:T(8,128)S(1)}, u32[]{:S(2)}, u32[]{:S(2)}) %collective-permute-start.4) | collective-permute-done | bytes 131104 | tf_op jit(solution)/shard_map/ppermute | solution.py:229
  14.3 0.0 collective-permute-done.5.refs_3_
  14.3 0.2 shard_map.89
  14.5 0.1 collective-permute-start.6
  14.5 1.2 %collective-permute-done.6.new_ref = f32[128,128]{1,0:T(8,128)S(1)} collective-permute-done((f32[128,128]{1,0:T(8,128)S(1)}, f32[128,128]{1,0:T(8,128)S(1)}, u32[]{:S(2)}, u32[]{:S(2)}) %collective-permute-start.6) | collective-permute-done | bytes 65568 | tf_op jit(solution)/shard_map/ppermute | solution.py:229
  15.8 3.7 %collective-permute-start.9 = (f32[128,128]{1,0:T(8,128)S(1)}, f32[128,128]{1,0:T(8,128)S(1)}, u32[]{:S(2)}, u32[]{:S(2)}) collective-permute-start(f32[128,128]{1,0:T(8,128)S(1)} %get-tuple-element.84.send_ref), channel_id=1, source_target_pairs={{0,6},{1,7},{2,3},{3,2},{4,5},{5,4},{6,0},{7,1},{8,14},{9,15},{10,... | collective-permute-start | bytes 196616 | tf_op jit(solution)/shard_map/ppermute | solution.py:229
  19.5 0.0 collective-permute-start.8
  19.5 1.2 %collective-permute-start = (f32[256,128]{1,0:T(8,128)S(1)}, f32[256,128]{1,0:T(8,128)S(1)}, u32[]{:S(2)}, u32[]{:S(2)}) collective-permute-start(f32[256,128]{1,0:T(8,128)S(1)} %get-tuple-element.75), channel_id=1, source_target_pairs={{0,8},{1,9},{2,10},{3,11},{4,12},{5,13},{6,14},{7,15},{8,0},{9,1},... | collective-permute-start | bytes 393224 | tf_op jit(solution)/shard_map/ppermute | solution.py:229
  20.7 0.8 %collective-permute-start.1 = (f32[256,128]{1,0:T(8,128)S(1)}, f32[256,128]{1,0:T(8,128)S(1)}, u32[]{:S(2)}, u32[]{:S(2)}) collective-permute-start(f32[256,128]{1,0:T(8,128)S(1)} %get-tuple-element.76), channel_id=1, source_target_pairs={{0,16},{1,17},{2,18},{3,19},{4,20},{5,21},{6,22},{7,23},{8,24},{9,... | collective-permute-start | bytes 393224 | tf_op jit(solution)/shard_map/ppermute | solution.py:229
  21.5 0.0 collective-permute-start.7
  21.5 0.4 collective-permute-done.9.refs_2_
  22.0 1.5 %collective-permute-start.2 = (f32[256,128]{1,0:T(8,128)S(1)}, f32[256,128]{1,0:T(8,128)S(1)}, u32[]{:S(2)}, u32[]{:S(2)}) collective-permute-start(f32[256,128]{1,0:T(8,128)S(1)} %get-tuple-element.77), channel_id=1, source_target_pairs={{0,24},{1,25},{2,26},{3,27},{4,28},{5,29},{6,30},{7,31},{8,16},{9,... | collective-permute-start | bytes 393224 | tf_op jit(solution)/shard_map/ppermute | solution.py:229
  23.4 1.2 %collective-permute-done.8.refs_1_ = f32[128,128]{1,0:T(8,128)S(1)} collective-permute-done((f32[128,128]{1,0:T(8,128)S(1)}, f32[128,128]{1,0:T(8,128)S(1)}, u32[]{:S(2)}, u32[]{:S(2)}) %collective-permute-start.8) | collective-permute-done | bytes 65568 | tf_op jit(solution)/shard_map/ppermute | solution.py:229
  24.6 1.3 %collective-permute-start.14 = (f32[256,128]{1,0:T(8,128)S(1)}, f32[256,128]{1,0:T(8,128)S(1)}, u32[]{:S(2)}, u32[]{:S(2)}) collective-permute-start(f32[256,128]{1,0:T(8,128)S(1)} %get-tuple-element.93), channel_id=1, source_target_pairs={{0,8},{1,9},{2,10},{3,11},{4,12},{5,13},{6,14},{7,15},{8,0},{9,1},... | collective-permute-start | bytes 393224 | tf_op jit(solution)/shard_map/ppermute | solution.py:229
  26.0 0.0 collective-permute-done.7.refs_0_
  26.0 0.1 collective-permute-start.10
  26.1 2.0 %shard_map.88 = (f32[512,256]{1,0:T(8,128)S(1)}, f32[512,256]{1,0:T(8,128)S(1)}, f32[512,256]{1,0:T(8,128)S(1)}, f32[512,256]{1,0:T(8,128)S(1)}) custom-call(bf16[512,1024]{1,0:T(8,128)(2,1)S(1)} %get-tuple-element.54.q_ref.refs_0_, bf16[512,1024]{1,0:T(8,128)(2,1)S(1)} %get-tuple-element.55.k_ref.refs_1_, ...), custom_call_target="tpu_custom_call" | custom-call | flops 603979776 | bytes 3145728 | tf_op jit(solution)/shard_map/pallas_call | solution.py:310
  28.1 0.0 collective-permute-done.refs_1_
  28.1 1.2 %collective-permute-start.15 = (f32[256,128]{1,0:T(8,128)S(1)}, f32[256,128]{1,0:T(8,128)S(1)}, u32[]{:S(2)}, u32[]{:S(2)}) collective-permute-start(f32[256,128]{1,0:T(8,128)S(1)} %get-tuple-element.94), channel_id=1, source_target_pairs={{0,16},{1,17},{2,18},{3,19},{4,20},{5,21},{6,22},{7,23},{8,24},{9,... | collective-permute-start | bytes 393224 | tf_op jit(solution)/shard_map/ppermute | solution.py:229
  29.3 0.0 collective-permute-done.1.refs_2_
  29.3 1.6 %collective-permute-start.16 = (f32[256,128]{1,0:T(8,128)S(1)}, f32[256,128]{1,0:T(8,128)S(1)}, u32[]{:S(2)}, u32[]{:S(2)}) collective-permute-start(f32[256,128]{1,0:T(8,128)S(1)} %get-tuple-element.95), channel_id=1, source_target_pairs={{0,24},{1,25},{2,26},{3,27},{4,28},{5,29},{6,30},{7,31},{8,16},{9,... | collective-permute-start | bytes 393224 | tf_op jit(solution)/shard_map/ppermute | solution.py:229
  30.9 1.9 %shard_map.87 = (f32[512,256]{1,0:T(8,128)S(1)}, f32[512,256]{1,0:T(8,128)S(1)}, f32[512,256]{1,0:T(8,128)S(1)}, f32[512,256]{1,0:T(8,128)S(1)}) custom-call(bf16[512,1024]{1,0:T(8,128)(2,1)S(1)} %get-tuple-element.54.q_ref.refs_0_, bf16[512,1024]{1,0:T(8,128)(2,1)S(1)} %get-tuple-element.55.k_ref.refs_1_, ...), custom_call_target="tpu_custom_call" | custom-call | flops 603979776 | bytes 3145728 | tf_op jit(solution)/shard_map/pallas_call | solution.py:310
  32.9 0.0 collective-permute-done.2.refs_3_
  32.9 0.0 collective-permute-done.10.refs_5_
  32.9 0.2 shard_map.92
  33.1 0.8 %collective-permute-start.11 = (f32[256,128]{1,0:T(8,128)S(1)}, f32[256,128]{1,0:T(8,128)S(1)}, u32[]{:S(2)}, u32[]{:S(2)}) collective-permute-start(f32[256,128]{1,0:T(8,128)S(1)} %get-tuple-element.89), channel_id=1, source_target_pairs={{0,8},{1,9},{2,10},{3,11},{4,12},{5,13},{6,14},{7,15},{8,0},{9,1},... | collective-permute-start | bytes 393224 | tf_op jit(solution)/shard_map/ppermute | solution.py:229
  33.9 1.2 %collective-permute-start.12 = (f32[256,128]{1,0:T(8,128)S(1)}, f32[256,128]{1,0:T(8,128)S(1)}, u32[]{:S(2)}, u32[]{:S(2)}) collective-permute-start(f32[256,128]{1,0:T(8,128)S(1)} %get-tuple-element.90), channel_id=1, source_target_pairs={{0,16},{1,17},{2,18},{3,19},{4,20},{5,21},{6,22},{7,23},{8,24},{9,... | collective-permute-start | bytes 393224 | tf_op jit(solution)/shard_map/ppermute | solution.py:229
  35.0 0.0 collective-permute-done.14.refs_21_
  35.0 1.6 %collective-permute-start.13 = (f32[256,128]{1,0:T(8,128)S(1)}, f32[256,128]{1,0:T(8,128)S(1)}, u32[]{:S(2)}, u32[]{:S(2)}) collective-permute-start(f32[256,128]{1,0:T(8,128)S(1)} %get-tuple-element.91), channel_id=1, source_target_pairs={{0,24},{1,25},{2,26},{3,27},{4,28},{5,29},{6,30},{7,31},{8,16},{9,... | collective-permute-start | bytes 393224 | tf_op jit(solution)/shard_map/ppermute | solution.py:229
  36.6 1.9 %shard_map.86 = (f32[512,256]{1,0:T(8,128)S(1)}, f32[512,256]{1,0:T(8,128)S(1)}, f32[512,256]{1,0:T(8,128)S(1)}, f32[512,256]{1,0:T(8,128)S(1)}) custom-call(bf16[512,1024]{1,0:T(8,128)(2,1)S(1)} %get-tuple-element.54.q_ref.refs_0_, bf16[512,1024]{1,0:T(8,128)(2,1)S(1)} %get-tuple-element.55.k_ref.refs_1_, ...), custom_call_target="tpu_custom_call" | custom-call | flops 603979776 | bytes 3145728 | tf_op jit(solution)/shard_map/pallas_call | solution.py:310
  38.6 1.9 %shard_map.85 = (f32[512,256]{1,0:T(8,128)S(1)}, f32[512,256]{1,0:T(8,128)S(1)}, f32[512,256]{1,0:T(8,128)S(1)}, f32[512,256]{1,0:T(8,128)S(1)}) custom-call(bf16[512,1024]{1,0:T(8,128)(2,1)S(1)} %get-tuple-element.54.q_ref.refs_0_, bf16[512,1024]{1,0:T(8,128)(2,1)S(1)} %get-tuple-element.55.k_ref.refs_1_, ...), custom_call_target="tpu_custom_call" | custom-call | flops 603979776 | bytes 3145728 | tf_op jit(solution)/shard_map/pallas_call | solution.py:310
  40.5 0.0 collective-permute-done.15.refs_22_
  40.5 0.0 collective-permute-done.16.refs_23_
  40.5 2.5 %shard_map.93 = (bf16[512,1024]{1,0:T(8,128)(2,1)}, bf16[512,1024]{1,0:T(8,128)(2,1)}, bf16[512,1024]{1,0:T(8,128)(2,1)}, bf16[512,1024]{1,0:T(8,128)(2,1)}) custom-call(s32[7]{0:T(128)} %lengths_hbm.3, bf16[512,1024]{1,0:T(8,128)(2,1)S(1)} %get-tuple-element.54.q_ref.refs_0_, bf16[512,1024]{1,0:T(8,128)(2,1)S(1)} %get-tuple-element.55.k_ref.refs_1_, ...), custom_call_target="tpu_custom_call" | custom-call | flops 268435456 | bytes 8388608 | tf_op jit(solution)/shard_map/pallas_call | solution.py:325
  43.0 0.0 collective-permute-done.11.refs_21_
  43.0 0.0 collective-permute-done.12.refs_22_
  43.1 0.0 collective-permute-done.13.refs_23_
  43.1 2.5 %shard_map.94 = (bf16[512,1024]{1,0:T(8,128)(2,1)}, bf16[512,1024]{1,0:T(8,128)(2,1)}, bf16[512,1024]{1,0:T(8,128)(2,1)}, bf16[512,1024]{1,0:T(8,128)(2,1)}) custom-call(s32[7]{0:T(128)} %lengths_hbm.3, bf16[512,1024]{1,0:T(8,128)(2,1)S(1)} %get-tuple-element.54.q_ref.refs_0_, ...), custom_call_target="tpu_custom_call", output_to_operand_aliasing={{0}: (25, {}), {1}: (26, {}), {2}: (27, {}), {3}: (28, {})} | custom-call | flops 268435456 | bytes 8388608 | tf_op jit(solution)/shard_map/pallas_call | solution.py:325
  (2 shorter events, 0.1 us)
Async XLA Ops:
  3.5 6.9 %collective-permute-start.3 = (f32[256,128]{1,0:T(8,128)S(1)}, f32[256,128]{1,0:T(8,128)S(1)}, u32[]{:S(2)}, u32[]{:S(2)}) collective-permute-start(f32[256,128]{1,0:T(8,128)S(1)} %get-tuple-element.79), channel_id=1, source_target_pairs={{0,8},{1,9},{2,10},{3,11},{4,12},{5,13},{6,14},{7,15},{8,0},{9,1},... | collective-permute-start | bytes 393224 | tf_op jit(solution)/shard_map/ppermute | solution.py:229
  6.5 7.8 %collective-permute-start.4 = (f32[256,128]{1,0:T(8,128)S(1)}, f32[256,128]{1,0:T(8,128)S(1)}, u32[]{:S(2)}, u32[]{:S(2)}) collective-permute-start(f32[256,128]{1,0:T(8,128)S(1)} %get-tuple-element.80), channel_id=1, source_target_pairs={{0,16},{1,17},{2,18},{3,19},{4,20},{5,21},{6,22},{7,23},{8,24},{9,... | collective-permute-start | bytes 393224 | tf_op jit(solution)/shard_map/ppermute | solution.py:229
  8.0 6.2 %collective-permute-start.5 = (f32[256,128]{1,0:T(8,128)S(1)}, f32[256,128]{1,0:T(8,128)S(1)}, u32[]{:S(2)}, u32[]{:S(2)}) collective-permute-start(f32[256,128]{1,0:T(8,128)S(1)} %get-tuple-element.81), channel_id=1, source_target_pairs={{0,24},{1,25},{2,26},{3,27},{4,28},{5,29},{6,30},{7,31},{8,16},{9,... | collective-permute-start | bytes 393224 | tf_op jit(solution)/shard_map/ppermute | solution.py:229
  14.5 1.3 %collective-permute-start.6 = (f32[128,128]{1,0:T(8,128)S(1)}, f32[128,128]{1,0:T(8,128)S(1)}, u32[]{:S(2)}, u32[]{:S(2)}) collective-permute-start(f32[128,128]{1,0:T(8,128)S(1)} %get-tuple-element.83), channel_id=1, source_target_pairs={{0,1},{1,0},{2,3},{3,2},{4,5},{5,4},{6,7},{7,6},{8,9},{9,8},{10,11... | collective-permute-start | bytes 196616 | tf_op jit(solution)/shard_map/ppermute | solution.py:229
  15.8 6.2 %collective-permute-start.9 = (f32[128,128]{1,0:T(8,128)S(1)}, f32[128,128]{1,0:T(8,128)S(1)}, u32[]{:S(2)}, u32[]{:S(2)}) collective-permute-start(f32[128,128]{1,0:T(8,128)S(1)} %get-tuple-element.84.send_ref), channel_id=1, source_target_pairs={{0,6},{1,7},{2,3},{3,2},{4,5},{5,4},{6,0},{7,1},{8,14},{9,15},{10,... | collective-permute-start | bytes 196616 | tf_op jit(solution)/shard_map/ppermute | solution.py:229
  19.5 5.2 %collective-permute-start.8 = (f32[128,128]{1,0:T(8,128)S(1)}, f32[128,128]{1,0:T(8,128)S(1)}, u32[]{:S(2)}, u32[]{:S(2)}) collective-permute-start(f32[128,128]{1,0:T(8,128)S(1)} %get-tuple-element.84.send_ref), channel_id=1, source_target_pairs={{0,4},{1,5},{2,3},{3,2},{4,0},{5,1},{6,7},{7,6},{8,12},{9,13},{10,... | collective-permute-start | bytes 196616 | tf_op jit(solution)/shard_map/ppermute | solution.py:229
  19.5 8.6 %collective-permute-start = (f32[256,128]{1,0:T(8,128)S(1)}, f32[256,128]{1,0:T(8,128)S(1)}, u32[]{:S(2)}, u32[]{:S(2)}) collective-permute-start(f32[256,128]{1,0:T(8,128)S(1)} %get-tuple-element.75), channel_id=1, source_target_pairs={{0,8},{1,9},{2,10},{3,11},{4,12},{5,13},{6,14},{7,15},{8,0},{9,1},... | collective-permute-start | bytes 393224 | tf_op jit(solution)/shard_map/ppermute | solution.py:229
  20.7 8.6 %collective-permute-start.1 = (f32[256,128]{1,0:T(8,128)S(1)}, f32[256,128]{1,0:T(8,128)S(1)}, u32[]{:S(2)}, u32[]{:S(2)}) collective-permute-start(f32[256,128]{1,0:T(8,128)S(1)} %get-tuple-element.76), channel_id=1, source_target_pairs={{0,16},{1,17},{2,18},{3,19},{4,20},{5,21},{6,22},{7,23},{8,24},{9,... | collective-permute-start | bytes 393224 | tf_op jit(solution)/shard_map/ppermute | solution.py:229
  21.5 4.5 %collective-permute-start.7 = (f32[128,128]{1,0:T(8,128)S(1)}, f32[128,128]{1,0:T(8,128)S(1)}, u32[]{:S(2)}, u32[]{:S(2)}) collective-permute-start(f32[128,128]{1,0:T(8,128)S(1)} %get-tuple-element.84.send_ref), channel_id=1, source_target_pairs={{0,2},{1,3},{2,0},{3,1},{4,5},{5,4},{6,7},{7,6},{8,10},{9,11},{10,... | collective-permute-start | bytes 196616 | tf_op jit(solution)/shard_map/ppermute | solution.py:229
  22.0 10.9 %collective-permute-start.2 = (f32[256,128]{1,0:T(8,128)S(1)}, f32[256,128]{1,0:T(8,128)S(1)}, u32[]{:S(2)}, u32[]{:S(2)}) collective-permute-start(f32[256,128]{1,0:T(8,128)S(1)} %get-tuple-element.77), channel_id=1, source_target_pairs={{0,24},{1,25},{2,26},{3,27},{4,28},{5,29},{6,30},{7,31},{8,16},{9,... | collective-permute-start | bytes 393224 | tf_op jit(solution)/shard_map/ppermute | solution.py:229
  24.6 10.4 %collective-permute-start.14 = (f32[256,128]{1,0:T(8,128)S(1)}, f32[256,128]{1,0:T(8,128)S(1)}, u32[]{:S(2)}, u32[]{:S(2)}) collective-permute-start(f32[256,128]{1,0:T(8,128)S(1)} %get-tuple-element.93), channel_id=1, source_target_pairs={{0,8},{1,9},{2,10},{3,11},{4,12},{5,13},{6,14},{7,15},{8,0},{9,1},... | collective-permute-start | bytes 393224 | tf_op jit(solution)/shard_map/ppermute | solution.py:229
  26.0 6.9 %collective-permute-start.10 = (f32[128,128]{1,0:T(8,128)S(1)}, f32[128,128]{1,0:T(8,128)S(1)}, u32[]{:S(2)}, u32[]{:S(2)}) collective-permute-start(f32[128,128]{1,0:T(8,128)S(1)} %get-tuple-element.87), channel_id=1, source_target_pairs={{0,1},{1,0},{2,3},{3,2},{4,5},{5,4},{6,7},{7,6},{8,9},{9,8},{10,11... | collective-permute-start | bytes 196616 | tf_op jit(solution)/shard_map/ppermute | solution.py:229
  28.1 12.5 %collective-permute-start.15 = (f32[256,128]{1,0:T(8,128)S(1)}, f32[256,128]{1,0:T(8,128)S(1)}, u32[]{:S(2)}, u32[]{:S(2)}) collective-permute-start(f32[256,128]{1,0:T(8,128)S(1)} %get-tuple-element.94), channel_id=1, source_target_pairs={{0,16},{1,17},{2,18},{3,19},{4,20},{5,21},{6,22},{7,23},{8,24},{9,... | collective-permute-start | bytes 393224 | tf_op jit(solution)/shard_map/ppermute | solution.py:229
  29.3 11.2 %collective-permute-start.16 = (f32[256,128]{1,0:T(8,128)S(1)}, f32[256,128]{1,0:T(8,128)S(1)}, u32[]{:S(2)}, u32[]{:S(2)}) collective-permute-start(f32[256,128]{1,0:T(8,128)S(1)} %get-tuple-element.95), channel_id=1, source_target_pairs={{0,24},{1,25},{2,26},{3,27},{4,28},{5,29},{6,30},{7,31},{8,16},{9,... | collective-permute-start | bytes 393224 | tf_op jit(solution)/shard_map/ppermute | solution.py:229
  33.1 10.0 %collective-permute-start.11 = (f32[256,128]{1,0:T(8,128)S(1)}, f32[256,128]{1,0:T(8,128)S(1)}, u32[]{:S(2)}, u32[]{:S(2)}) collective-permute-start(f32[256,128]{1,0:T(8,128)S(1)} %get-tuple-element.89), channel_id=1, source_target_pairs={{0,8},{1,9},{2,10},{3,11},{4,12},{5,13},{6,14},{7,15},{8,0},{9,1},... | collective-permute-start | bytes 393224 | tf_op jit(solution)/shard_map/ppermute | solution.py:229
  33.9 9.2 %collective-permute-start.12 = (f32[256,128]{1,0:T(8,128)S(1)}, f32[256,128]{1,0:T(8,128)S(1)}, u32[]{:S(2)}, u32[]{:S(2)}) collective-permute-start(f32[256,128]{1,0:T(8,128)S(1)} %get-tuple-element.90), channel_id=1, source_target_pairs={{0,16},{1,17},{2,18},{3,19},{4,20},{5,21},{6,22},{7,23},{8,24},{9,... | collective-permute-start | bytes 393224 | tf_op jit(solution)/shard_map/ppermute | solution.py:229
  35.0 8.0 %collective-permute-start.13 = (f32[256,128]{1,0:T(8,128)S(1)}, f32[256,128]{1,0:T(8,128)S(1)}, u32[]{:S(2)}, u32[]{:S(2)}) collective-permute-start(f32[256,128]{1,0:T(8,128)S(1)} %get-tuple-element.91), channel_id=1, source_target_pairs={{0,24},{1,25},{2,26},{3,27},{4,28},{5,29},{6,30},{7,31},{8,16},{9,... | collective-permute-start | bytes 393224 | tf_op jit(solution)/shard_map/ppermute | solution.py:229

commit v4 on v3

--- a/solution.py
+++ b/solution.py
@@ -13,8 +13,8 @@
 HEAD = 128
 TILE = 256
 GROUPS = 4
-STATE_VMEM = 12
-WRITE = 2
+STATE_VMEM = 8
+WRITE = 4
 F32 = jnp.float32
 BF16 = jnp.bfloat16
 AXES = ("seq", "resp")
@@ -34,122 +34,154 @@
     return jnp.logical_or(row == 0, lax.axis_index("seq") < limit)
 
 
-def state_kernel(n, *refs):
-    ins = refs[:5]
-    share_refs = refs[5 : 5 + n]
-    rest_refs = refs[5 + n : 5 + 2 * n]
-    q_ref, k_ref, v_ref, g_ref = held = refs[5 + 2 * n : 9 + 2 * n]
-    share, rest, lengths_ref, sem = refs[9 + 2 * n :]
-    piece = share_refs[0].shape[0]
-    counts = pltpu.make_async_copy(ins[4], lengths_ref, sem.at[4])
+def state_kernel(n, tiles, share, lengths_hbm, *refs):
+    prompt = lax.axis_index("resp") == 0
+    keys_values = prompt == share
+    sources = refs[:4]
+    piece_refs = refs[4 : 4 + n]
+    held = refs[4 + n : 6 + n]
+    sums = refs[6 + n : 5 + n + tiles]
+    total, lengths_ref, sem, count_sem = refs[-4:]
+    piece = piece_refs[0].shape[0]
+    counts = pltpu.make_async_copy(lengths_hbm, lengths_ref, count_sem)
+    cut = [pl.ds(i * TILE, TILE) for i in range(tiles)]
+
+    def copies(pair):
+        return [
+            [pltpu.make_async_copy(pair[x].at[c], held[x].at[c], sem.at[x, i]) for x in (0, 1)]
+            for i, c in enumerate(cut)
+        ]
+
+    def start(pair):
+        for tile in copies(pair):
+            for copy in tile:
+                copy.start()
+
     counts.start()
-    copies = [pltpu.make_async_copy(ins[i], held[i], sem.at[i]) for i in (1, 2, 0, 3)]
-    for copy in copies:
-        copy.start()
+
+    @pl.when(keys_values)
+    def _():
+        start(sources[:2])
+
+    @pl.when(jnp.logical_not(keys_values))
+    def _():
+        start(sources[2:])
+
+    waits = copies(sources[:2])
     place = lax.axis_index("seq")
-    prompt = lax.axis_index("resp") == 0
     heads = [pl.ds(h * HEAD, HEAD) for h in range(HEADS)]
-    counts.wait()
-    keep = kept(lengths_ref)
-    copies[0].wait()
-    copies[1].wait()
-    for h in heads:
-        rest[h, :] = jnp.where(keep, dot(k_ref[:, h], v_ref[:, h], TN), 0.0)
-    copies[2].wait()
-    copies[3].wait()
-    for h in heads:
-        kv = rest[h, :]
-        qg = jnp.where(keep, dot(q_ref[:, h], g_ref[:, h], TN), 0.0)
-        share[h, :] = jnp.where(prompt, kv, qg)
-        rest[h, :] = jnp.where(prompt, qg, kv)
+    for i in range(tiles):
+        if i == 0:
+            counts.wait()
+        for copy in waits[i]:
+            copy.wait()
+
+        @pl.when(jnp.logical_not(kept(lengths_ref)))
+        def _():
+            for ref in held:
+                ref[cut[i], :] = jnp.zeros((TILE, ref.shape[1]), BF16)
+
+        for h in heads:
+            new = dot(held[0][cut[i], h], held[1][cut[i], h], TN)
+            if i < tiles - 1:
+                sums[i][h, :] = new
+                continue
+            parts = [ref[h, :] for ref in sums] + [new]
+            whole = sum(parts[1:], parts[0])
+            upto = None
+            for ref, part in zip(sums, parts):
+                upto = part if upto is None else upto + part
+                ref[h, :] = jnp.where(keys_values, upto, whole - upto if tiles > 2 else new)
+            total[h, :] = whole
     for m in range(n):
         at = pl.multiple_of(jnp.bitwise_xor(place, m) * piece, piece)
-        share_refs[m][...] = share[pl.ds(at, piece), :]
-        rest_refs[m][...] = rest[pl.ds(at, piece), :]
-
-
-def inner_kernel(factor, first, q_ref, k_ref, v_ref, g_ref, *outs):
-    tiles = q_ref.shape[0] // TILE
-    cut = [pl.ds(i * TILE, TILE) for i in range(tiles)]
+        piece_refs[m][...] = total[pl.ds(at, piece), :]
+
+
+def inner_kernel(factor, first, *refs):
+    outs = refs[4:]
     rows = lax.broadcasted_iota(jnp.int32, (TILE, TILE), 0)
     columns = lax.broadcasted_iota(jnp.int32, (TILE, TILE), 1)
     causal = rows >= columns
-    for h in range(outs[0].shape[1] // HEAD):
-        here = pl.ds((first + h) * HEAD, HEAD)
-        q, k, v, g = ([ref[c, here] for c in cut] for ref in (q_ref, k_ref, v_ref, g_ref))
-        sums = [[None] * tiles for _ in range(4)]
-
-        def add(which, at, term):
-            old = sums[which][at]
-            sums[which][at] = term if old is None else old + term
-
-        for i in range(tiles):
-            for j in range(i + 1):
-                a = dot(q[i], k[j], NT) * factor
-                p = dot(g[i], v[j], NT) * factor
-                if i == j:
-                    a = jnp.where(causal, a, 0.0)
-                    p = jnp.where(causal, p, 0.0)
-                a = a.astype(BF16)
-                p = p.astype(BF16)
-                add(0, i, dot(a, v[j], NN))
-                add(1, i, dot(p, k[j], NN))
-                add(2, j, dot(p, q[i], TN))
-                add(3, j, dot(a, g[i], TN))
-        for ref, parts in zip(outs, sums):
-            for c, part in zip(cut, parts):
-                ref[c, pl.ds(h * HEAD, HEAD)] = part
-
-
-def outer_kernel(factor, groups, n, first, lengths_hbm, *refs):
-    arrays = refs[:4]
-    parts = refs[4 : 4 + 4 * groups]
-    refs = refs[4 + 4 * groups :]
+
+    def write(arrays):
+        for h in range(outs[0].shape[1] // HEAD):
+            here = pl.ds((first + h) * HEAD, HEAD)
+            there = pl.ds(h * HEAD, HEAD)
+            for i in range(arrays[0].shape[0] // TILE):
+                c = pl.ds(i * TILE, TILE)
+                q, k, v, g = (ref[c, here] for ref in arrays)
+                a = jnp.where(causal, dot(q, k, NT) * factor, 0.0).astype(BF16)
+                p = jnp.where(causal, dot(g, v, NT) * factor, 0.0).astype(BF16)
+                outs[0][c, there] = dot(a, v, NN)
+                outs[1][c, there] = dot(p, k, NN)
+                outs[2][c, there] = dot(p, q, TN)
+                outs[3][c, there] = dot(a, g, TN)
+
+    prompt = lax.axis_index("resp") == 0
+    a, b, c, d = refs[:4]
+
+    @pl.when(prompt)
+    def _():
+        write((c, a, b, d))
+
+    @pl.when(jnp.logical_not(prompt))
+    def _():
+        write((a, c, d, b))
+
+
+def outer_kernel(factor, groups, n, tiles, first, *refs):
+    arrays = refs[:2]
+    parts = refs[2 : 2 + 4 * groups]
+    refs = refs[2 + 4 * groups :]
     pieces = refs[:n]
-    outs = refs[n : n + 4] if first else refs[n + 4 : n + 8]
-    buffers = refs[-6:-4]
-    state, lengths_ref, sem, count_sem = refs[-4:]
-    counts = pltpu.make_async_copy(lengths_hbm, lengths_ref, count_sem)
-    counts.start()
+    sums = refs[n : n + tiles - 1]
+    refs = refs[n + tiles - 1 :]
+    outs = refs[:4] if first else refs[4:8]
+    buffers = refs[-4:-2]
+    state, sem = refs[-2:]
     place = lax.axis_index("seq")
     prompt = lax.axis_index("resp") == 0
     piece = pieces[0].shape[0]
     for m in range(n):
         at = pl.multiple_of(jnp.bitwise_xor(place, m) * piece, piece)
         state[pl.ds(at, piece), :] = pieces[m][...]
-    counts.wait()
-    keep = kept(lengths_ref)
     span = HEADS // groups
 
-    def write(sides):
+    def write(sides, added):
         copies = []
-        for head in range(HEADS):
-            h = pl.ds(head * HEAD, HEAD)
-            within = pl.ds(head % span * HEAD, HEAD)
-            low = state[h, :].astype(BF16)
-            for buffer, (which, source, dims) in zip(buffers, sides):
-                part = parts[head // span * 4 + which][:, within]
-                total = part + factor * dot(arrays[source][:, h], low, dims)
-                buffer[:, h] = jnp.where(keep, total, 0.0).astype(BF16)
-            if head % WRITE == WRITE - 1:
-                at = head // WRITE
-                wide = pl.ds(at * WRITE * HEAD, WRITE * HEAD)
-                for i, (which, _, _) in enumerate(sides):
-                    copy = pltpu.make_async_copy(
-                        buffers[i].at[:, wide], outs[which].at[:, wide], sem.at[i, at]
-                    )
-                    copy.start()
-                    copies.append(copy)
+        for tile in range(tiles):
+            c = pl.ds(tile * TILE, TILE)
+            for head in range(HEADS):
+                h = pl.ds(head * HEAD, HEAD)
+                within = pl.ds(head % span * HEAD, HEAD)
+                total = state[h, :]
+                if added[tile] is not None:
+                    total = total + added[tile][h, :]
+                low = total.astype(BF16)
+                for buffer, (which, source, dims) in zip(buffers, sides):
+                    part = parts[head // span * 4 + which][c, within]
+                    out = part + factor * dot(arrays[source][c, h], low, dims)
+                    buffer[c, h] = out.astype(BF16)
+                if head % WRITE == WRITE - 1:
+                    at = head // WRITE
+                    wide = pl.ds(at * WRITE * HEAD, WRITE * HEAD)
+                    for i, (which, _, _) in enumerate(sides):
+                        copy = pltpu.make_async_copy(
+                            buffers[i].at[c, wide], outs[which].at[c, wide], sem.at[i, tile, at]
+                        )
+                        copy.start()
+                        copies.append(copy)
         for copy in copies:
             copy.wait()
 
     @pl.when(prompt == first)
     def _():
-        write(((0, 0, NN), (1, 3, NT)))
+        write(((0, 0, NN), (1, 1, NT)), (None, *sums))
 
     @pl.when(prompt != first)
     def _():
-        write(((2, 2, NT), (3, 1, NN)))
+        write(((2, 1, NT), (3, 0, NN)), (*sums, None))
 
 
 def pair_kernel(mine_ref, new_ref, send_ref, sum_ref):
@@ -232,6 +264,7 @@
     array = pltpu.VMEM((tokens, width), BF16)
     stack = pltpu.VMEM((HEADS * HEAD, HEAD), F32)
     counts = pltpu.SMEM(lengths.shape, jnp.int32)
+    tiles = tokens // TILE
     piece = HEADS * HEAD // n
     piece_shape = jax.ShapeDtypeStruct((piece, HEAD), F32)
     half_shape = jax.ShapeDtypeStruct((piece // 2, HEAD), F32)
@@ -240,17 +273,29 @@
     def far(x):
         return pltpu.with_memory_space_constraint(x, pltpu.HBM)
 
-    *pieces, q, k, v, g = pl.pallas_call(
-        functools.partial(state_kernel, n),
-        in_specs=[there] * 5,
-        out_specs=[whole] * (2 * n + 4),
-        scratch_shapes=[stack] * 2 + [counts, pltpu.SemaphoreType.DMA((5,))],
-        out_shape=[piece_shape] * (2 * n) + [jax.ShapeDtypeStruct((tokens, width), BF16)] * 4,
-        compiler_params=pltpu.CompilerParams(vmem_limit_bytes=STATE_VMEM * 2**20),
-        cost_estimate=pl.CostEstimate(
-            flops=4 * size * HEAD, bytes_accessed=8 * size, transcendentals=0
-        ),
-    )(far(q), far(k), far(v), far(g), far(lengths))
+    def state(share):
+        made = pl.pallas_call(
+            functools.partial(state_kernel, n, tiles, share),
+            in_specs=[there] * 5,
+            out_specs=[whole] * (n + 1 + tiles),
+            scratch_shapes=[
+                stack,
+                counts,
+                pltpu.SemaphoreType.DMA((2, tiles)),
+                pltpu.SemaphoreType.DMA,
+            ],
+            out_shape=[piece_shape] * n
+            + [jax.ShapeDtypeStruct((tokens, width), BF16)] * 2
+            + [jax.ShapeDtypeStruct((HEADS * HEAD, HEAD), F32)] * (tiles - 1),
+            compiler_params=pltpu.CompilerParams(vmem_limit_bytes=STATE_VMEM * 2**20),
+            cost_estimate=pl.CostEstimate(
+                flops=2 * size * HEAD, bytes_accessed=4 * size, transcendentals=0
+            ),
+        )(far(lengths), far(k), far(v), far(q), far(g))
+        return made[:n], made[n : n + 2], made[n + 2 :]
+
+    share, share_arrays, share_sums = state(True)
+    rest, rest_arrays, rest_sums = state(False)
 
     def swapped(pieces):
         came = [pieces[0]]
@@ -274,8 +319,8 @@
             compiler_params=small,
         )(*pieces)
 
-    *share, mine, give = scan(True, *swapped(pieces[:n]))
-    rest = swapped(pieces[n:])
+    *share, mine, give = scan(True, *swapped(share))
+    rest = swapped(rest)
     share = swapped(share)
 
     def across(x, bits):
@@ -318,28 +363,27 @@
                 bytes_accessed=24 * size // GROUPS,
                 transcendentals=0,
             ),
-        )(q, k, v, g)
+        )(*share_arrays, *rest_arrays)
     outs = []
-    for first, pieces in ((True, share), (False, rest)):
-        fixed = 5 + 4 * GROUPS + n
+    ends = (
+        (True, share, rest_arrays, share_sums),
+        (False, rest, share_arrays, rest_sums),
+    )
+    for first, pieces, arrays, sums in ends:
+        fixed = 2 + 4 * GROUPS + n + len(sums)
         outs = pl.pallas_call(
-            functools.partial(outer_kernel, factor, GROUPS, n, first),
-            in_specs=[there] + [whole] * (fixed - 1) + [there] * len(outs),
+            functools.partial(outer_kernel, factor, GROUPS, n, tiles, first),
+            in_specs=[whole] * fixed + [there] * len(outs),
             out_specs=[there] * 4,
             scratch_shapes=[array] * 2
-            + [
-                stack,
-                counts,
-                pltpu.SemaphoreType.DMA((2, HEADS // WRITE)),
-                pltpu.SemaphoreType.DMA,
-            ],
+            + [stack, pltpu.SemaphoreType.DMA((2, tiles, HEADS // WRITE))],
             out_shape=[jax.ShapeDtypeStruct((tokens, width), BF16)] * 4,
             input_output_aliases={fixed + i: i for i in range(len(outs))},
             compiler_params=pltpu.CompilerParams(vmem_limit_bytes=8 * 2**20),
             cost_estimate=pl.CostEstimate(
                 flops=4 * size * HEAD, bytes_accessed=16 * size, transcendentals=0
             ),
-        )(far(lengths), q, k, v, g, *parts, *pieces, *outs)
+        )(*arrays, *parts, *pieces, *sums, *outs)
     return tuple(x.reshape(1, tokens, width) for x in outs)
 
 

time: 45.9 us -> 45.3 us (0.987)
  Pallas kernels: 16 us -> 14.6 us
  waiting for transfers between devices: 9.15 us -> 9.82 us
    pallas_call x4, Pallas kernels: 7.8 us -> 6.59 us  [per_device(): pl.pallas_call(functools.partial(inner_kernel, factor, group * HEADS // G...]
    ppermute x17, waiting for transfers between devices: 9.15 us -> 9.82 us  [move(): return lax.ppermute(x, AXES, pairs)]
    pallas_call x3 -> x4, Pallas kernels: 7.84 us -> 7.61 us  [the longest x2 4.04 us: state(): pl.pallas_call(functools.partial(state_kernel, n, tiles, share), in_specs...]
  transfers between devices with their start and end apart: 17 -> 17, of which waited for: 5 -> 5; matrix products, arithmetic and copies ran while one was open for 0% -> 0% of each run, Pallas kernels for 23% -> 24%
where the time goes in v4:
time: 45.3 us; the launch traced here: 45.1 us
  starting transfers between devices  19.8 us (44%)
  Pallas kernels  14.6 us (32%)
  waiting for transfers between devices  9.82 us (22%)
  between operations  0.94 us (2%)
    ppermute x17, starting transfers between devices, move(): return lax.ppermute(x, AXES, pairs)  19.8 us
    ppermute x17, waiting for transfers between devices, move(): return lax.ppermute(x, AXES, pairs)  9.82 us
    pallas_call x4, Pallas kernels, per_device(): pl.pallas_call(functools.partial(inner_kernel, factor, group * HEADS // G...  6.59 us
    pallas_call x2, Pallas kernels, state(): pl.pallas_call(functools.partial(state_kernel, n, tiles, share), in_specs...  4.04 us
    pallas_call x2, Pallas kernels, per_device(): pl.pallas_call(functools.partial(outer_kernel, factor, GROUPS, n, tiles,...  3.57 us
  transfers between devices with their start and end apart: 17, of which 5 were waited for; matrix products, arithmetic and copies ran while one was open for 0% of the time, Pallas kernels for 24%

profile of v4, /device:TPU:0, one launch (start us, length us, event | category | flops | bytes accessed | tf_op | source)
XLA Modules:
  0.0 45.1 jit_solution(12980003072747721886)
XLA Ops:
  0.6 2.0 %shard_map.84 = (f32[256,128]{1,0:T(8,128)S(1)}, f32[256,128]{1,0:T(8,128)S(1)}, f32[256,128]{1,0:T(8,128)S(1)}, f32[256,128]{1,0:T(8,128)S(1)}, bf16[512,1024]{...) custom-call(s32[7]{0:T(128)} %lengths_hbm.3, bf16[512,1024]{1,0:T(8,128)(2,1)} %bitcast.8, ...), custom_call_target="tpu_custom_call" | custom-call | flops 134217728 | bytes 2097152 | tf_op jit(solution)/shard_map/pallas_call | solution.py:277
  2.7 3.0 %collective-permute-start.3 = (f32[256,128]{1,0:T(8,128)S(1)}, f32[256,128]{1,0:T(8,128)S(1)}, u32[]{:S(2)}, u32[]{:S(2)}) collective-permute-start(f32[256,128]{1,0:T(8,128)S(1)} %get-tuple-element.81), channel_id=1, source_target_pairs={{0,8},{1,9},{2,10},{3,11},{4,12},{5,13},{6,14},{7,15},{8,0},{9,1},... | collective-permute-start | bytes 393224 | tf_op jit(solution)/shard_map/ppermute | solution.py:261
  5.7 1.5 %collective-permute-start.4 = (f32[256,128]{1,0:T(8,128)S(1)}, f32[256,128]{1,0:T(8,128)S(1)}, u32[]{:S(2)}, u32[]{:S(2)}) collective-permute-start(f32[256,128]{1,0:T(8,128)S(1)} %get-tuple-element.82), channel_id=1, source_target_pairs={{0,16},{1,17},{2,18},{3,19},{4,20},{5,21},{6,22},{7,23},{8,24},{9,... | collective-permute-start | bytes 393224 | tf_op jit(solution)/shard_map/ppermute | solution.py:261
  7.2 0.0 collective-permute-start.5
  7.2 2.3 %collective-permute-done.3.refs_1_ = f32[256,128]{1,0:T(8,128)S(1)} collective-permute-done((f32[256,128]{1,0:T(8,128)S(1)}, f32[256,128]{1,0:T(8,128)S(1)}, u32[]{:S(2)}, u32[]{:S(2)}) %collective-permute-start.3) | collective-permute-done | bytes 131104 | tf_op jit(solution)/shard_map/ppermute | solution.py:261
  9.6 3.9 %collective-permute-done.4.refs_2_ = f32[256,128]{1,0:T(8,128)S(1)} collective-permute-done((f32[256,128]{1,0:T(8,128)S(1)}, f32[256,128]{1,0:T(8,128)S(1)}, u32[]{:S(2)}, u32[]{:S(2)}) %collective-permute-start.4) | collective-permute-done | bytes 131104 | tf_op jit(solution)/shard_map/ppermute | solution.py:261
  13.5 0.0 collective-permute-done.5.refs_3_
  13.5 0.2 shard_map.90
  13.7 0.1 collective-permute-start.6
  13.7 1.2 %collective-permute-done.6.new_ref = f32[128,128]{1,0:T(8,128)S(1)} collective-permute-done((f32[128,128]{1,0:T(8,128)S(1)}, f32[128,128]{1,0:T(8,128)S(1)}, u32[]{:S(2)}, u32[]{:S(2)}) %collective-permute-start.6) | collective-permute-done | bytes 65568 | tf_op jit(solution)/shard_map/ppermute | solution.py:261
  15.0 3.7 %collective-permute-start.9 = (f32[128,128]{1,0:T(8,128)S(1)}, f32[128,128]{1,0:T(8,128)S(1)}, u32[]{:S(2)}, u32[]{:S(2)}) collective-permute-start(f32[128,128]{1,0:T(8,128)S(1)} %get-tuple-element.86.send_ref), channel_id=1, source_target_pairs={{0,6},{1,7},{2,3},{3,2},{4,5},{5,4},{6,0},{7,1},{8,14},{9,15},{10,... | collective-permute-start | bytes 196616 | tf_op jit(solution)/shard_map/ppermute | solution.py:261
  18.7 0.0 collective-permute-start.8
  18.7 2.0 %shard_map.85 = (f32[256,128]{1,0:T(8,128)S(1)}, f32[256,128]{1,0:T(8,128)S(1)}, f32[256,128]{1,0:T(8,128)S(1)}, f32[256,128]{1,0:T(8,128)S(1)}, bf16[512,1024]{...) custom-call(s32[7]{0:T(128)} %lengths_hbm.3, bf16[512,1024]{1,0:T(8,128)(2,1)} %bitcast.9, ...), custom_call_target="tpu_custom_call" | custom-call | flops 134217728 | bytes 2097152 | tf_op jit(solution)/shard_map/pallas_call | solution.py:277
  20.7 1.3 %collective-permute-start = (f32[256,128]{1,0:T(8,128)S(1)}, f32[256,128]{1,0:T(8,128)S(1)}, u32[]{:S(2)}, u32[]{:S(2)}) collective-permute-start(f32[256,128]{1,0:T(8,128)S(1)} %get-tuple-element.77), channel_id=1, source_target_pairs={{0,8},{1,9},{2,10},{3,11},{4,12},{5,13},{6,14},{7,15},{8,0},{9,1},... | collective-permute-start | bytes 393224 | tf_op jit(solution)/shard_map/ppermute | solution.py:261
  22.0 0.8 %collective-permute-start.1 = (f32[256,128]{1,0:T(8,128)S(1)}, f32[256,128]{1,0:T(8,128)S(1)}, u32[]{:S(2)}, u32[]{:S(2)}) collective-permute-start(f32[256,128]{1,0:T(8,128)S(1)} %get-tuple-element.78), channel_id=1, source_target_pairs={{0,16},{1,17},{2,18},{3,19},{4,20},{5,21},{6,22},{7,23},{8,24},{9,... | collective-permute-start | bytes 393224 | tf_op jit(solution)/shard_map/ppermute | solution.py:261
  22.8 0.0 collective-permute-start.7
  22.8 0.0 collective-permute-done.9.refs_2_
  22.8 1.4 %collective-permute-start.2 = (f32[256,128]{1,0:T(8,128)S(1)}, f32[256,128]{1,0:T(8,128)S(1)}, u32[]{:S(2)}, u32[]{:S(2)}) collective-permute-start(f32[256,128]{1,0:T(8,128)S(1)} %get-tuple-element.79), channel_id=1, source_target_pairs={{0,24},{1,25},{2,26},{3,27},{4,28},{5,29},{6,30},{7,31},{8,16},{9,... | collective-permute-start | bytes 393224 | tf_op jit(solution)/shard_map/ppermute | solution.py:261
  24.3 0.0 collective-permute-done.8.refs_1_
  24.3 1.2 %collective-permute-start.14 = (f32[256,128]{1,0:T(8,128)S(1)}, f32[256,128]{1,0:T(8,128)S(1)}, u32[]{:S(2)}, u32[]{:S(2)}) collective-permute-start(f32[256,128]{1,0:T(8,128)S(1)} %get-tuple-element.96), channel_id=1, source_target_pairs={{0,8},{1,9},{2,10},{3,11},{4,12},{5,13},{6,14},{7,15},{8,0},{9,1},... | collective-permute-start | bytes 393224 | tf_op jit(solution)/shard_map/ppermute | solution.py:261
  25.5 1.6 %collective-permute-done.7.refs_0_ = f32[128,128]{1,0:T(8,128)S(1)} collective-permute-done((f32[128,128]{1,0:T(8,128)S(1)}, f32[128,128]{1,0:T(8,128)S(1)}, u32[]{:S(2)}, u32[]{:S(2)}) %collective-permute-start.7) | collective-permute-done | bytes 65568 | tf_op jit(solution)/shard_map/ppermute | solution.py:261
  27.1 0.1 collective-permute-start.10
  27.2 1.6 %shard_map.89 = (f32[512,256]{1,0:T(8,128)S(1)}, f32[512,256]{1,0:T(8,128)S(1)}, f32[512,256]{1,0:T(8,128)S(1)}, f32[512,256]{1,0:T(8,128)S(1)}) custom-call(bf16[512,1024]{1,0:T(8,128)(2,1)S(1)} %get-tuple-element.56.refs_0_, bf16[512,1024]{1,0:T(8,128)(2,1)S(1)} %get-tuple-element.57.refs_1_, bf16[512,1024]{1,0:T(8,128)(2,1)S(1)} %get-tuple-element.58.refs_2_.refs_0_, ...), custom_call_target="tpu_custom_call" | custom-call | flops 603979776 | bytes 3145728 | tf_op jit(solution)/shard_map/pallas_call | solution.py:355
  28.8 0.0 collective-permute-done.refs_1_
  28.8 1.3 %collective-permute-start.15 = (f32[256,128]{1,0:T(8,128)S(1)}, f32[256,128]{1,0:T(8,128)S(1)}, u32[]{:S(2)}, u32[]{:S(2)}) collective-permute-start(f32[256,128]{1,0:T(8,128)S(1)} %get-tuple-element.97), channel_id=1, source_target_pairs={{0,16},{1,17},{2,18},{3,19},{4,20},{5,21},{6,22},{7,23},{8,24},{9,... | collective-permute-start | bytes 393224 | tf_op jit(solution)/shard_map/ppermute | solution.py:261
  30.1 0.0 collective-permute-done.1.refs_2_
  30.1 1.7 %collective-permute-start.16 = (f32[256,128]{1,0:T(8,128)S(1)}, f32[256,128]{1,0:T(8,128)S(1)}, u32[]{:S(2)}, u32[]{:S(2)}) collective-permute-start(f32[256,128]{1,0:T(8,128)S(1)} %get-tuple-element.98), channel_id=1, source_target_pairs={{0,24},{1,25},{2,26},{3,27},{4,28},{5,29},{6,30},{7,31},{8,16},{9,... | collective-permute-start | bytes 393224 | tf_op jit(solution)/shard_map/ppermute | solution.py:261
  31.8 1.6 %shard_map.88 = (f32[512,256]{1,0:T(8,128)S(1)}, f32[512,256]{1,0:T(8,128)S(1)}, f32[512,256]{1,0:T(8,128)S(1)}, f32[512,256]{1,0:T(8,128)S(1)}) custom-call(bf16[512,1024]{1,0:T(8,128)(2,1)S(1)} %get-tuple-element.56.refs_0_, bf16[512,1024]{1,0:T(8,128)(2,1)S(1)} %get-tuple-element.57.refs_1_, bf16[512,1024]{1,0:T(8,128)(2,1)S(1)} %get-tuple-element.58.refs_2_.refs_0_, ...), custom_call_target="tpu_custom_call" | custom-call | flops 603979776 | bytes 3145728 | tf_op jit(solution)/shard_map/pallas_call | solution.py:355
  33.5 0.0 collective-permute-done.2.refs_3_
  33.5 0.0 collective-permute-done.10.refs_5_
  33.5 0.2 shard_map.93
  33.7 0.6 %collective-permute-start.11 = (f32[256,128]{1,0:T(8,128)S(1)}, f32[256,128]{1,0:T(8,128)S(1)}, u32[]{:S(2)}, u32[]{:S(2)}) collective-permute-start(f32[256,128]{1,0:T(8,128)S(1)} %get-tuple-element.91), channel_id=1, source_target_pairs={{0,8},{1,9},{2,10},{3,11},{4,12},{5,13},{6,14},{7,15},{8,0},{9,1},... | collective-permute-start | bytes 393224 | tf_op jit(solution)/shard_map/ppermute | solution.py:261
  34.3 1.2 %collective-permute-start.12 = (f32[256,128]{1,0:T(8,128)S(1)}, f32[256,128]{1,0:T(8,128)S(1)}, u32[]{:S(2)}, u32[]{:S(2)}) collective-permute-start(f32[256,128]{1,0:T(8,128)S(1)} %get-tuple-element.92), channel_id=1, source_target_pairs={{0,16},{1,17},{2,18},{3,19},{4,20},{5,21},{6,22},{7,23},{8,24},{9,... | collective-permute-start | bytes 393224 | tf_op jit(solution)/shard_map/ppermute | solution.py:261
  35.5 0.0 collective-permute-done.14.refs_19_
  35.5 1.7 %collective-permute-start.13 = (f32[256,128]{1,0:T(8,128)S(1)}, f32[256,128]{1,0:T(8,128)S(1)}, u32[]{:S(2)}, u32[]{:S(2)}) collective-permute-start(f32[256,128]{1,0:T(8,128)S(1)} %get-tuple-element.93), channel_id=1, source_target_pairs={{0,24},{1,25},{2,26},{3,27},{4,28},{5,29},{6,30},{7,31},{8,16},{9,... | collective-permute-start | bytes 393224 | tf_op jit(solution)/shard_map/ppermute | solution.py:261
  37.2 1.6 %shard_map.87 = (f32[512,256]{1,0:T(8,128)S(1)}, f32[512,256]{1,0:T(8,128)S(1)}, f32[512,256]{1,0:T(8,128)S(1)}, f32[512,256]{1,0:T(8,128)S(1)}) custom-call(bf16[512,1024]{1,0:T(8,128)(2,1)S(1)} %get-tuple-element.56.refs_0_, bf16[512,1024]{1,0:T(8,128)(2,1)S(1)} %get-tuple-element.57.refs_1_, bf16[512,1024]{1,0:T(8,128)(2,1)S(1)} %get-tuple-element.58.refs_2_.refs_0_, ...), custom_call_target="tpu_custom_call" | custom-call | flops 603979776 | bytes 3145728 | tf_op jit(solution)/shard_map/pallas_call | solution.py:355
  38.8 1.8 %shard_map.86 = (f32[512,256]{1,0:T(8,128)S(1)}, f32[512,256]{1,0:T(8,128)S(1)}, f32[512,256]{1,0:T(8,128)S(1)}, f32[512,256]{1,0:T(8,128)S(1)}) custom-call(bf16[512,1024]{1,0:T(8,128)(2,1)S(1)} %get-tuple-element.56.refs_0_, bf16[512,1024]{1,0:T(8,128)(2,1)S(1)} %get-tuple-element.57.refs_1_, bf16[512,1024]{1,0:T(8,128)(2,1)S(1)} %get-tuple-element.58.refs_2_.refs_0_, ...), custom_call_target="tpu_custom_call" | custom-call | flops 603979776 | bytes 3145728 | tf_op jit(solution)/shard_map/pallas_call | solution.py:355
  40.6 0.0 collective-permute-done.15.refs_20_
  40.6 0.0 collective-permute-done.16.refs_21_
  40.6 1.8 %shard_map.94 = (bf16[512,1024]{1,0:T(8,128)(2,1)}, bf16[512,1024]{1,0:T(8,128)(2,1)}, bf16[512,1024]{1,0:T(8,128)(2,1)}, bf16[512,1024]{1,0:T(8,128)(2,1)}) custom-call(bf16[512,1024]{1,0:T(8,128)(2,1)S(1)} %get-tuple-element.58.refs_2_.refs_0_, bf16[512,1024]{1,0:T(8,128)(2,1)S(1)} %get-tuple-element.59.refs_3_.refs_1_, ...), custom_call_target="tpu_custom_call" | custom-call | flops 268435456 | bytes 8388608 | tf_op jit(solution)/shard_map/pallas_call | solution.py:374
  42.5 0.0 collective-permute-done.11.refs_19_
  42.5 0.7 %collective-permute-done.12.refs_20_ = f32[256,128]{1,0:T(8,128)S(1)} collective-permute-done((f32[256,128]{1,0:T(8,128)S(1)}, f32[256,128]{1,0:T(8,128)S(1)}, u32[]{:S(2)}, u32[]{:S(2)}) %collective-permute-start.12) | collective-permute-done | bytes 131104 | tf_op jit(solution)/shard_map/ppermute | solution.py:261
  43.2 0.0 collective-permute-done.13.refs_21_
  43.2 1.7 %shard_map.95 = (bf16[512,1024]{1,0:T(8,128)(2,1)}, bf16[512,1024]{1,0:T(8,128)(2,1)}, bf16[512,1024]{1,0:T(8,128)(2,1)}, bf16[512,1024]{1,0:T(8,128)(2,1)}) custom-call(bf16[512,1024]{1,0:T(8,128)(2,1)S(1)} %get-tuple-element.56.refs_0_, ...), custom_call_target="tpu_custom_call", output_to_operand_aliasing={{0}: (23, {}), {1}: (24, {}), {2}: (25, {}), {3}: (26, {})} | custom-call | flops 268435456 | bytes 8388608 | tf_op jit(solution)/shard_map/pallas_call | solution.py:374
  (2 shorter events, 0.1 us)
Async XLA Ops:
  2.7 6.9 %collective-permute-start.3 = (f32[256,128]{1,0:T(8,128)S(1)}, f32[256,128]{1,0:T(8,128)S(1)}, u32[]{:S(2)}, u32[]{:S(2)}) collective-permute-start(f32[256,128]{1,0:T(8,128)S(1)} %get-tuple-element.81), channel_id=1, source_target_pairs={{0,8},{1,9},{2,10},{3,11},{4,12},{5,13},{6,14},{7,15},{8,0},{9,1},... | collective-permute-start | bytes 393224 | tf_op jit(solution)/shard_map/ppermute | solution.py:261
  5.7 7.8 %collective-permute-start.4 = (f32[256,128]{1,0:T(8,128)S(1)}, f32[256,128]{1,0:T(8,128)S(1)}, u32[]{:S(2)}, u32[]{:S(2)}) collective-permute-start(f32[256,128]{1,0:T(8,128)S(1)} %get-tuple-element.82), channel_id=1, source_target_pairs={{0,16},{1,17},{2,18},{3,19},{4,20},{5,21},{6,22},{7,23},{8,24},{9,... | collective-permute-start | bytes 393224 | tf_op jit(solution)/shard_map/ppermute | solution.py:261
  7.2 6.3 %collective-permute-start.5 = (f32[256,128]{1,0:T(8,128)S(1)}, f32[256,128]{1,0:T(8,128)S(1)}, u32[]{:S(2)}, u32[]{:S(2)}) collective-permute-start(f32[256,128]{1,0:T(8,128)S(1)} %get-tuple-element.83), channel_id=1, source_target_pairs={{0,24},{1,25},{2,26},{3,27},{4,28},{5,29},{6,30},{7,31},{8,16},{9,... | collective-permute-start | bytes 393224 | tf_op jit(solution)/shard_map/ppermute | solution.py:261
  13.7 1.3 %collective-permute-start.6 = (f32[128,128]{1,0:T(8,128)S(1)}, f32[128,128]{1,0:T(8,128)S(1)}, u32[]{:S(2)}, u32[]{:S(2)}) collective-permute-start(f32[128,128]{1,0:T(8,128)S(1)} %get-tuple-element.85), channel_id=1, source_target_pairs={{0,1},{1,0},{2,3},{3,2},{4,5},{5,4},{6,7},{7,6},{8,9},{9,8},{10,11... | collective-permute-start | bytes 196616 | tf_op jit(solution)/shard_map/ppermute | solution.py:261
  15.0 7.8 %collective-permute-start.9 = (f32[128,128]{1,0:T(8,128)S(1)}, f32[128,128]{1,0:T(8,128)S(1)}, u32[]{:S(2)}, u32[]{:S(2)}) collective-permute-start(f32[128,128]{1,0:T(8,128)S(1)} %get-tuple-element.86.send_ref), channel_id=1, source_target_pairs={{0,6},{1,7},{2,3},{3,2},{4,5},{5,4},{6,0},{7,1},{8,14},{9,15},{10,... | collective-permute-start | bytes 196616 | tf_op jit(solution)/shard_map/ppermute | solution.py:261
  18.7 5.6 %collective-permute-start.8 = (f32[128,128]{1,0:T(8,128)S(1)}, f32[128,128]{1,0:T(8,128)S(1)}, u32[]{:S(2)}, u32[]{:S(2)}) collective-permute-start(f32[128,128]{1,0:T(8,128)S(1)} %get-tuple-element.86.send_ref), channel_id=1, source_target_pairs={{0,4},{1,5},{2,3},{3,2},{4,0},{5,1},{6,7},{7,6},{8,12},{9,13},{10,... | collective-permute-start | bytes 196616 | tf_op jit(solution)/shard_map/ppermute | solution.py:261
  20.7 8.1 %collective-permute-start = (f32[256,128]{1,0:T(8,128)S(1)}, f32[256,128]{1,0:T(8,128)S(1)}, u32[]{:S(2)}, u32[]{:S(2)}) collective-permute-start(f32[256,128]{1,0:T(8,128)S(1)} %get-tuple-element.77), channel_id=1, source_target_pairs={{0,8},{1,9},{2,10},{3,11},{4,12},{5,13},{6,14},{7,15},{8,0},{9,1},... | collective-permute-start | bytes 393224 | tf_op jit(solution)/shard_map/ppermute | solution.py:261
  22.0 8.1 %collective-permute-start.1 = (f32[256,128]{1,0:T(8,128)S(1)}, f32[256,128]{1,0:T(8,128)S(1)}, u32[]{:S(2)}, u32[]{:S(2)}) collective-permute-start(f32[256,128]{1,0:T(8,128)S(1)} %get-tuple-element.78), channel_id=1, source_target_pairs={{0,16},{1,17},{2,18},{3,19},{4,20},{5,21},{6,22},{7,23},{8,24},{9,... | collective-permute-start | bytes 393224 | tf_op jit(solution)/shard_map/ppermute | solution.py:261
  22.8 4.3 %collective-permute-start.7 = (f32[128,128]{1,0:T(8,128)S(1)}, f32[128,128]{1,0:T(8,128)S(1)}, u32[]{:S(2)}, u32[]{:S(2)}) collective-permute-start(f32[128,128]{1,0:T(8,128)S(1)} %get-tuple-element.86.send_ref), channel_id=1, source_target_pairs={{0,2},{1,3},{2,0},{3,1},{4,5},{5,4},{6,7},{7,6},{8,10},{9,11},{10,... | collective-permute-start | bytes 196616 | tf_op jit(solution)/shard_map/ppermute | solution.py:261
  22.8 10.6 %collective-permute-start.2 = (f32[256,128]{1,0:T(8,128)S(1)}, f32[256,128]{1,0:T(8,128)S(1)}, u32[]{:S(2)}, u32[]{:S(2)}) collective-permute-start(f32[256,128]{1,0:T(8,128)S(1)} %get-tuple-element.79), channel_id=1, source_target_pairs={{0,24},{1,25},{2,26},{3,27},{4,28},{5,29},{6,30},{7,31},{8,16},{9,... | collective-permute-start | bytes 393224 | tf_op jit(solution)/shard_map/ppermute | solution.py:261
  24.3 11.2 %collective-permute-start.14 = (f32[256,128]{1,0:T(8,128)S(1)}, f32[256,128]{1,0:T(8,128)S(1)}, u32[]{:S(2)}, u32[]{:S(2)}) collective-permute-start(f32[256,128]{1,0:T(8,128)S(1)} %get-tuple-element.96), channel_id=1, source_target_pairs={{0,8},{1,9},{2,10},{3,11},{4,12},{5,13},{6,14},{7,15},{8,0},{9,1},... | collective-permute-start | bytes 393224 | tf_op jit(solution)/shard_map/ppermute | solution.py:261
  27.1 6.4 %collective-permute-start.10 = (f32[128,128]{1,0:T(8,128)S(1)}, f32[128,128]{1,0:T(8,128)S(1)}, u32[]{:S(2)}, u32[]{:S(2)}) collective-permute-start(f32[128,128]{1,0:T(8,128)S(1)} %get-tuple-element.89), channel_id=1, source_target_pairs={{0,1},{1,0},{2,3},{3,2},{4,5},{5,4},{6,7},{7,6},{8,9},{9,8},{10,11... | collective-permute-start | bytes 196616 | tf_op jit(solution)/shard_map/ppermute | solution.py:261
  28.8 11.8 %collective-permute-start.15 = (f32[256,128]{1,0:T(8,128)S(1)}, f32[256,128]{1,0:T(8,128)S(1)}, u32[]{:S(2)}, u32[]{:S(2)}) collective-permute-start(f32[256,128]{1,0:T(8,128)S(1)} %get-tuple-element.97), channel_id=1, source_target_pairs={{0,16},{1,17},{2,18},{3,19},{4,20},{5,21},{6,22},{7,23},{8,24},{9,... | collective-permute-start | bytes 393224 | tf_op jit(solution)/shard_map/ppermute | solution.py:261
  30.1 10.5 %collective-permute-start.16 = (f32[256,128]{1,0:T(8,128)S(1)}, f32[256,128]{1,0:T(8,128)S(1)}, u32[]{:S(2)}, u32[]{:S(2)}) collective-permute-start(f32[256,128]{1,0:T(8,128)S(1)} %get-tuple-element.98), channel_id=1, source_target_pairs={{0,24},{1,25},{2,26},{3,27},{4,28},{5,29},{6,30},{7,31},{8,16},{9,... | collective-permute-start | bytes 393224 | tf_op jit(solution)/shard_map/ppermute | solution.py:261
  33.7 8.8 %collective-permute-start.11 = (f32[256,128]{1,0:T(8,128)S(1)}, f32[256,128]{1,0:T(8,128)S(1)}, u32[]{:S(2)}, u32[]{:S(2)}) collective-permute-start(f32[256,128]{1,0:T(8,128)S(1)} %get-tuple-element.91), channel_id=1, source_target_pairs={{0,8},{1,9},{2,10},{3,11},{4,12},{5,13},{6,14},{7,15},{8,0},{9,1},... | collective-permute-start | bytes 393224 | tf_op jit(solution)/shard_map/ppermute | solution.py:261
  34.3 9.0 %collective-permute-start.12 = (f32[256,128]{1,0:T(8,128)S(1)}, f32[256,128]{1,0:T(8,128)S(1)}, u32[]{:S(2)}, u32[]{:S(2)}) collective-permute-start(f32[256,128]{1,0:T(8,128)S(1)} %get-tuple-element.92), channel_id=1, source_target_pairs={{0,16},{1,17},{2,18},{3,19},{4,20},{5,21},{6,22},{7,23},{8,24},{9,... | collective-permute-start | bytes 393224 | tf_op jit(solution)/shard_map/ppermute | solution.py:261
  35.5 7.7 %collective-permute-start.13 = (f32[256,128]{1,0:T(8,128)S(1)}, f32[256,128]{1,0:T(8,128)S(1)}, u32[]{:S(2)}, u32[]{:S(2)}) collective-permute-start(f32[256,128]{1,0:T(8,128)S(1)} %get-tuple-element.93), channel_id=1, source_target_pairs={{0,24},{1,25},{2,26},{3,27},{4,28},{5,29},{6,30},{7,31},{8,16},{9,... | collective-permute-start | bytes 393224 | tf_op jit(solution)/shard_map/ppermute | solution.py:261

commit v5 on v4

--- a/solution.py
+++ b/solution.py
@@ -34,55 +34,13 @@
     return jnp.logical_or(row == 0, lax.axis_index("seq") < limit)
 
 
-def state_kernel(n, tiles, share, lengths_hbm, *refs):
-    prompt = lax.axis_index("resp") == 0
-    keys_values = prompt == share
-    sources = refs[:4]
-    piece_refs = refs[4 : 4 + n]
-    held = refs[4 + n : 6 + n]
-    sums = refs[6 + n : 5 + n + tiles]
-    total, lengths_ref, sem, count_sem = refs[-4:]
-    piece = piece_refs[0].shape[0]
-    counts = pltpu.make_async_copy(lengths_hbm, lengths_ref, count_sem)
-    cut = [pl.ds(i * TILE, TILE) for i in range(tiles)]
-
-    def copies(pair):
-        return [
-            [pltpu.make_async_copy(pair[x].at[c], held[x].at[c], sem.at[x, i]) for x in (0, 1)]
-            for i, c in enumerate(cut)
-        ]
-
-    def start(pair):
-        for tile in copies(pair):
-            for copy in tile:
-                copy.start()
-
-    counts.start()
-
-    @pl.when(keys_values)
-    def _():
-        start(sources[:2])
-
-    @pl.when(jnp.logical_not(keys_values))
-    def _():
-        start(sources[2:])
-
-    waits = copies(sources[:2])
-    place = lax.axis_index("seq")
+def tile_sums(tiles, keys_values, held, sums, total, ready):
     heads = [pl.ds(h * HEAD, HEAD) for h in range(HEADS)]
     for i in range(tiles):
-        if i == 0:
-            counts.wait()
-        for copy in waits[i]:
-            copy.wait()
-
-        @pl.when(jnp.logical_not(kept(lengths_ref)))
-        def _():
-            for ref in held:
-                ref[cut[i], :] = jnp.zeros((TILE, ref.shape[1]), BF16)
-
+        c = pl.ds(i * TILE, TILE)
+        ready(i)
         for h in heads:
-            new = dot(held[0][cut[i], h], held[1][cut[i], h], TN)
+            new = dot(held[0][c, h], held[1][c, h], TN)
             if i < tiles - 1:
                 sums[i][h, :] = new
                 continue
@@ -93,9 +51,72 @@
                 upto = part if upto is None else upto + part
                 ref[h, :] = jnp.where(keys_values, upto, whole - upto if tiles > 2 else new)
             total[h, :] = whole
-    for m in range(n):
+
+
+def cut_pieces(total, piece_refs):
+    piece = piece_refs[0].shape[0]
+    place = lax.axis_index("seq")
+    for m, ref in enumerate(piece_refs):
         at = pl.multiple_of(jnp.bitwise_xor(place, m) * piece, piece)
-        piece_refs[m][...] = total[pl.ds(at, piece), :]
+        ref[...] = total[pl.ds(at, piece), :]
+
+
+def share_kernel(n, tiles, lengths_hbm, *refs):
+    prompt = lax.axis_index("resp") == 0
+    sources = refs[:4]
+    piece_refs = refs[4 : 4 + n]
+    held = refs[4 + n : 8 + n]
+    sums = refs[8 + n : 7 + n + tiles]
+    total, lengths_ref, sem, count_sem = refs[-4:]
+    counts = pltpu.make_async_copy(lengths_hbm, lengths_ref, count_sem)
+    cut = [pl.ds(i * TILE, TILE) for i in range(tiles)]
+
+    def copies(order):
+        return [
+            [pltpu.make_async_copy(sources[s].at[c], held[x].at[c], sem.at[x, i]) for x, s in part]
+            for part in (tuple(enumerate(order))[:2], tuple(enumerate(order))[2:])
+            for i, c in enumerate(cut)
+        ]
+
+    def start(order):
+        for tile in copies(order):
+            for copy in tile:
+                copy.start()
+
+    counts.start()
+
+    @pl.when(prompt)
+    def _():
+        start((0, 1, 2, 3))
+
+    @pl.when(jnp.logical_not(prompt))
+    def _():
+        start((2, 3, 0, 1))
+
+    waits = copies((0, 1, 2, 3))
+    counts.wait()
+
+    def ready(at):
+        for copy in waits[at]:
+            copy.wait()
+        pair = held[:2] if at < tiles else held[2:]
+
+        @pl.when(jnp.logical_not(kept(lengths_ref)))
+        def _():
+            for ref in pair:
+                ref[cut[at % tiles], :] = jnp.zeros((TILE, ref.shape[1]), BF16)
+
+    tile_sums(tiles, prompt, held[:2], sums, total, ready)
+    cut_pieces(total, piece_refs)
+    for i in range(tiles):
+        ready(tiles + i)
+
+
+def rest_kernel(n, tiles, *refs):
+    answers = lax.axis_index("resp") > 0
+    sums = refs[2 + n : 1 + n + tiles]
+    tile_sums(tiles, answers, refs[:2], sums, refs[-1], lambda i: None)
+    cut_pieces(refs[-1], refs[2 : 2 + n])
 
 
 def inner_kernel(factor, first, *refs):
@@ -273,29 +294,36 @@
     def far(x):
         return pltpu.with_memory_space_constraint(x, pltpu.HBM)
 
-    def state(share):
-        made = pl.pallas_call(
-            functools.partial(state_kernel, n, tiles, share),
-            in_specs=[there] * 5,
-            out_specs=[whole] * (n + 1 + tiles),
-            scratch_shapes=[
-                stack,
-                counts,
-                pltpu.SemaphoreType.DMA((2, tiles)),
-                pltpu.SemaphoreType.DMA,
-            ],
-            out_shape=[piece_shape] * n
-            + [jax.ShapeDtypeStruct((tokens, width), BF16)] * 2
-            + [jax.ShapeDtypeStruct((HEADS * HEAD, HEAD), F32)] * (tiles - 1),
-            compiler_params=pltpu.CompilerParams(vmem_limit_bytes=STATE_VMEM * 2**20),
-            cost_estimate=pl.CostEstimate(
-                flops=2 * size * HEAD, bytes_accessed=4 * size, transcendentals=0
-            ),
-        )(far(lengths), far(k), far(v), far(q), far(g))
-        return made[:n], made[n : n + 2], made[n + 2 :]
-
-    share, share_arrays, share_sums = state(True)
-    rest, rest_arrays, rest_sums = state(False)
+    array_shape = jax.ShapeDtypeStruct((tokens, width), BF16)
+    sums_shape = [jax.ShapeDtypeStruct((HEADS * HEAD, HEAD), F32)] * (tiles - 1)
+    grant = pltpu.CompilerParams(vmem_limit_bytes=STATE_VMEM * 2**20)
+    work = pl.CostEstimate(flops=2 * size * HEAD, bytes_accessed=4 * size, transcendentals=0)
+    made = pl.pallas_call(
+        functools.partial(share_kernel, n, tiles),
+        in_specs=[there] * 5,
+        out_specs=[whole] * (n + 3 + tiles),
+        scratch_shapes=[
+            stack,
+            counts,
+            pltpu.SemaphoreType.DMA((4, tiles)),
+            pltpu.SemaphoreType.DMA,
+        ],
+        out_shape=[piece_shape] * n + [array_shape] * 4 + sums_shape,
+        compiler_params=grant,
+        cost_estimate=work,
+    )(far(lengths), far(k), far(v), far(q), far(g))
+    share, share_sums = made[:n], made[n + 4 :]
+    share_arrays, rest_arrays = made[n : n + 2], made[n + 2 : n + 4]
+    made = pl.pallas_call(
+        functools.partial(rest_kernel, n, tiles),
+        in_specs=[whole] * 2,
+        out_specs=[whole] * (n - 1 + tiles),
+        scratch_shapes=[stack],
+        out_shape=[piece_shape] * n + sums_shape,
+        compiler_params=grant,
+        cost_estimate=work,
+    )(*rest_arrays)
+    rest, rest_sums = made[:n], made[n:]
 
     def swapped(pieces):
         came = [pieces[0]]

time: 45.3 us -> 44 us (0.971)
  Pallas kernels: 14.6 us -> 13.3 us
    pallas_call x2, Pallas kernels: 4.04 us -> 2.78 us  [the longest x1 2.23 us: per_device(): pl.pallas_call(functools.partial(share_kernel, n, tiles), in_specs=[there...]
  transfers between devices with their start and end apart: 17 -> 17, of which waited for: 5 -> 6; matrix products, arithmetic and copies ran while one was open for 0% -> 0% of each run, Pallas kernels for 24% -> 21%
where the time goes in v5:
time: 44 us; the launch traced here: 43.9 us
  starting transfers between devices  19.7 us (45%)
  Pallas kernels  13.3 us (30%)
  waiting for transfers between devices  9.87 us (22%)
  between operations  0.95 us (2%)
    ppermute x17, starting transfers between devices, move(): return lax.ppermute(x, AXES, pairs)  19.7 us
    ppermute x17, waiting for transfers between devices, move(): return lax.ppermute(x, AXES, pairs)  9.87 us
    pallas_call x4, Pallas kernels, per_device(): pl.pallas_call(functools.partial(inner_kernel, factor, group * HEADS // G...  6.6 us
    pallas_call x2, Pallas kernels, per_device(): pl.pallas_call(functools.partial(outer_kernel, factor, GROUPS, n, tiles,...  3.57 us
    pallas_call x1, Pallas kernels, per_device(): pl.pallas_call(functools.partial(share_kernel, n, tiles), in_specs=[there...  2.23 us
  transfers between devices with their start and end apart: 17, of which 6 were waited for; matrix products, arithmetic and copies ran while one was open for 0% of the time, Pallas kernels for 21%

profile of v5, /device:TPU:0, one launch (start us, length us, event | category | flops | bytes accessed | tf_op | source)
XLA Modules:
  0.0 43.9 jit_solution(3510015769976166607)
XLA Ops:
  0.6 2.2 %shard_map.84 = (f32[256,128]{1,0:T(8,128)S(1)}, f32[256,128]{1,0:T(8,128)S(1)}, f32[256,128]{1,0:T(8,128)S(1)}, f32[256,128]{1,0:T(8,128)S(1)}, bf16[512,1024]{...) custom-call(s32[7]{0:T(128)} %lengths_hbm.1, ...), custom_call_target="tpu_custom_call" | custom-call | flops 134217728 | bytes 2097152 | tf_op jit(solution)/shard_map/pallas_call | solution.py:301
  2.9 3.0 %collective-permute-start.3 = (f32[256,128]{1,0:T(8,128)S(1)}, f32[256,128]{1,0:T(8,128)S(1)}, u32[]{:S(2)}, u32[]{:S(2)}) collective-permute-start(f32[256,128]{1,0:T(8,128)S(1)} %get-tuple-element.81), channel_id=1, source_target_pairs={{0,8},{1,9},{2,10},{3,11},{4,12},{5,13},{6,14},{7,15},{8,0},{9,1},... | collective-permute-start | bytes 393224 | tf_op jit(solution)/shard_map/ppermute | solution.py:282
  5.9 1.5 %collective-permute-start.4 = (f32[256,128]{1,0:T(8,128)S(1)}, f32[256,128]{1,0:T(8,128)S(1)}, u32[]{:S(2)}, u32[]{:S(2)}) collective-permute-start(f32[256,128]{1,0:T(8,128)S(1)} %get-tuple-element.82), channel_id=1, source_target_pairs={{0,16},{1,17},{2,18},{3,19},{4,20},{5,21},{6,22},{7,23},{8,24},{9,... | collective-permute-start | bytes 393224 | tf_op jit(solution)/shard_map/ppermute | solution.py:282
  7.4 0.0 collective-permute-start.5
  7.4 2.3 %collective-permute-done.3.refs_1_ = f32[256,128]{1,0:T(8,128)S(1)} collective-permute-done((f32[256,128]{1,0:T(8,128)S(1)}, f32[256,128]{1,0:T(8,128)S(1)}, u32[]{:S(2)}, u32[]{:S(2)}) %collective-permute-start.3) | collective-permute-done | bytes 131104 | tf_op jit(solution)/shard_map/ppermute | solution.py:282
  9.8 3.9 %collective-permute-done.4.refs_2_ = f32[256,128]{1,0:T(8,128)S(1)} collective-permute-done((f32[256,128]{1,0:T(8,128)S(1)}, f32[256,128]{1,0:T(8,128)S(1)}, u32[]{:S(2)}, u32[]{:S(2)}) %collective-permute-start.4) | collective-permute-done | bytes 131104 | tf_op jit(solution)/shard_map/ppermute | solution.py:282
  13.7 0.0 collective-permute-done.5.refs_3_
  13.7 0.2 shard_map.90
  13.9 0.1 collective-permute-start.6
  13.9 1.2 %collective-permute-done.6.new_ref = f32[128,128]{1,0:T(8,128)S(1)} collective-permute-done((f32[128,128]{1,0:T(8,128)S(1)}, f32[128,128]{1,0:T(8,128)S(1)}, u32[]{:S(2)}, u32[]{:S(2)}) %collective-permute-start.6) | collective-permute-done | bytes 65568 | tf_op jit(solution)/shard_map/ppermute | solution.py:282
  15.2 3.7 %collective-permute-start.9 = (f32[128,128]{1,0:T(8,128)S(1)}, f32[128,128]{1,0:T(8,128)S(1)}, u32[]{:S(2)}, u32[]{:S(2)}) collective-permute-start(f32[128,128]{1,0:T(8,128)S(1)} %get-tuple-element.86.send_ref), channel_id=1, source_target_pairs={{0,6},{1,7},{2,3},{3,2},{4,5},{5,4},{6,0},{7,1},{8,14},{9,15},{10,... | collective-permute-start | bytes 196616 | tf_op jit(solution)/shard_map/ppermute | solution.py:282
  18.9 0.0 collective-permute-start.8
  18.9 0.5 %shard_map.89 = (f32[256,128]{1,0:T(8,128)S(1)}, f32[256,128]{1,0:T(8,128)S(1)}, f32[256,128]{1,0:T(8,128)S(1)}, f32[256,128]{1,0:T(8,128)S(1)}, f32[1024,128]{1,0:T(8,128)S(1)}) custom-call(bf16[512,1024]{1,0:T(8,128)(2,1)S(1)} %get-tuple-element.58.refs_2_.refs_0_, bf16[512,1024]{1,0:T(8,128)(2,1)S(1)} %get-tuple-element.59.refs_3_.refs_1_), custom_call_target="tpu_custom_call" | custom-call | flops 134217728 | bytes 2097152 | tf_op jit(solution)/shard_map/pallas_call | solution.py:317
  19.4 1.3 %collective-permute-start = (f32[256,128]{1,0:T(8,128)S(1)}, f32[256,128]{1,0:T(8,128)S(1)}, u32[]{:S(2)}, u32[]{:S(2)}) collective-permute-start(f32[256,128]{1,0:T(8,128)S(1)} %get-tuple-element.77), channel_id=1, source_target_pairs={{0,8},{1,9},{2,10},{3,11},{4,12},{5,13},{6,14},{7,15},{8,0},{9,1},... | collective-permute-start | bytes 393224 | tf_op jit(solution)/shard_map/ppermute | solution.py:282
  20.7 0.8 %collective-permute-start.1 = (f32[256,128]{1,0:T(8,128)S(1)}, f32[256,128]{1,0:T(8,128)S(1)}, u32[]{:S(2)}, u32[]{:S(2)}) collective-permute-start(f32[256,128]{1,0:T(8,128)S(1)} %get-tuple-element.78), channel_id=1, source_target_pairs={{0,16},{1,17},{2,18},{3,19},{4,20},{5,21},{6,22},{7,23},{8,24},{9,... | collective-permute-start | bytes 393224 | tf_op jit(solution)/shard_map/ppermute | solution.py:282
  21.6 0.0 collective-permute-start.7
  21.6 0.0 collective-permute-done.9.refs_2_
  21.6 1.4 %collective-permute-start.2 = (f32[256,128]{1,0:T(8,128)S(1)}, f32[256,128]{1,0:T(8,128)S(1)}, u32[]{:S(2)}, u32[]{:S(2)}) collective-permute-start(f32[256,128]{1,0:T(8,128)S(1)} %get-tuple-element.79), channel_id=1, source_target_pairs={{0,24},{1,25},{2,26},{3,27},{4,28},{5,29},{6,30},{7,31},{8,16},{9,... | collective-permute-start | bytes 393224 | tf_op jit(solution)/shard_map/ppermute | solution.py:282
  23.0 1.1 %collective-permute-done.8.refs_1_ = f32[128,128]{1,0:T(8,128)S(1)} collective-permute-done((f32[128,128]{1,0:T(8,128)S(1)}, f32[128,128]{1,0:T(8,128)S(1)}, u32[]{:S(2)}, u32[]{:S(2)}) %collective-permute-start.8) | collective-permute-done | bytes 65568 | tf_op jit(solution)/shard_map/ppermute | solution.py:282
  24.1 1.2 %collective-permute-start.14 = (f32[256,128]{1,0:T(8,128)S(1)}, f32[256,128]{1,0:T(8,128)S(1)}, u32[]{:S(2)}, u32[]{:S(2)}) collective-permute-start(f32[256,128]{1,0:T(8,128)S(1)} %get-tuple-element.96), channel_id=1, source_target_pairs={{0,8},{1,9},{2,10},{3,11},{4,12},{5,13},{6,14},{7,15},{8,0},{9,1},... | collective-permute-start | bytes 393224 | tf_op jit(solution)/shard_map/ppermute | solution.py:282
  25.3 0.5 %collective-permute-done.7.refs_0_ = f32[128,128]{1,0:T(8,128)S(1)} collective-permute-done((f32[128,128]{1,0:T(8,128)S(1)}, f32[128,128]{1,0:T(8,128)S(1)}, u32[]{:S(2)}, u32[]{:S(2)}) %collective-permute-start.7) | collective-permute-done | bytes 65568 | tf_op jit(solution)/shard_map/ppermute | solution.py:282
  25.9 0.1 collective-permute-start.10
  25.9 1.6 %shard_map.88 = (f32[512,256]{1,0:T(8,128)S(1)}, f32[512,256]{1,0:T(8,128)S(1)}, f32[512,256]{1,0:T(8,128)S(1)}, f32[512,256]{1,0:T(8,128)S(1)}) custom-call(bf16[512,1024]{1,0:T(8,128)(2,1)S(1)} %get-tuple-element.56.refs_0_, bf16[512,1024]{1,0:T(8,128)(2,1)S(1)} %get-tuple-element.57.refs_1_, bf16[512,1024]{1,0:T(8,128)(2,1)S(1)} %get-tuple-element.58.refs_2_.refs_0_, ...), custom_call_target="tpu_custom_call" | custom-call | flops 603979776 | bytes 3145728 | tf_op jit(solution)/shard_map/pallas_call | solution.py:383
  27.6 0.0 collective-permute-done.refs_1_
  27.6 1.2 %collective-permute-start.15 = (f32[256,128]{1,0:T(8,128)S(1)}, f32[256,128]{1,0:T(8,128)S(1)}, u32[]{:S(2)}, u32[]{:S(2)}) collective-permute-start(f32[256,128]{1,0:T(8,128)S(1)} %get-tuple-element.97), channel_id=1, source_target_pairs={{0,16},{1,17},{2,18},{3,19},{4,20},{5,21},{6,22},{7,23},{8,24},{9,... | collective-permute-start | bytes 393224 | tf_op jit(solution)/shard_map/ppermute | solution.py:282
  28.8 0.0 collective-permute-done.1.refs_2_
  28.8 1.8 %collective-permute-start.16 = (f32[256,128]{1,0:T(8,128)S(1)}, f32[256,128]{1,0:T(8,128)S(1)}, u32[]{:S(2)}, u32[]{:S(2)}) collective-permute-start(f32[256,128]{1,0:T(8,128)S(1)} %get-tuple-element.98), channel_id=1, source_target_pairs={{0,24},{1,25},{2,26},{3,27},{4,28},{5,29},{6,30},{7,31},{8,16},{9,... | collective-permute-start | bytes 393224 | tf_op jit(solution)/shard_map/ppermute | solution.py:282
  30.6 1.6 %shard_map.87 = (f32[512,256]{1,0:T(8,128)S(1)}, f32[512,256]{1,0:T(8,128)S(1)}, f32[512,256]{1,0:T(8,128)S(1)}, f32[512,256]{1,0:T(8,128)S(1)}) custom-call(bf16[512,1024]{1,0:T(8,128)(2,1)S(1)} %get-tuple-element.56.refs_0_, bf16[512,1024]{1,0:T(8,128)(2,1)S(1)} %get-tuple-element.57.refs_1_, bf16[512,1024]{1,0:T(8,128)(2,1)S(1)} %get-tuple-element.58.refs_2_.refs_0_, ...), custom_call_target="tpu_custom_call" | custom-call | flops 603979776 | bytes 3145728 | tf_op jit(solution)/shard_map/pallas_call | solution.py:383
  32.2 0.0 collective-permute-done.2.refs_3_
  32.2 0.0 collective-permute-done.10.refs_5_
  32.2 0.2 shard_map.93
  32.4 0.6 %collective-permute-start.11 = (f32[256,128]{1,0:T(8,128)S(1)}, f32[256,128]{1,0:T(8,128)S(1)}, u32[]{:S(2)}, u32[]{:S(2)}) collective-permute-start(f32[256,128]{1,0:T(8,128)S(1)} %get-tuple-element.91), channel_id=1, source_target_pairs={{0,8},{1,9},{2,10},{3,11},{4,12},{5,13},{6,14},{7,15},{8,0},{9,1},... | collective-permute-start | bytes 393224 | tf_op jit(solution)/shard_map/ppermute | solution.py:282
  33.0 1.2 %collective-permute-start.12 = (f32[256,128]{1,0:T(8,128)S(1)}, f32[256,128]{1,0:T(8,128)S(1)}, u32[]{:S(2)}, u32[]{:S(2)}) collective-permute-start(f32[256,128]{1,0:T(8,128)S(1)} %get-tuple-element.92), channel_id=1, source_target_pairs={{0,16},{1,17},{2,18},{3,19},{4,20},{5,21},{6,22},{7,23},{8,24},{9,... | collective-permute-start | bytes 393224 | tf_op jit(solution)/shard_map/ppermute | solution.py:282
  34.2 0.0 collective-permute-done.14.refs_19_
  34.2 1.8 %collective-permute-start.13 = (f32[256,128]{1,0:T(8,128)S(1)}, f32[256,128]{1,0:T(8,128)S(1)}, u32[]{:S(2)}, u32[]{:S(2)}) collective-permute-start(f32[256,128]{1,0:T(8,128)S(1)} %get-tuple-element.93), channel_id=1, source_target_pairs={{0,24},{1,25},{2,26},{3,27},{4,28},{5,29},{6,30},{7,31},{8,16},{9,... | collective-permute-start | bytes 393224 | tf_op jit(solution)/shard_map/ppermute | solution.py:282
  35.9 1.6 %shard_map.86 = (f32[512,256]{1,0:T(8,128)S(1)}, f32[512,256]{1,0:T(8,128)S(1)}, f32[512,256]{1,0:T(8,128)S(1)}, f32[512,256]{1,0:T(8,128)S(1)}) custom-call(bf16[512,1024]{1,0:T(8,128)(2,1)S(1)} %get-tuple-element.56.refs_0_, bf16[512,1024]{1,0:T(8,128)(2,1)S(1)} %get-tuple-element.57.refs_1_, bf16[512,1024]{1,0:T(8,128)(2,1)S(1)} %get-tuple-element.58.refs_2_.refs_0_, ...), custom_call_target="tpu_custom_call" | custom-call | flops 603979776 | bytes 3145728 | tf_op jit(solution)/shard_map/pallas_call | solution.py:383
  37.6 1.8 %shard_map.85 = (f32[512,256]{1,0:T(8,128)S(1)}, f32[512,256]{1,0:T(8,128)S(1)}, f32[512,256]{1,0:T(8,128)S(1)}, f32[512,256]{1,0:T(8,128)S(1)}) custom-call(bf16[512,1024]{1,0:T(8,128)(2,1)S(1)} %get-tuple-element.56.refs_0_, bf16[512,1024]{1,0:T(8,128)(2,1)S(1)} %get-tuple-element.57.refs_1_, bf16[512,1024]{1,0:T(8,128)(2,1)S(1)} %get-tuple-element.58.refs_2_.refs_0_, ...), custom_call_target="tpu_custom_call" | custom-call | flops 603979776 | bytes 3145728 | tf_op jit(solution)/shard_map/pallas_call | solution.py:383
  39.3 0.0 collective-permute-done.15.refs_20_
  39.4 0.0 collective-permute-done.16.refs_21_
  39.4 1.8 %shard_map.94 = (bf16[512,1024]{1,0:T(8,128)(2,1)}, bf16[512,1024]{1,0:T(8,128)(2,1)}, bf16[512,1024]{1,0:T(8,128)(2,1)}, bf16[512,1024]{1,0:T(8,128)(2,1)}) custom-call(bf16[512,1024]{1,0:T(8,128)(2,1)S(1)} %get-tuple-element.58.refs_2_.refs_0_, bf16[512,1024]{1,0:T(8,128)(2,1)S(1)} %get-tuple-element.59.refs_3_.refs_1_, ...), custom_call_target="tpu_custom_call" | custom-call | flops 268435456 | bytes 8388608 | tf_op jit(solution)/shard_map/pallas_call | solution.py:402
  41.2 0.0 collective-permute-done.11.refs_19_
  41.2 0.7 %collective-permute-done.12.refs_20_ = f32[256,128]{1,0:T(8,128)S(1)} collective-permute-done((f32[256,128]{1,0:T(8,128)S(1)}, f32[256,128]{1,0:T(8,128)S(1)}, u32[]{:S(2)}, u32[]{:S(2)}) %collective-permute-start.12) | collective-permute-done | bytes 131104 | tf_op jit(solution)/shard_map/ppermute | solution.py:282
  42.0 0.0 collective-permute-done.13.refs_21_
  42.0 1.7 %shard_map.95 = (bf16[512,1024]{1,0:T(8,128)(2,1)}, bf16[512,1024]{1,0:T(8,128)(2,1)}, bf16[512,1024]{1,0:T(8,128)(2,1)}, bf16[512,1024]{1,0:T(8,128)(2,1)}) custom-call(bf16[512,1024]{1,0:T(8,128)(2,1)S(1)} %get-tuple-element.56.refs_0_, ...), custom_call_target="tpu_custom_call", output_to_operand_aliasing={{0}: (23, {}), {1}: (24, {}), {2}: (25, {}), {3}: (26, {})} | custom-call | flops 268435456 | bytes 8388608 | tf_op jit(solution)/shard_map/pallas_call | solution.py:402
  (2 shorter events, 0.1 us)
Async XLA Ops:
  2.9 6.9 %collective-permute-start.3 = (f32[256,128]{1,0:T(8,128)S(1)}, f32[256,128]{1,0:T(8,128)S(1)}, u32[]{:S(2)}, u32[]{:S(2)}) collective-permute-start(f32[256,128]{1,0:T(8,128)S(1)} %get-tuple-element.81), channel_id=1, source_target_pairs={{0,8},{1,9},{2,10},{3,11},{4,12},{5,13},{6,14},{7,15},{8,0},{9,1},... | collective-permute-start | bytes 393224 | tf_op jit(solution)/shard_map/ppermute | solution.py:282
  5.9 7.8 %collective-permute-start.4 = (f32[256,128]{1,0:T(8,128)S(1)}, f32[256,128]{1,0:T(8,128)S(1)}, u32[]{:S(2)}, u32[]{:S(2)}) collective-permute-start(f32[256,128]{1,0:T(8,128)S(1)} %get-tuple-element.82), channel_id=1, source_target_pairs={{0,16},{1,17},{2,18},{3,19},{4,20},{5,21},{6,22},{7,23},{8,24},{9,... | collective-permute-start | bytes 393224 | tf_op jit(solution)/shard_map/ppermute | solution.py:282
  7.4 6.3 %collective-permute-start.5 = (f32[256,128]{1,0:T(8,128)S(1)}, f32[256,128]{1,0:T(8,128)S(1)}, u32[]{:S(2)}, u32[]{:S(2)}) collective-permute-start(f32[256,128]{1,0:T(8,128)S(1)} %get-tuple-element.83), channel_id=1, source_target_pairs={{0,24},{1,25},{2,26},{3,27},{4,28},{5,29},{6,30},{7,31},{8,16},{9,... | collective-permute-start | bytes 393224 | tf_op jit(solution)/shard_map/ppermute | solution.py:282
  13.9 1.3 %collective-permute-start.6 = (f32[128,128]{1,0:T(8,128)S(1)}, f32[128,128]{1,0:T(8,128)S(1)}, u32[]{:S(2)}, u32[]{:S(2)}) collective-permute-start(f32[128,128]{1,0:T(8,128)S(1)} %get-tuple-element.85), channel_id=1, source_target_pairs={{0,1},{1,0},{2,3},{3,2},{4,5},{5,4},{6,7},{7,6},{8,9},{9,8},{10,11... | collective-permute-start | bytes 196616 | tf_op jit(solution)/shard_map/ppermute | solution.py:282
  15.2 6.4 %collective-permute-start.9 = (f32[128,128]{1,0:T(8,128)S(1)}, f32[128,128]{1,0:T(8,128)S(1)}, u32[]{:S(2)}, u32[]{:S(2)}) collective-permute-start(f32[128,128]{1,0:T(8,128)S(1)} %get-tuple-element.86.send_ref), channel_id=1, source_target_pairs={{0,6},{1,7},{2,3},{3,2},{4,5},{5,4},{6,0},{7,1},{8,14},{9,15},{10,... | collective-permute-start | bytes 196616 | tf_op jit(solution)/shard_map/ppermute | solution.py:282
  18.9 5.2 %collective-permute-start.8 = (f32[128,128]{1,0:T(8,128)S(1)}, f32[128,128]{1,0:T(8,128)S(1)}, u32[]{:S(2)}, u32[]{:S(2)}) collective-permute-start(f32[128,128]{1,0:T(8,128)S(1)} %get-tuple-element.86.send_ref), channel_id=1, source_target_pairs={{0,4},{1,5},{2,3},{3,2},{4,0},{5,1},{6,7},{7,6},{8,12},{9,13},{10,... | collective-permute-start | bytes 196616 | tf_op jit(solution)/shard_map/ppermute | solution.py:282
  19.4 8.1 %collective-permute-start = (f32[256,128]{1,0:T(8,128)S(1)}, f32[256,128]{1,0:T(8,128)S(1)}, u32[]{:S(2)}, u32[]{:S(2)}) collective-permute-start(f32[256,128]{1,0:T(8,128)S(1)} %get-tuple-element.77), channel_id=1, source_target_pairs={{0,8},{1,9},{2,10},{3,11},{4,12},{5,13},{6,14},{7,15},{8,0},{9,1},... | collective-permute-start | bytes 393224 | tf_op jit(solution)/shard_map/ppermute | solution.py:282
  20.7 8.1 %collective-permute-start.1 = (f32[256,128]{1,0:T(8,128)S(1)}, f32[256,128]{1,0:T(8,128)S(1)}, u32[]{:S(2)}, u32[]{:S(2)}) collective-permute-start(f32[256,128]{1,0:T(8,128)S(1)} %get-tuple-element.78), channel_id=1, source_target_pairs={{0,16},{1,17},{2,18},{3,19},{4,20},{5,21},{6,22},{7,23},{8,24},{9,... | collective-permute-start | bytes 393224 | tf_op jit(solution)/shard_map/ppermute | solution.py:282
  21.6 4.3 %collective-permute-start.7 = (f32[128,128]{1,0:T(8,128)S(1)}, f32[128,128]{1,0:T(8,128)S(1)}, u32[]{:S(2)}, u32[]{:S(2)}) collective-permute-start(f32[128,128]{1,0:T(8,128)S(1)} %get-tuple-element.86.send_ref), channel_id=1, source_target_pairs={{0,2},{1,3},{2,0},{3,1},{4,5},{5,4},{6,7},{7,6},{8,10},{9,11},{10,... | collective-permute-start | bytes 196616 | tf_op jit(solution)/shard_map/ppermute | solution.py:282
  21.6 10.6 %collective-permute-start.2 = (f32[256,128]{1,0:T(8,128)S(1)}, f32[256,128]{1,0:T(8,128)S(1)}, u32[]{:S(2)}, u32[]{:S(2)}) collective-permute-start(f32[256,128]{1,0:T(8,128)S(1)} %get-tuple-element.79), channel_id=1, source_target_pairs={{0,24},{1,25},{2,26},{3,27},{4,28},{5,29},{6,30},{7,31},{8,16},{9,... | collective-permute-start | bytes 393224 | tf_op jit(solution)/shard_map/ppermute | solution.py:282
  24.1 10.1 %collective-permute-start.14 = (f32[256,128]{1,0:T(8,128)S(1)}, f32[256,128]{1,0:T(8,128)S(1)}, u32[]{:S(2)}, u32[]{:S(2)}) collective-permute-start(f32[256,128]{1,0:T(8,128)S(1)} %get-tuple-element.96), channel_id=1, source_target_pairs={{0,8},{1,9},{2,10},{3,11},{4,12},{5,13},{6,14},{7,15},{8,0},{9,1},... | collective-permute-start | bytes 393224 | tf_op jit(solution)/shard_map/ppermute | solution.py:282
  25.9 6.3 %collective-permute-start.10 = (f32[128,128]{1,0:T(8,128)S(1)}, f32[128,128]{1,0:T(8,128)S(1)}, u32[]{:S(2)}, u32[]{:S(2)}) collective-permute-start(f32[128,128]{1,0:T(8,128)S(1)} %get-tuple-element.89), channel_id=1, source_target_pairs={{0,1},{1,0},{2,3},{3,2},{4,5},{5,4},{6,7},{7,6},{8,9},{9,8},{10,11... | collective-permute-start | bytes 196616 | tf_op jit(solution)/shard_map/ppermute | solution.py:282
  27.6 11.8 %collective-permute-start.15 = (f32[256,128]{1,0:T(8,128)S(1)}, f32[256,128]{1,0:T(8,128)S(1)}, u32[]{:S(2)}, u32[]{:S(2)}) collective-permute-start(f32[256,128]{1,0:T(8,128)S(1)} %get-tuple-element.97), channel_id=1, source_target_pairs={{0,16},{1,17},{2,18},{3,19},{4,20},{5,21},{6,22},{7,23},{8,24},{9,... | collective-permute-start | bytes 393224 | tf_op jit(solution)/shard_map/ppermute | solution.py:282
  28.8 10.5 %collective-permute-start.16 = (f32[256,128]{1,0:T(8,128)S(1)}, f32[256,128]{1,0:T(8,128)S(1)}, u32[]{:S(2)}, u32[]{:S(2)}) collective-permute-start(f32[256,128]{1,0:T(8,128)S(1)} %get-tuple-element.98), channel_id=1, source_target_pairs={{0,24},{1,25},{2,26},{3,27},{4,28},{5,29},{6,30},{7,31},{8,16},{9,... | collective-permute-start | bytes 393224 | tf_op jit(solution)/shard_map/ppermute | solution.py:282
  32.4 8.8 %collective-permute-start.11 = (f32[256,128]{1,0:T(8,128)S(1)}, f32[256,128]{1,0:T(8,128)S(1)}, u32[]{:S(2)}, u32[]{:S(2)}) collective-permute-start(f32[256,128]{1,0:T(8,128)S(1)} %get-tuple-element.91), channel_id=1, source_target_pairs={{0,8},{1,9},{2,10},{3,11},{4,12},{5,13},{6,14},{7,15},{8,0},{9,1},... | collective-permute-start | bytes 393224 | tf_op jit(solution)/shard_map/ppermute | solution.py:282
  33.0 8.9 %collective-permute-start.12 = (f32[256,128]{1,0:T(8,128)S(1)}, f32[256,128]{1,0:T(8,128)S(1)}, u32[]{:S(2)}, u32[]{:S(2)}) collective-permute-start(f32[256,128]{1,0:T(8,128)S(1)} %get-tuple-element.92), channel_id=1, source_target_pairs={{0,16},{1,17},{2,18},{3,19},{4,20},{5,21},{6,22},{7,23},{8,24},{9,... | collective-permute-start | bytes 393224 | tf_op jit(solution)/shard_map/ppermute | solution.py:282
  34.2 7.8 %collective-permute-start.13 = (f32[256,128]{1,0:T(8,128)S(1)}, f32[256,128]{1,0:T(8,128)S(1)}, u32[]{:S(2)}, u32[]{:S(2)}) collective-permute-start(f32[256,128]{1,0:T(8,128)S(1)} %get-tuple-element.93), channel_id=1, source_target_pairs={{0,24},{1,25},{2,26},{3,27},{4,28},{5,29},{6,30},{7,31},{8,16},{9,... | collective-permute-start | bytes 393224 | tf_op jit(solution)/shard_map/ppermute | solution.py:282
